TPU v7x, 256 devices: a whole 4x4x8 slice. The times are simulated.
256 devices in a mesh: req: 16 (over y, x_hi, core), blk: 16 (over z, x_lo).
Axes of the slice: x: 4 (x_hi: 2, x_lo: 2; x = x_hi * 2 + x_lo), y: 4, z: 8, core: 2. Of those that a mesh axis runs over, the one named last changes fastest.
Arguments:
- tokens: bfloat16 [32, 256, 1600], P('req'), may hold values from -6 to 6
- cache_kv: bfloat16 [4, 8192, 16, 128], P(None, 'req', 'blk'), may hold values from -500 to 500
- w_qkv: bfloat16 [1600, 16, 192], P(None, 'blk'), may hold values from -0.15625 to 0.15625
- w_out: bfloat16 [16, 64, 1600], P('blk'), may hold values from -0.1875 to 0.1875
- w_fc: bfloat16 [1600, 6400], P(None, 'blk'), may hold values from -0.15625 to 0.15625
- w_proj: bfloat16 [6400, 1600], P('blk'), may hold values from -0.078125 to 0.078125
- embed_table: bfloat16 [50256, 1600], P('req', 'blk'), may hold values from -6 to 6
- group_ids: int32 [32], replicated, may hold values from 0 to 3, never falling along the last dimension, each value on 1 to 16 neighbouring positions
- cache_len: int32 [4], replicated, may hold values from 512 to 8192, as said below
- accept: int32 [2, 32, 256], P(None, 'req'), may hold values 0 or 1
- new_ids: int32 [2, 32, 256], replicated, may hold values from 0 to 50255
Outputs:
- denoised: bfloat16 [32, 256, 1600], P('req')
Inputs may be any that keep to these rules, and one draw needn't show every extreme that they name: `group_ids`: requests of one group stand in consecutive order; each of the 4 groups holds 1 to 16 requests and one holds exactly 16. Cache positions 0 to cache_len[g] - 1 of group g are live; one group's cache is full in every draw.
All inputs are finite; a program needn't handle non-finite values. No bound on the sum of `accept` on one device may be relied on, other than what follows from the above.
Results may differ from a plain program's by a relative error of at most 0.04.
Values may be sent and summed in bfloat16 or wider, within the bound.
A program may use at most 128 MiB of HBM per device.

v0:
```python
import jax
import jax.numpy as jnp
from jax import lax
from jax.sharding import PartitionSpec as P

PASSES = 2


def layer_norm(values):
    centre = values - jnp.mean(values, -1, keepdims=True)
    spread = jnp.mean(centre * centre, -1, keepdims=True)
    return centre * lax.rsqrt(spread + 1e-05)


def attend(projected, own_cache, lengths, head_dim):
    queries = projected[..., :head_dim]
    keys_new = projected[..., head_dim : 2 * head_dim]
    values_new = projected[..., 2 * head_dim :]
    factor = head_dim ** (-0.5)
    scores = (
        jnp.einsum("rqhd,rkhd->rhqk", queries, keys_new, preferred_element_type=jnp.float32)
        * factor
    )
    highest = jnp.max(scores, -1)
    weights_raw = jnp.exp(scores - highest[..., None])
    totals = jnp.sum(weights_raw, -1)
    gathered = jnp.einsum(
        "rhqk,rkhd->rhqd",
        weights_raw.astype(jnp.bfloat16),
        values_new,
        preferred_element_type=jnp.float32,
    )
    cache_size = own_cache.shape[1]
    key_span = min(1024, cache_size)

    def visit_block(block_index, carried):
        highest, totals, gathered = carried
        cache_piece = lax.dynamic_slice_in_dim(own_cache, block_index * key_span, key_span, 1)
        scores = (
            jnp.einsum(
                "rqhd,rkhd->rhqk",
                queries,
                cache_piece[..., :head_dim],
                preferred_element_type=jnp.float32,
            )
            * factor
        )
        position = block_index * key_span + jnp.arange(key_span, dtype=jnp.int32)
        scores = jnp.where(
            position[None, None, None, :] < lengths[:, None, None, None], scores, -1e30
        )
        raised = jnp.maximum(highest, jnp.max(scores, -1))
        shrink = jnp.exp(highest - raised)
        weights_raw = jnp.exp(scores - raised[..., None])
        totals = totals * shrink + jnp.sum(weights_raw, -1)
        gathered = gathered * shrink[..., None] + jnp.einsum(
            "rhqk,rkhd->rhqd",
            weights_raw.astype(jnp.bfloat16),
            cache_piece[..., head_dim:],
            preferred_element_type=jnp.float32,
        )
        return (raised, totals, gathered)

    highest, totals, gathered = lax.fori_loop(
        0, cache_size // key_span, visit_block, (highest, totals, gathered)
    )
    mixed_heads = gathered / totals[..., None]
    return jnp.transpose(mixed_heads, (0, 2, 1, 3)).astype(jnp.bfloat16)


def shards(
    tokens, cache_kv, w_qkv, w_out, w_fc, w_proj, embed_table, group_ids, cache_len, accept, new_ids
):
    req_index = lax.axis_index("req")
    per_device = tokens.shape[0]
    kv_width = cache_kv.shape[3]
    head_dim = kv_width // 2
    my_groups = lax.dynamic_slice_in_dim(group_ids, req_index * per_device, per_device)
    every_cache = lax.all_gather(cache_kv, "req", axis=1, tiled=True)
    own_cache = jnp.take(every_cache, my_groups, axis=0)
    lengths = jnp.take(cache_len, my_groups)
    vocab_dev = embed_table.shape[0]
    relative = new_ids - req_index * vocab_dev
    inside = (relative >= 0) & (relative < vocab_dev)
    looked = jnp.take(embed_table, jnp.clip(relative, 0, vocab_dev - 1), axis=0)
    looked = jnp.where(inside[..., None], looked, jnp.zeros((), jnp.bfloat16))
    picked = (
        lax.psum_scatter(looked, "req", scatter_dimension=1, tiled=True)
        .astype(jnp.float32)
        .astype(jnp.bfloat16)
    )
    fresh_rows = lax.all_gather(picked, "blk", axis=3, tiled=True)
    current = tokens
    for pass_index in range(PASSES):
        state_f32 = current.astype(jnp.float32)
        normed = layer_norm(state_f32).astype(jnp.bfloat16)
        projected = jnp.einsum(
            "rbd,dhc->rbhc", normed, w_qkv, preferred_element_type=jnp.float32
        ).astype(jnp.bfloat16)
        head_rows = attend(projected, own_cache, lengths, head_dim)
        partial_terms = jnp.einsum(
            "rbhc,hcd->rbd", head_rows, w_out, preferred_element_type=jnp.float32
        )
        middle = state_f32 + lax.psum(partial_terms.astype(jnp.bfloat16), "blk").astype(jnp.float32)
        normed_mid = layer_norm(middle).astype(jnp.bfloat16)
        hidden = jax.nn.gelu(
            jnp.einsum("rbd,df->rbf", normed_mid, w_fc, preferred_element_type=jnp.float32),
            approximate=True,
        ).astype(jnp.bfloat16)
        grown_rows = jnp.einsum("rbf,fd->rbd", hidden, w_proj, preferred_element_type=jnp.float32)
        current = (
            middle + lax.psum(grown_rows.astype(jnp.bfloat16), "blk").astype(jnp.float32)
        ).astype(jnp.bfloat16)
        current = jnp.where(accept[pass_index][..., None] == 1, fresh_rows[pass_index], current)
    return current


def solution(mesh):
    return jax.shard_map(
        shards,
        mesh=mesh,
        in_specs=(
            P("req", None, None),
            P(None, "req", "blk", None),
            P(None, "blk", None),
            P("blk", None, None),
            P(None, "blk"),
            P("blk", None),
            P("req", "blk"),
            P(),
            P(),
            P(None, "req", None),
            P(),
        ),
        out_specs=P("req", None, None),
        check_vma=False,
    )
```

profile of v0, /device:TPU:12, one launch (start us, length us, event | category | flops | bytes accessed | tf_op | source)
XLA Modules:
  0.0 969.1 jit_solution(16571325852743032627)
XLA Ops:
  9.8 57.4 %gather_fusion = bf16[16384,100]{1,0:T(8,128)(2,1)} fusion(bf16[3141,100]{1,0:T(8,128)(2,1)S(1)} %copy.29, s32[16384]{0:T(1024)S(1)} %broadcast_clamp_fusion), kind=kCustom, calls=%fused_computation | custom fusion | bytes 6619136 | tf_op jit(solution)/shard_map/jit(_take)/gather | solution.py:85
  67.2 7.7 copy.44
  74.9 2.3 select_select_fusion
  77.2 5.1 copy.31
  87.3 5.7 slice_bitcast_fusion.1
  93.0 4.4 gather_fusion.3
  97.3 4.3 gather_fusion.2
  101.6 4.2 maximum_select_fusion
  105.8 6.4 copy.37
  112.2 34.5 %while.34 = (s32[]{:T(128)}, f32[2,1,256]{2,0,1:T(2,128)S(1)}, f32[2,1,256]{2,0,1:T(2,128)S(1)}, f32[2,1,256,64]{2,3,0,1:T(8,128)S(1)}, s32[2]{0:T(128)S(1)}, /*...) while((s32[]{:T(128)}, f32[2,1,256]{2,0,1:T(2,128)S(1)}, ...), condition=%wide.region_8.9_spmd, body=%wide.region_5.8_spmd.sunk | while | flops 140055040 | bytes 7192775 | solution.py:64
  149.9 87.5 %all-reduce.15.cloned.1.call-done = bf16[2,32,256,100]{2,0,3,1:T(2,128)(2,1)} async-done(((bf16[2,32,256,100]{2,0,3,1:T(2,128)(2,1)}), bf16[2,32,256,100]{2,0,3,1:T(2,128)(2,1)}) %all-reduce.15.cloned.1.call-update) | async-done | bytes 3276816
  239.5 154.3 %all-reduce.7.cloned.1.call-done = bf16[2,256,1600]{1,2,0:T(8,128)(2,1)} async-done(((bf16[2,256,1600]{1,2,0:T(8,128)(2,1)}), bf16[2,256,1600]{1,2,0:T(8,128)(2,1)}) %all-reduce.7.cloned.1.call-update) | async-done | bytes 1638416 | tf_op jit(solution)/shard_map/psum | solution.py:104
  393.9 2.0 fusion.38
  396.6 5.1 convolution_convert_fusion.3
  401.8 77.0 %all-gather.3.cloned.1.call-done = bf16[2,2,256,1600]{2,1,0,3:T(2,128)(2,1)} async-done(((bf16[2,2,256,100]{2,1,0,3:T(2,128)(2,1)}), bf16[2,2,256,1600]{2,1,0,3:T(2,128)(2,1)}) %all-gather.3.cloned.1.call-update) | async-done | bytes 3276816 | tf_op jit(solution)/shard_map/all_gather | solution.py:92
  478.8 5.4 fusion.135
  484.1 138.7 %all-reduce.9.cloned.1.call-done = bf16[2,256,1600]{1,2,0:T(8,128)(2,1)} async-done(((bf16[2,256,1600]{1,2,0:T(8,128)(2,1)}), bf16[2,256,1600]{1,2,0:T(8,128)(2,1)}) %all-reduce.9.cloned.1.call-update) | async-done | bytes 1638416 | tf_op jit(solution)/shard_map/psum | solution.py:112
  622.9 3.4 convert_reduce_fusion
  628.1 34.4 %while.35 = (s32[]{:T(128)}, f32[2,1,256]{2,0,1:T(2,128)S(1)}, f32[2,1,256]{2,0,1:T(2,128)S(1)}, f32[2,1,256,64]{2,3,0,1:T(8,128)S(1)}, s32[2]{0:T(128)S(1)}, /*...) while((s32[]{:T(128)}, f32[2,1,256]{2,0,1:T(2,128)S(1)}, ...), condition=%wide.region_20.21_spmd, body=%wide.region_17.20_spmd.sunk | while | flops 140055040 | bytes 7192775 | solution.py:64
  664.6 142.5 %all-reduce.11.cloned.1.call-done = bf16[2,256,1600]{1,2,0:T(8,128)(2,1)} async-done(((bf16[2,256,1600]{1,2,0:T(8,128)(2,1)}), bf16[2,256,1600]{1,2,0:T(8,128)(2,1)}) %all-reduce.11.cloned.1.call-update) | async-done | bytes 1638416 | tf_op jit(solution)/shard_map/psum | solution.py:104
  807.1 2.0 fusion.39
  809.8 5.1 convolution_convert_fusion.2
  815.0 142.9 %all-reduce.13.cloned.1.call-done = bf16[2,256,1600]{1,2,0:T(8,128)(2,1)} async-done(((bf16[2,256,1600]{1,2,0:T(8,128)(2,1)}), bf16[2,256,1600]{1,2,0:T(8,128)(2,1)}) %all-reduce.13.cloned.1.call-update) | async-done | bytes 1638416 | tf_op jit(solution)/shard_map/psum | solution.py:112
  957.8 4.4 fusion.43
  (209 shorter events, 85.9 us)
Async XLA Ops:
  6.5 390.0 %copy-start = (bf16[400,1600]{1,0:T(8,128)(2,1)S(1)}, bf16[400,1600]{1,0:T(8,128)(2,1)}, u32[]{:S(2)}) copy-start(bf16[400,1600]{1,0:T(8,128)(2,1)} %param.20) | copy-start | bytes 3840004
  6.5 80.7 %all-gather.5.cloned.1.call-start = ((), (), s32[]{:S(2)}) async-start(), calls=%async_computation.1 | async-start | bytes 8912896 | tf_op jit(solution)/shard_map/all_gather | solution.py:79
  7.3 230.1 %all-reduce.15.cloned.1.call-start = ((), (), s32[]{:S(2)}) async-start(), calls=%async_computation.6 | async-start | bytes 6553600
  82.3 1.5 copy-start.2
  82.3 311.5 %all-reduce.7.cloned.1.call-start = ((), (), s32[]{:S(2)}) async-start(), calls=%async_computation.2 | async-start | bytes 3276800 | tf_op jit(solution)/shard_map/psum | solution.py:104
  83.8 1.1 copy-start.11
  84.9 1.3 copy-start.10
  84.9 1.4 copy-start.1
  85.5 7.5 copy-start.7
  105.8 6.4 slice-start
  112.2 34.5 %copy-start.8 = (bf16[1,64,1600]{2,1,0:T(8,128)(2,1)S(1)}, bf16[1,64,1600]{2,1,0:T(8,128)(2,1)}, u32[]{:S(2)}) copy-start(bf16[1,64,1600]{2,1,0:T(8,128)(2,1)} %param.18) | copy-start | bytes 614404
  146.7 1.9 copy-start.13
  148.6 330.2 %all-gather.3.cloned.1.call-start = ((), (), s32[]{:S(2)}) async-start(), calls=%async_computation | async-start | bytes 3481600 | tf_op jit(solution)/shard_map/all_gather | solution.py:92
  239.3 383.6 %all-reduce.9.cloned.1.call-start = ((), (), s32[]{:S(2)}) async-start(), calls=%async_computation.3 | async-start | bytes 3276800 | tf_op jit(solution)/shard_map/psum | solution.py:112
  393.9 2.0 copy-start.5
  396.6 5.2 copy-start.9
  401.7 405.4 %all-reduce.11.cloned.1.call-start = ((), (), s32[]{:S(2)}) async-start(), calls=%async_computation.4 | async-start | bytes 3276800 | tf_op jit(solution)/shard_map/psum | solution.py:104
  622.9 3.9 copy-start.12
  626.3 1.2 copy-start.3
  662.5 144.6 %copy-start.4 = (bf16[2,256,1600]{1,2,0:T(8,128)(2,1)S(1)}, bf16[2,256,1600]{1,2,0:T(8,128)(2,1)}, u32[]{:S(2)}) copy-start(bf16[2,256,1600]{1,2,0:T(8,128)(2,1)} %copy-done.3) | copy-start | bytes 4915204
  664.3 293.5 %all-reduce.13.cloned.1.call-start = ((), (), s32[]{:S(2)}) async-start(), calls=%async_computation.5 | async-start | bytes 3276800 | tf_op jit(solution)/shard_map/psum | solution.py:112
  807.1 2.0 copy-start.6
Sparse Core Ops, SparseCore 0:
  10.1 77.1 all-gather.4
  89.9 147.3 all-reduce.14
  240.0 153.7 all-reduce.6
  395.6 83.0 all-gather.2
  481.5 141.3 all-reduce.8
  664.5 142.6 all-reduce.10
  815.1 142.7 all-reduce.12
where the time goes:
time: 971 us; the launch traced here: 969 us
  waiting for transfers between devices  744 us (77%)
  local copies, waits for them, and re-layouts  103 us (11%)
  matrix products  72.2 us (7%)
  other arithmetic  33.7 us (3%)
  between operations  14.4 us (1%)
    psum x2, waiting for transfers between devices, shards(): lax.psum(partial_terms.astype(jnp.bfloat16), 'blk').astype(jnp.float32)  297 us
    psum x2, waiting for transfers between devices, shards(): lax.psum(grown_rows.astype(jnp.bfloat16), 'blk').astype(jnp.float32)  282 us
    unnamed x8, waiting for transfers between devices  88.3 us
    all_gather x1, waiting for transfers between devices, shards(): fresh_rows = lax.all_gather(picked, 'blk', axis=3, tiled=True)  77 us
    gather x2, local copies, waits for them, and re-layouts, shards(): looked = jnp.take(embed_table, jnp.clip(relative, 0, vocab_dev - 1), axis=0)  65.1 us
    dot_general x16, matrix products, visit_block(): jnp.einsum('rhqk,rkhd->rhqd', weights_raw.astype(jnp.bfloat16), cache_pie...  29.2 us
    dot_general x16, matrix products, visit_block(): jnp.einsum('rqhd,rkhd->rhqk', queries, cache_piece[..., :head_dim], prefe...  26.9 us
  transfers between devices with their start and end apart: 7, of which 7 were waited for; matrix products, arithmetic and copies ran while one was open for 16% of the time, Pallas kernels for 0%

commit v1 on v0

v1 whole, which is shorter than its diff:
```python
import functools

import jax
import jax.numpy as jnp
from jax import lax
from jax.experimental import pallas as pl
from jax.experimental.pallas import tpu as pltpu
from jax.sharding import PartitionSpec as P

PASSES = 2
MESH = pl.DeviceIdType.MESH
NEG = -1e30


def layer_norm(values):
    centre = values - jnp.mean(values, -1, keepdims=True)
    spread = jnp.mean(centre * centre, -1, keepdims=True)
    return centre * lax.rsqrt(spread + 1e-05)


class Net:
    def __init__(self):
        blk = lax.axis_index("blk")
        self.z = blk // 2
        self.x = blk % 2
        self.right = self.ring(1) * 2 + self.x
        self.left = self.ring(-1) * 2 + self.x
        self.pair = self.z * 2 + 1 - self.x
        self.started = []

    def ring(self, offset):
        return lax.rem(self.z + 8 + offset, 8)

    def greet(self):
        barrier = pltpu.get_barrier_semaphore()
        for other in (self.right, self.left, self.pair):
            pl.semaphore_signal(barrier, inc=1, device_id={"blk": other}, device_id_type=MESH)
        pl.semaphore_wait(barrier, 3)

    def send(self, src, dst, sems, slot, other):
        copy = pltpu.make_async_remote_copy(
            src_ref=src,
            dst_ref=dst,
            send_sem=sems[0].at[slot],
            recv_sem=sems[1].at[slot],
            device_id={"blk": other},
            device_id_type=MESH,
        )
        copy.start()
        self.started.append(copy)

    def arrived(self, dst, sems, slot):
        pltpu.make_async_remote_copy(
            src_ref=dst,
            dst_ref=dst,
            send_sem=sems[0].at[slot],
            recv_sem=sems[1].at[slot],
            device_id={"blk": self.pair},
            device_id_type=MESH,
        ).wait_recv()

    def finish(self):
        for copy in self.started:
            copy.wait_send()


R_A, R_B, R_O, L_A, L_B, L_O, X_A, X_B = 0, 4, 8, 12, 16, 20, 24, 25
GATHER_SLOTS = 33


def gather_begin_low(net, out, sems, half):
    low = out.at[net.z, net.x, 0:half]
    net.send(low, low, sems, R_A + 0, net.right)
    net.send(low, low, sems, L_A + 0, net.left)
    net.send(low, low, sems, X_A, net.pair)


def gather_begin_high(net, out, sems, half):
    high = out.at[net.z, net.x, half : 2 * half]
    net.send(high, high, sems, R_B + 0, net.right)
    net.send(high, high, sems, L_B + 0, net.left)
    net.send(high, high, sems, X_B + 0, net.pair)


def gather_rest(net, out, sems, half):
    other = 1 - net.x
    peer_low = out.at[net.z, other, 0:half]
    net.arrived(peer_low, sems, X_A)
    net.send(peer_low, peer_low, sems, R_O + 0, net.right)
    net.send(peer_low, peer_low, sems, L_O + 0, net.left)
    for step in range(1, 5):
        before, after = net.ring(-step), net.ring(step)
        piece = out.at[before, net.x, 0:half]
        net.arrived(piece, sems, R_A + step - 1)
        if step < 4:
            net.send(piece, piece, sems, R_A + step, net.right)
        piece = out.at[after, net.x, half : 2 * half]
        net.arrived(piece, sems, L_B + step - 1)
        if step < 4:
            net.send(piece, piece, sems, L_B + step, net.left)
        net.send(piece, piece, sems, X_B + (step if step < 4 else 7), net.pair)
        piece = out.at[after, other, 0:half]
        net.arrived(piece, sems, L_O + step - 1)
        if step < 4:
            net.send(piece, piece, sems, L_O + step, net.left)
        if step < 4:
            piece = out.at[after, net.x, 0:half]
            net.arrived(piece, sems, L_A + step - 1)
            if step < 3:
                net.send(piece, piece, sems, L_A + step, net.left)
            piece = out.at[before, net.x, half : 2 * half]
            net.arrived(piece, sems, R_B + step - 1)
            if step < 3:
                net.send(piece, piece, sems, R_B + step, net.right)
            net.send(piece, piece, sems, X_B + 3 + step, net.pair)
            piece = out.at[before, other, 0:half]
            net.arrived(piece, sems, R_O + step - 1)
            if step < 3:
                net.send(piece, piece, sems, R_O + step, net.right)
    for slot, offset in ((0, 0), (1, 1), (2, 2), (3, 3), (7, 4), (4, -1), (5, -2), (6, -3)):
        net.arrived(out.at[net.ring(offset), other, half : 2 * half], sems, X_B + slot)


def gather_kernel(x_ref, out, send_sems, recv_sems):
    net = Net()
    sems = (send_sems, recv_sems)
    half = x_ref.shape[0] // 2
    out[net.z, net.x] = x_ref[...]
    net.greet()
    gather_begin_low(net, out, sems, half)
    gather_begin_high(net, out, sems, half)
    gather_rest(net, out, sems, half)
    net.finish()


def gather_blk(x, collective_id):
    return pl.pallas_call(
        gather_kernel,
        out_shape=jax.ShapeDtypeStruct((8, 2) + x.shape, x.dtype),
        in_specs=[pl.BlockSpec(memory_space=pltpu.VMEM)],
        out_specs=pl.BlockSpec(memory_space=pltpu.VMEM),
        scratch_shapes=[
            pltpu.SemaphoreType.DMA((GATHER_SLOTS,)),
            pltpu.SemaphoreType.DMA((GATHER_SLOTS,)),
        ],
        compiler_params=pltpu.CompilerParams(
            collective_id=collective_id, has_side_effects=True, vmem_limit_bytes=32 << 20
        ),
        name=f"gather_blk_{collective_id}",
    )(x)


P_B, P_A, RR_A, RR_B, LL_A, LL_B = 0, 8, 9, 13, 16, 19
REDUCE_SLOTS = 23


def reduce_kernel(
    part, middle, fresh, accept, out,
    peer_high, peer_low, stage_low, to_right, to_left, right_low, right_high, left_low, left_high,
    send_r, recv_r, send_g, recv_g,
):
    net = Net()
    sems, gather_sems = (send_r, recv_r), (send_g, recv_g)
    half = part.shape[2] // 2
    other = 1 - net.x
    f32 = jnp.float32
    net.greet()

    for slot, offset in enumerate((4, 3, -3, 2, -2, 1, -1, 0)):
        place = net.ring(offset)
        net.send(part.at[place, other, half : 2 * half], peer_high.at[slot], sems, P_B + slot, net.pair)
        if slot == 0:
            net.send(part.at[place, :, 0:half], right_low.at[0], sems, RR_A, net.right)
            place = net.ring(-3)
            net.send(part.at[place, :, 0:half], left_low.at[0], sems, LL_A, net.left)

    def own_high(slot, offset):
        net.arrived(peer_high.at[slot], sems, P_B + slot)
        mine = part[net.ring(offset), net.x, half : 2 * half]
        return mine.astype(f32) + peer_high[slot].astype(f32)

    to_left[...] = own_high(0, 4).astype(jnp.bfloat16)
    net.send(to_left, left_high.at[0], sems, LL_B, net.left)
    to_right[...] = own_high(1, 3).astype(jnp.bfloat16)
    net.send(to_right, right_high.at[0], sems, RR_B, net.right)

    def pass_low(buf, slot, step, offset, target):
        piece = buf.at[step]
        net.arrived(piece, sems, slot + step)
        total = piece[...].astype(f32) + part[net.ring(offset), :, 0:half].astype(f32)
        buf[step] = total.astype(jnp.bfloat16)
        net.send(piece, buf.at[step + 1], sems, slot + step + 1, target)

    def pass_high(buf, slot, step, peer_slot, offset, target):
        total = own_high(peer_slot, offset)
        piece = buf.at[step]
        net.arrived(piece, sems, slot + step)
        buf[step] = (total + piece[...].astype(f32)).astype(jnp.bfloat16)
        net.send(piece, buf.at[step + 1], sems, slot + step + 1, target)

    pass_low(right_low, RR_A, 0, 3, net.right)
    pass_low(left_low, LL_A, 0, -2, net.left)
    pass_high(left_high, LL_B, 0, 2, -3, net.left)
    pass_high(right_high, RR_B, 0, 3, 2, net.right)
    pass_low(right_low, RR_A, 1, 2, net.right)
    pass_low(left_low, LL_A, 1, -1, net.left)
    pass_high(left_high, LL_B, 1, 4, -2, net.left)
    pass_high(right_high, RR_B, 1, 5, 1, net.right)
    pass_low(right_low, RR_A, 2, 1, net.right)
    pass_high(left_high, LL_B, 2, 6, -1, net.left)

    net.arrived(left_low.at[2], sems, LL_A + 2)
    net.arrived(right_low.at[3], sems, RR_A + 3)

    def low_total(parity):
        return (
            part[net.z, parity, 0:half].astype(f32)
            + right_low[3, parity].astype(f32)
            + left_low[2, parity].astype(f32)
        )

    stage_low[...] = low_total(other).astype(jnp.bfloat16)
    net.send(stage_low, peer_low, sems, P_A, net.pair)

    def close(total, rows):
        layer_out = (middle[rows] + total).astype(jnp.bfloat16)
        out[net.z, net.x, rows] = jnp.where(accept[rows] == 1, fresh[rows], layer_out)

    total = own_high(7, 0)
    net.arrived(right_high.at[2], sems, RR_B + 2)
    net.arrived(left_high.at[3], sems, LL_B + 3)
    total = total + right_high[2].astype(f32) + left_high[3].astype(f32)
    close(total, slice(half, 2 * half))
    gather_begin_high(net, out, gather_sems, half)
    total = low_total(net.x)
    net.arrived(peer_low, sems, P_A)
    close(total + peer_low[...].astype(f32), slice(0, half))
    gather_begin_low(net, out, gather_sems, half)
    gather_rest(net, out, gather_sems, half)
    net.finish()


def reduce_blk(part, middle, fresh, accept, collective_id):
    _, _, rows, width = part.shape
    half = rows // 2
    block = (half, width)
    bf16 = jnp.bfloat16
    return pl.pallas_call(
        reduce_kernel,
        out_shape=jax.ShapeDtypeStruct(part.shape, bf16),
        in_specs=[pl.BlockSpec(memory_space=pltpu.VMEM)] * 4,
        out_specs=pl.BlockSpec(memory_space=pltpu.VMEM),
        scratch_shapes=[
            pltpu.VMEM((8,) + block, bf16),
            pltpu.VMEM(block, bf16),
            pltpu.VMEM(block, bf16),
            pltpu.VMEM(block, bf16),
            pltpu.VMEM(block, bf16),
            pltpu.VMEM((4, 2) + block, bf16),
            pltpu.VMEM((3,) + block, bf16),
            pltpu.VMEM((3, 2) + block, bf16),
            pltpu.VMEM((4,) + block, bf16),
            pltpu.SemaphoreType.DMA((REDUCE_SLOTS,)),
            pltpu.SemaphoreType.DMA((REDUCE_SLOTS,)),
            pltpu.SemaphoreType.DMA((GATHER_SLOTS,)),
            pltpu.SemaphoreType.DMA((GATHER_SLOTS,)),
        ],
        compiler_params=pltpu.CompilerParams(
            collective_id=collective_id, has_side_effects=True, vmem_limit_bytes=32 << 20
        ),
        name=f"reduce_blk_{collective_id}",
    )(part, middle, fresh, accept)


def attend_kernel(groups, lengths, queries, own, cache, out, span):
    request = pl.program_id(0)
    length = lengths[request]
    q = queries[0]
    rows = q.shape[0]
    f32 = jnp.float32

    def scores_of(keys):
        return lax.dot_general(q, keys, (((1,), (1,)), ((), ())), preferred_element_type=f32)

    def weigh(weights, values):
        return jnp.dot(weights.astype(jnp.bfloat16), values, preferred_element_type=f32)

    own_block = own[0]
    scores = scores_of(own_block)
    top = jnp.max(scores, -1, keepdims=True)
    weights = jnp.exp(scores - top)
    total = jnp.sum(weights, -1, keepdims=True)
    mixed = weigh(weights, own_block)

    def visit(index, carried):
        top, total, mixed = carried
        start = pl.multiple_of(index * span, span)
        block = cache[0, pl.ds(start, span), :]
        position = start + lax.broadcasted_iota(jnp.int32, (1, span), 1)
        bias = jnp.where(position < length, 0.0, NEG).astype(f32)
        scores = scores_of(block) + bias
        raised = jnp.maximum(top, jnp.max(scores, -1, keepdims=True))
        shrink = jnp.exp(top - raised)
        weights = jnp.exp(scores - raised)
        total = total * shrink + jnp.sum(weights, -1, keepdims=True)
        return raised, total, mixed * shrink + weigh(weights, block)

    blocks = (length + span - 1) // span
    top, total, mixed = lax.fori_loop(0, blocks, visit, (top, total, mixed))
    head = (mixed / total).astype(f32)
    lane = lax.broadcasted_iota(jnp.int32, (rows, 128), 1)

    @pl.when(request == 0)
    def _():
        out[...] = pltpu.roll(head, 64, 1).astype(out.dtype)

    @pl.when(request == 1)
    def _():
        out[...] = jnp.where(lane < 64, out[...].astype(f32), head).astype(out.dtype)


def attend(queries, own, cache, groups, lengths):
    requests, rows, _ = queries.shape
    size = cache.shape[1]
    return pl.pallas_call(
        functools.partial(attend_kernel, span=1024),
        out_shape=jax.ShapeDtypeStruct((rows, 128), jnp.bfloat16),
        grid_spec=pltpu.PrefetchScalarGridSpec(
            num_scalar_prefetch=2,
            grid=(requests,),
            in_specs=[
                pl.BlockSpec((1, rows, 128), lambda r, g, n: (r, 0, 0)),
                pl.BlockSpec((1, rows, 128), lambda r, g, n: (r, 0, 0)),
                pl.BlockSpec((1, size, 128), lambda r, g, n: (g[r], 0, 0)),
            ],
            out_specs=pl.BlockSpec((rows, 128), lambda r, g, n: (0, 0)),
        ),
        compiler_params=pltpu.CompilerParams(vmem_limit_bytes=40 << 20),
        name="attend",
    )(groups, lengths, queries, own, cache)


def shards(
    tokens, cache_kv, w_qkv, w_out, w_fc, w_proj, embed_table, group_ids, cache_len, accept, new_ids
):
    req_index = lax.axis_index("req")
    blk_index = lax.axis_index("blk")
    requests, rows, width = tokens.shape
    kv_width = cache_kv.shape[3]
    head_dim = kv_width // 2
    all_rows = requests * rows
    share = all_rows // 16
    bf16, f32 = jnp.bfloat16, jnp.float32
    my_groups = lax.dynamic_slice_in_dim(group_ids, req_index * requests, requests)
    lengths = jnp.take(cache_len, my_groups)
    every_cache = lax.all_gather(cache_kv[:, :, 0, :], "req", axis=1, tiled=True)
    all_w_out = lax.all_gather(w_out[0], "blk", axis=0, tiled=True)
    vocab_dev = embed_table.shape[0]
    relative = new_ids - req_index * vocab_dev
    inside = (relative >= 0) & (relative < vocab_dev)
    looked = jnp.take(embed_table, jnp.clip(relative, 0, vocab_dev - 1), axis=0)
    looked = jnp.where(inside[..., None], looked, jnp.zeros((), bf16))
    picked = lax.psum_scatter(looked, "req", scatter_dimension=1, tiled=True)
    picked = picked.reshape(PASSES, 16, share, picked.shape[-1])
    mine = lax.all_to_all(picked, "blk", split_axis=1, concat_axis=3, tiled=True)
    mine = mine.reshape(PASSES, share, width)
    my_accept = lax.dynamic_slice_in_dim(
        accept.reshape(PASSES, all_rows, 1), blk_index * share, share, 1
    )
    w_qkv = w_qkv[:, 0, :]
    w_q = jnp.pad(w_qkv[:, :head_dim], ((0, 0), (0, head_dim)))
    w_kv = w_qkv[:, head_dim:]
    current = tokens.reshape(all_rows, width)
    for pass_index in range(PASSES):
        state_f32 = current.astype(f32)
        normed = layer_norm(state_f32).astype(bf16)
        q = jnp.dot(normed, w_q, preferred_element_type=f32).astype(bf16)
        q = q * jnp.asarray(head_dim**-0.5, bf16)
        kv = jnp.dot(normed, w_kv, preferred_element_type=f32).astype(bf16)
        heads = attend(
            q.reshape(requests, rows, kv_width),
            kv.reshape(requests, rows, kv_width),
            every_cache,
            my_groups,
            lengths,
        )
        every_head = gather_blk(heads, 2 * pass_index + 1).reshape(16, rows, requests, head_dim)
        head_rows = jnp.transpose(every_head, (2, 1, 0, 3)).reshape(all_rows, 16 * head_dim)
        middle = state_f32 + jnp.dot(head_rows, all_w_out, preferred_element_type=f32)
        normed_mid = layer_norm(middle).astype(bf16)
        hidden = jax.nn.gelu(
            jnp.dot(normed_mid, w_fc, preferred_element_type=f32), approximate=True
        ).astype(bf16)
        grown = jnp.dot(hidden, w_proj, preferred_element_type=f32).astype(bf16)
        my_middle = lax.dynamic_slice_in_dim(middle, blk_index * share, share, 0)
        current = reduce_blk(
            grown.reshape(8, 2, share, width),
            my_middle,
            mine[pass_index],
            my_accept[pass_index],
            2 * pass_index + 2,
        ).reshape(all_rows, width)
    return current.reshape(requests, rows, width)


def solution(mesh):
    return jax.shard_map(
        shards,
        mesh=mesh,
        in_specs=(
            P("req", None, None),
            P(None, "req", "blk", None),
            P(None, "blk", None),
            P("blk", None, None),
            P(None, "blk"),
            P("blk", None),
            P("req", "blk"),
            P(),
            P(),
            P(None, "req", None),
            P(),
        ),
        out_specs=P("req", None, None),
        check_vma=False,
    )
```

time: 971 us -> 590 us (0.61)
  waiting for transfers between devices: 744 us -> 263 us
  Pallas kernels: 0 us -> 145 us
  matrix products: 72.2 us -> 22.3 us
  other arithmetic: 33.7 us -> 13.4 us
  local copies, waits for them, and re-layouts: 103 us -> 113 us
    psum x4 -> x0, waiting for transfers between devices: 578 us -> none  [the longest x2 297 us: shards(): lax.psum(partial_terms.astype(jnp.bfloat16), 'blk').astype(jnp.float32)]
    pallas_call x0 -> x6, Pallas kernels: none -> 145 us  [the longest x2 88 us: reduce_blk(): pl.pallas_call(reduce_kernel, out_shape=jax.ShapeDtypeStruct(part.shape,...]
    unnamed x8 -> x4, waiting for transfers between devices: 88.3 us -> 139 us
    dot_general x42 -> x8, matrix products: 72.2 us -> 22.3 us  [the longest x2 9.9 us: shards(): grown = jnp.dot(hidden, w_proj, preferred_element_type=f32).astype(bf16)]
    all_gather x2, waiting for transfers between devices: 77.3 us -> 114 us  [the longest x1 61.3 us: shards(): lax.all_gather(cache_kv[:, :, 0, :], 'req', axis=1, tiled=True)]
    gather x3 -> x0, local copies, waits for them, and re-layouts: 14.4 us -> none  [shards(): own_cache = jnp.take(every_cache, my_groups, axis=0)]
    unnamed x32 -> x42, local copies, waits for them, and re-layouts: 5.13 us -> 18.9 us
    reduce_sum x18 -> x0, other arithmetic: 10.3 us -> none  [the longest x16 10.1 us: visit_block(): totals = totals * shrink + jnp.sum(weights_raw, -1)]
  transfers between devices with their start and end apart: 7 -> 4, of which waited for: 7 -> 4; matrix products, arithmetic and copies ran while one was open for 16% -> 4% of each run, Pallas kernels for 0% -> 6%
where the time goes in v1:
time: 590 us; the launch traced here: 580 us
  waiting for transfers between devices  263 us (45%)
  Pallas kernels  145 us (25%)
  local copies, waits for them, and re-layouts  113 us (19%)
  matrix products  22.3 us (4%)
  between operations  14.2 us (2%)
  other arithmetic  13.4 us (2%)
  starting transfers between devices  7.86 us (1%)
    unnamed x4, waiting for transfers between devices  139 us
    pallas_call x2, Pallas kernels, reduce_blk(): pl.pallas_call(reduce_kernel, out_shape=jax.ShapeDtypeStruct(part.shape,...  88 us
    gather x2, local copies, waits for them, and re-layouts, shards(): looked = jnp.take(embed_table, jnp.clip(relative, 0, vocab_dev - 1), axis=0)  68.2 us
    all_gather x1, waiting for transfers between devices, shards(): lax.all_gather(cache_kv[:, :, 0, :], 'req', axis=1, tiled=True)  61.3 us
    all_gather x1, waiting for transfers between devices, shards(): all_w_out = lax.all_gather(w_out[0], 'blk', axis=0, tiled=True)  53 us
    pallas_call x2, Pallas kernels, gather_blk(): pl.pallas_call(gather_kernel, out_shape=jax.ShapeDtypeStruct((8, 2) + x.s...  45.6 us
    unnamed x42, local copies, waits for them, and re-layouts  18.9 us
  transfers between devices with their start and end apart: 4, of which 4 were waited for; matrix products, arithmetic and copies ran while one was open for 4% of the time, Pallas kernels for 6%

profile of v1, /device:TPU:12, one launch (start us, length us, event | category | flops | bytes accessed | tf_op | source)
XLA Modules:
  0.0 579.8 jit_solution(14501484302380631786)
XLA Ops:
  9.2 57.9 %gather_fusion.1 = bf16[16384,100]{1,0:T(8,128)(2,1)} fusion(bf16[3141,100]{1,0:T(8,128)(2,1)S(1)} %copy.48, s32[16384]{0:T(1024)S(1)} %broadcast_clamp_fusion), kind=kCustom, calls=%fused_computation.1 | custom fusion | bytes 6619136 | tf_op jit(solution)/shard_map/jit(_take)/gather | solution.py:361
  67.1 10.3 %copy.49 = bf16[2,32,256,100]{2,0,3,1:T(2,128)(2,1)} copy(bf16[2,32,256,100]{3,2,1,0:T(8,128)(2,1)} %bitcast.94) | data formatting | bytes 6553600 | tf_op jit(solution)/shard_map/jit(_take)/gather | solution.py:361
  77.4 6.8 %broadcast_select_fusion.1 = bf16[2,32,256,100]{2,0,3,1:T(2,128)(2,1)} fusion(pred[2,32,256]{2,0,1:T(4,128)(4,1)S(1)} %copy.46, bf16[2,32,256,100]{2,0,3,1:T(2,128)(2,1)} %copy.49, pred[2,32,256]{2,0,1:T(4,128)(4,1)S(1)} %copy.47), kind=kLoop, calls=%fused_computation.3 | loop fusion | flops 3276800 | bytes 6586368 | tf_op jit(solution)/shard_map/jit(_where)/select_n | solution.py:362
  85.8 2.9 copy.40
  95.5 137.5 %all-reduce.3.cloned.1.call-done = bf16[2,32,256,100]{2,0,3,1:T(2,128)(2,1)} async-done(((bf16[2,32,256,100]{2,0,3,1:T(2,128)(2,1)}), bf16[2,32,256,100]{2,0,3,1:T(2,128)(2,1)}) %all-reduce.3.cloned.1.call-update) | async-done | bytes 3276816
  238.3 7.8 %all-to-all-start = ((bf16[2,16,32,100]{3,2,0,1:T(8,128)(2,1)}), bf16[2,16,32,100]{3,2,0,1:T(8,128)(2,1)}, u32[]{:S(2)}, u32[]{:S(2)}) async-start(bf16[2,16,32,100]{3,2,0,1:T(8,128)(2,1)} %copy.51), calls=%async_computation | async-start | bytes 524288 | tf_op jit(solution)/shard_map/all_to_all | solution.py:365
  248.0 10.3 %all-to-all-done = bf16[2,16,32,100]{3,2,0,1:T(8,128)(2,1)} async-done(((bf16[2,16,32,100]{3,2,0,1:T(8,128)(2,1)}), bf16[2,16,32,100]{3,2,0,1:T(8,128)(2,1)}, u32[]{:S(2)}, u32[]{:S(2)}) %all-to-all-start) | async-done | bytes 204832 | tf_op jit(solution)/shard_map/all_to_all | solution.py:365
  259.8 61.3 %all-gather.5.cloned.1.call-done = bf16[4,8192,1,128]{3,1,0,2:T(8,128)(2,1)} async-done(((bf16[4,512,1,128]{3,1,0,2:T(8,128)(2,1)}), bf16[4,8192,1,128]{3,1,0,2:T(8,128)(2,1)}) %all-gather.5.cloned.1.call-update) | async-done | bytes 8388624 | tf_op jit(solution)/shard_map/all_gather | solution.py:356
  321.1 3.4 copy-done.1
  324.5 5.8 %attend.2.x_ref = bf16[256,128]{1,0:T(8,128)(2,1)S(1)} custom-call(s32[2]{0:T(128)S(1)} %get-tuple-element.8.groups, s32[2]{0:T(128)S(1)} %and_select_fusion.lengths, bf16[2,256,128]{2,1,0:T(8,128)(2,1)S(1)} %bitcast.92, bf16[2,256,128]{2,1,0:T(8,128)(2,1)S(1)} %bitcast.90, bf16[4,8192,128]{2,1,0:T(8,128)(2,1)S(1)} %bitcast.85), custom_call_target="tpu_custom_call" | custom-call | tf_op jit(solution)/shard_map/attend/pallas_call | solution.py:325
  330.3 26.9 %gather_blk_1.1 = bf16[8,2,256,128]{3,2,1,0:T(8,128)(2,1)S(1)} custom-call(bf16[256,128]{1,0:T(8,128)(2,1)S(1)} %attend.2.x_ref), custom_call_target="tpu_custom_call" | custom-call | tf_op jit(solution)/shard_map/gather_blk_1/pallas_call | solution.py:137
  361.0 53.0 %all-gather.7.cloned.1.call-done = bf16[1,1024,1600]{2,1,0:T(8,128)(2,1)} async-done(((bf16[1,64,1600]{2,1,0:T(8,128)(2,1)}), bf16[1,1024,1600]{2,1,0:T(8,128)(2,1)}) %all-gather.7.cloned.1.call-update) | async-done | bytes 3276816 | tf_op jit(solution)/shard_map/all_gather | solution.py:357
  414.1 5.4 fusion.62
  421.8 4.5 convolution_convert_fusion.1
  426.3 2.5 copy.45
  430.3 45.2 %reduce_blk_2.1 = bf16[8,2,32,1600]{3,2,1,0:T(8,128)(2,1)S(1)} custom-call(bf16[8,2,32,1600]{3,2,1,0:T(8,128)(2,1)S(1)} %bitcast.87, f32[32,1600]{1,0:T(8,128)S(1)} %constant_dynamic-slice_fusion.3.middle, bf16[32,1600]{1,0:T(8,128)(2,1)S(1)} %squeeze.24.fresh, s32[32,1]{1,0:T(8,128)S(1)} %copy.54.accept), custom_call_target="tpu_custom_call" | custom-call | tf_op jit(solution)/shard_map/reduce_blk_2/pallas_call | solution.py:248
  479.0 3.4 copy-done.2
  482.4 5.8 %attend.3.x_ref = bf16[256,128]{1,0:T(8,128)(2,1)S(1)} custom-call(s32[2]{0:T(128)S(1)} %get-tuple-element.8.groups, s32[2]{0:T(128)S(1)} %and_select_fusion.lengths, bf16[2,256,128]{2,1,0:T(8,128)(2,1)S(1)} %bitcast.93, bf16[2,256,128]{2,1,0:T(8,128)(2,1)S(1)} %bitcast.91, bf16[4,8192,128]{2,1,0:T(8,128)(2,1)S(1)} %bitcast.86), custom_call_target="tpu_custom_call" | custom-call | tf_op jit(solution)/shard_map/attend/pallas_call | solution.py:325
  488.2 18.7 %gather_blk_3.1 = bf16[8,2,256,128]{3,2,1,0:T(8,128)(2,1)S(1)} custom-call(bf16[256,128]{1,0:T(8,128)(2,1)S(1)} %attend.3.x_ref), custom_call_target="tpu_custom_call" | custom-call | tf_op jit(solution)/shard_map/gather_blk_3/pallas_call | solution.py:137
  510.1 2.5 copy.56
  517.5 5.4 convolution_convert_fusion
  522.9 2.7 copy.58
  525.6 42.8 %reduce_blk_4.1 = bf16[8,2,32,1600]{3,2,1,0:T(8,128)(2,1)S(1)} custom-call(bf16[8,2,32,1600]{3,2,1,0:T(8,128)(2,1)S(1)} %bitcast.88, f32[32,1600]{1,0:T(8,128)S(1)} %constant_dynamic-slice_fusion.1.middle, bf16[32,1600]{1,0:T(8,128)(2,1)S(1)} %squeeze.26.fresh, s32[32,1]{1,0:T(8,128)S(1)} %copy.60.accept), custom_call_target="tpu_custom_call" | custom-call | tf_op jit(solution)/shard_map/reduce_blk_4/pallas_call | solution.py:248
  569.6 3.6 copy.61
  (93 shorter events, 39.3 us)
Async XLA Ops:
  6.5 415.2 %copy-start = (bf16[400,1600]{1,0:T(8,128)(2,1)S(1)}, bf16[400,1600]{1,0:T(8,128)(2,1)}, u32[]{:S(2)}) copy-start(bf16[400,1600]{1,0:T(8,128)(2,1)} %param.16) | copy-start | bytes 3840004
  6.5 226.5 %all-reduce.3.cloned.1.call-start = ((), (), s32[]{:S(2)}) async-start(), calls=%async_computation.3 | async-start | bytes 6553600
  84.2 1.5 copy-start.7
  84.3 236.8 %all-gather.5.cloned.1.call-start = ((), (), s32[]{:S(2)}) async-start(), calls=%async_computation.1 | async-start | bytes 8912896 | tf_op jit(solution)/shard_map/all_gather | solution.py:356
  85.0 329.0 %all-gather.7.cloned.1.call-start = ((), (), s32[]{:S(2)}) async-start(), calls=%async_computation.2 | async-start | bytes 3620864 | tf_op jit(solution)/shard_map/all_gather | solution.py:357
  85.8 3.7 copy-start.12
  85.8 3.7 copy-start.15
  85.8 5.0 copy-start.13
  85.8 5.1 copy-start.6
  93.9 152.4 %copy-start.16 = (pred[128]{0:T(512)(128)(4,1)S(1)}, pred[128]{0:T(512)(128)(4,1)}, u32[]{:S(2)}) copy-start(pred[128]{0:T(512)(128)(4,1)} %constant.67.clone.1) | copy-start | bytes 388
  238.3 20.0 %all-to-all-start = ((bf16[2,16,32,100]{3,2,0,1:T(8,128)(2,1)}), bf16[2,16,32,100]{3,2,0,1:T(8,128)(2,1)}, u32[]{:S(2)}, u32[]{:S(2)}) async-start(bf16[2,16,32,100]{3,2,0,1:T(8,128)(2,1)} %copy.51), calls=%async_computation | async-start | bytes 524288 | tf_op jit(solution)/shard_map/all_to_all | solution.py:365
  321.1 3.4 copy-start.1
  419.5 1.8 copy-start.8
  428.8 1.5 copy-start.3
  476.6 1.1 copy-start.11
  479.0 3.4 copy-start.2
  506.9 1.0 copy-start.5
  510.1 2.7 copy-start.10
  515.2 1.7 copy-start.9
  515.2 2.3 copy-start.14
  568.4 1.2 copy-start.4
Sparse Core Ops, SparseCore 0:
  84.4 148.5 all-reduce.2
  235.8 85.2 all-gather.4
  322.9 91.1 all-gather.6

commit v2 on v1

--- a/solution.py
+++ b/solution.py
@@ -272,6 +272,166 @@
     )(part, middle, fresh, accept)
 
 
+PIECES = (0, 2, 1, 3)
+
+
+def gather_req_kernel(own, out, copy_sem, send_sems, recv_sems):
+    me = lax.axis_index("req")
+    y, x, core = me // 4, (me // 2) % 2, me % 2
+
+    def device(step, other_x, other_core=False):
+        return (
+            lax.rem(y + 4 + step, 4) * 4
+            + (1 - x if other_x else x) * 2
+            + (1 - core if other_core else core)
+        )
+
+    up, down, side, twin = device(1, 0), device(-1, 0), device(0, 1), device(0, 0, True)
+    barrier = pltpu.get_barrier_semaphore()
+    for other in (up, down, side, twin):
+        pl.semaphore_signal(barrier, inc=1, device_id={"req": other}, device_id_type=MESH)
+    pl.semaphore_wait(barrier, 4)
+    started = []
+
+    def copy_of(src, dst, slot, other):
+        return pltpu.make_async_remote_copy(
+            src_ref=src,
+            dst_ref=dst,
+            send_sem=send_sems.at[slot],
+            recv_sem=recv_sems.at[slot],
+            device_id={"req": other},
+            device_id_type=MESH,
+        )
+
+    def send(src, dst, slot, other):
+        copy = copy_of(src, dst, slot, other)
+        copy.start()
+        started.append(copy)
+
+    def arrived(dst, slot):
+        copy_of(dst, dst, slot, twin).wait_recv()
+
+    U0, D0, SIDE, U1, D1, UF0, UF1, DF0, DF1, TWIN = 0, 4, 8, 12, 16, 20, 22, 24, 26, 28
+    places = {(0, 0): 0, (0, 1): 1, (-1, 0): 2, (1, 0): 3, (-1, 1): 4, (1, 1): 5, (2, 0): 6, (2, 1): 7}
+
+    def share(step, other_x, g):
+        piece = out.at[g, device(step, other_x)]
+        send(piece, piece, TWIN + 4 * places[(step, other_x)] + g, twin)
+
+    for g in PIECES:
+        dst = out.at[g, me]
+        send(own.at[g], dst, U0 + g, up)
+        send(own.at[g], dst, D0 + g, down)
+        send(own.at[g], dst, SIDE + g, side)
+    keep = pltpu.make_async_copy(own, out.at[:, me], copy_sem)
+    keep.start()
+    for g in PIECES:
+        send(own.at[g], out.at[g, me], TWIN + g, twin)
+
+    def from_below(g, other_x, base, forward):
+        piece = out.at[g, device(-1, other_x)]
+        arrived(piece, base + g)
+        if g < 2:
+            send(piece, piece, forward + g, up)
+        share(-1, other_x, g)
+
+    def from_above(g, other_x, base, forward):
+        piece = out.at[g, device(1, other_x)]
+        arrived(piece, base + g)
+        if g >= 2:
+            send(piece, piece, forward + g - 2, down)
+        share(1, other_x, g)
+
+    def from_far(g, other_x):
+        piece = out.at[g, device(2, other_x)]
+        if g < 2:
+            arrived(piece, (UF1 if other_x else UF0) + g)
+        else:
+            arrived(piece, (DF1 if other_x else DF0) + g - 2)
+        share(2, other_x, g)
+
+    for g in PIECES:
+        piece = out.at[g, side]
+        arrived(piece, SIDE + g)
+        send(piece, piece, U1 + g, up)
+        send(piece, piece, D1 + g, down)
+        share(0, 1, g)
+        from_below(g, 0, U0, UF0)
+        from_above(g, 0, D0, DF0)
+    for g in PIECES:
+        from_far(g, 0)
+        from_below(g, 1, U1, UF1)
+        from_above(g, 1, D1, DF1)
+    for g in PIECES:
+        from_far(g, 1)
+    for (step, other_x), place in places.items():
+        for g in PIECES:
+            arrived(out.at[g, device(step, other_x, True)], TWIN + 4 * place + g)
+    keep.wait()
+    for copy in started:
+        copy.wait_send()
+
+
+def gather_req(own, collective_id):
+    groups = own.shape[0]
+    return pl.pallas_call(
+        gather_req_kernel,
+        out_shape=jax.ShapeDtypeStruct((groups, 16) + own.shape[1:], own.dtype),
+        in_specs=[pl.BlockSpec(memory_space=pl.ANY)],
+        out_specs=pl.BlockSpec(memory_space=pl.ANY),
+        scratch_shapes=[
+            pltpu.SemaphoreType.DMA,
+            pltpu.SemaphoreType.DMA((60,)),
+            pltpu.SemaphoreType.DMA((60,)),
+        ],
+        compiler_params=pltpu.CompilerParams(
+            collective_id=collective_id, has_side_effects=True, vmem_limit_bytes=4 << 20
+        ),
+        name="gather_req",
+    )(own)
+
+
+SLOTS = 128
+
+
+def fresh_columns(embed_table, new_ids, req_index):
+    vocab_dev = embed_table.shape[0]
+    passes = new_ids.shape[0]
+    bf16 = jnp.bfloat16
+    by_device = jnp.transpose(new_ids.reshape(passes, 16, -1), (1, 0, 2)).reshape(16, -1)
+    count = by_device.shape[1]
+    earlier = (jnp.arange(count)[:, None] < jnp.arange(count)[None, :]).astype(bf16)
+
+    def ranks(inside):
+        return jnp.dot(inside.astype(bf16), earlier, preferred_element_type=jnp.float32).astype(jnp.int32)
+
+    relative = by_device - req_index * vocab_dev
+    inside = (relative >= 0) & (relative < vocab_dev)
+    rank = jnp.where(inside, ranks(inside), -1)
+    chosen = rank[:, None, :] == jnp.arange(SLOTS)[None, :, None]
+    wanted = jnp.sum(jnp.where(chosen, relative[:, None, :], 0), -1)
+    sent = jnp.take(embed_table, wanted, axis=0)
+    got = lax.all_to_all(sent, "req", split_axis=0, concat_axis=0, tiled=True)
+
+    mine = lax.dynamic_index_in_dim(by_device, req_index, 0, keepdims=True)
+    owners = jnp.arange(16)[:, None]
+    theirs = mine - owners * vocab_dev
+    theirs_inside = (theirs >= 0) & (theirs < vocab_dev)
+    place = jnp.sum(jnp.where(theirs_inside, owners * SLOTS + ranks(theirs_inside), 0), 0)
+    quick = jnp.take(got.reshape(16 * SLOTS, -1), jnp.minimum(place, 16 * SLOTS - 1), axis=0)
+
+    owner = by_device // vocab_dev
+    asked = jnp.sum((owner[:, None, :] == owners[None]).astype(jnp.int32), -1)
+    crowded = jnp.max(asked) > SLOTS
+
+    def dense():
+        looked = jnp.take(embed_table, jnp.clip(relative, 0, vocab_dev - 1).reshape(-1), axis=0)
+        looked = jnp.where(inside.reshape(-1)[:, None], looked, jnp.zeros((), bf16))
+        return lax.psum_scatter(looked, "req", scatter_dimension=0, tiled=True)
+
+    return lax.cond(crowded, dense, lambda: quick)
+
+
 def attend_kernel(groups, lengths, queries, own, cache, out, span):
     request = pl.program_id(0)
     length = lengths[request]
@@ -353,14 +513,9 @@
     bf16, f32 = jnp.bfloat16, jnp.float32
     my_groups = lax.dynamic_slice_in_dim(group_ids, req_index * requests, requests)
     lengths = jnp.take(cache_len, my_groups)
-    every_cache = lax.all_gather(cache_kv[:, :, 0, :], "req", axis=1, tiled=True)
+    every_cache = gather_req(cache_kv[:, :, 0, :], 5).reshape(cache_kv.shape[0], -1, kv_width)
     all_w_out = lax.all_gather(w_out[0], "blk", axis=0, tiled=True)
-    vocab_dev = embed_table.shape[0]
-    relative = new_ids - req_index * vocab_dev
-    inside = (relative >= 0) & (relative < vocab_dev)
-    looked = jnp.take(embed_table, jnp.clip(relative, 0, vocab_dev - 1), axis=0)
-    looked = jnp.where(inside[..., None], looked, jnp.zeros((), bf16))
-    picked = lax.psum_scatter(looked, "req", scatter_dimension=1, tiled=True)
+    picked = fresh_columns(embed_table, new_ids, req_index)
     picked = picked.reshape(PASSES, 16, share, picked.shape[-1])
     mine = lax.all_to_all(picked, "blk", split_axis=1, concat_axis=3, tiled=True)
     mine = mine.reshape(PASSES, share, width)

time: 590 us -> 328 us (0.56); the launches traced: 580 us -> 325 us
  waiting for transfers between devices: 263 us -> 4.69 us
  local copies, waits for them, and re-layouts: 113 us -> 54 us
  Pallas kernels: 145 us -> 196 us
  starting transfers between devices: 7.86 us -> 21.7 us
    unnamed x4 -> x1, waiting for transfers between devices: 139 us -> 0.55 us
    all_gather x1 -> x0, waiting for transfers between devices: 61.3 us -> none  [shards(): lax.all_gather(cache_kv[:, :, 0, :], 'req', axis=1, tiled=True)]
    gather x2 -> x3, local copies, waits for them, and re-layouts: 68.2 us -> 9.69 us  [the longest x2 6.48 us: fresh_columns(): sent = jnp.take(embed_table, wanted, axis=0)]
    all_gather x1, waiting for transfers between devices: 53 us -> 0.02 us  [shards(): all_w_out = lax.all_gather(w_out[0], 'blk', axis=0, tiled=True)]
    pallas_call x0 -> x1, Pallas kernels: none -> 41.7 us  [gather_req(): pl.pallas_call(gather_req_kernel, out_shape=jax.ShapeDtypeStruct((groups,...]
    pallas_call x2, Pallas kernels: 11.6 us -> 25.6 us  [attend(): pl.pallas_call(functools.partial(attend_kernel, span=1024), out_shape=jax...]
    all_to_all x1, waiting for transfers between devices: 10.3 us -> 0.01 us  [shards(): lax.all_to_all(picked, 'blk', split_axis=1, concat_axis=3, tiled=True)]
    all_to_all x0 -> x1, starting transfers between devices: none -> 7.34 us  [fresh_columns(): got = lax.all_to_all(sent, 'req', split_axis=0, concat_axis=0, tiled=True)]
  transfers between devices with their start and end apart: 4 -> 3, of which waited for: 4 -> 1; matrix products, arithmetic and copies ran while one was open for 4% -> 5% of each run, Pallas kernels for 6% -> 24%
where the time goes in v2:
time: 328 us; the launch traced here: 325 us
  Pallas kernels  196 us (60%)
  local copies, waits for them, and re-layouts  54 us (16%)
  matrix products  23 us (7%)
  starting transfers between devices  21.7 us (7%)
  between operations  16 us (5%)
  other arithmetic  9.7 us (3%)
  waiting for transfers between devices  4.69 us (1%)
    pallas_call x2, Pallas kernels, reduce_blk(): pl.pallas_call(reduce_kernel, out_shape=jax.ShapeDtypeStruct(part.shape,...  84.9 us
    pallas_call x2, Pallas kernels, gather_blk(): pl.pallas_call(gather_kernel, out_shape=jax.ShapeDtypeStruct((8, 2) + x.s...  43.7 us
    pallas_call x1, Pallas kernels, gather_req(): pl.pallas_call(gather_req_kernel, out_shape=jax.ShapeDtypeStruct((groups,...  41.7 us
    pallas_call x2, Pallas kernels, attend(): pl.pallas_call(functools.partial(attend_kernel, span=1024), out_shape=jax...  25.6 us
    unnamed x44, local copies, waits for them, and re-layouts  19.7 us
    all_to_all x1, starting transfers between devices, shards(): lax.all_to_all(picked, 'blk', split_axis=1, concat_axis=3, tiled=True)  14.4 us
    dot_general x2, matrix products, shards(): grown = jnp.dot(hidden, w_proj, preferred_element_type=f32).astype(bf16)  9.87 us
    dot_general x2, matrix products, shards(): jnp.dot(head_rows, all_w_out, preferred_element_type=f32)  7.76 us
  transfers between devices with their start and end apart: 3, of which 1 were waited for; matrix products, arithmetic and copies ran while one was open for 5% of the time, Pallas kernels for 24%

profile of v2, /device:TPU:12, one launch (start us, length us, event | category | flops | bytes accessed | tf_op | source)
XLA Modules:
  0.0 324.9 jit_solution(4784150822357006803)
XLA Ops:
  11.4 6.2 %gather_fusion.3 = bf16[2048,100]{1,0:T(8,128)(2,1)S(1)} fusion(bf16[3141,100]{1,0:T(8,128)(2,1)S(1)} %copy.89, s32[2048]{0:T(1024)S(1)} %fusion.57), kind=kCustom, calls=%fused_computation.3 | custom fusion | bytes 827392 | tf_op jit(solution)/shard_map/jit(_take)/gather | solution.py:413
  18.7 7.3 %all-to-all-start = ((bf16[16,128,100]{1,2,0:T(8,128)(2,1)}), bf16[16,128,100]{1,2,0:T(8,128)(2,1)S(1)}, u32[]{:S(2)}, u32[]{:S(2)}) async-start(bf16[16,128,100]{1,2,0:T(8,128)(2,1)} %broadcast_select_fusion.1), calls=%async_computation.1 | async-start | bytes 851968 | tf_op jit(solution)/shard_map/all_to_all | solution.py:414
  28.3 4.1 %all-to-all-done = bf16[16,128,100]{1,2,0:T(8,128)(2,1)S(1)} async-done(((bf16[16,128,100]{1,2,0:T(8,128)(2,1)}), bf16[16,128,100]{1,2,0:T(8,128)(2,1)S(1)}, u32[]{:S(2)}, u32[]{:S(2)}) %all-to-all-start) | async-done | bytes 409632 | tf_op jit(solution)/shard_map/all_to_all | solution.py:414
  32.4 4.6 %conditional.1 = (bf16[1024,100]{1,0:T(8,128)(2,1)}) conditional(s32[]{:T(128)} %convert_element_type.83, (s32[16]{0:T(128)S(1)}, s32[16,1024]{1,0:T(8,128)S(1)}, pred[16,1024]{1,0:T(8,128)(4,1)S(1)}, s32[16,1024]{1,0:T(8,128)S(1)}, bf16[16,128,100]{1,2,0:T(8,128)(2,1)S(1)}) %tuple.19, (pred[16,1024]{1,0:T(8,128)(4,1)S(1)}, ...), branch_computations={%region_7.9_spmd, %region_9.11_spmd} | conditional | flops 3457024 | bytes 26717184 | solution.py:432
  32.9 3.2 gather_fusion
  37.6 3.8 %copy.83 = f32[2,256,1600]{2,1,0:T(8,128)} copy(bf16[2,256,1600]{1,2,0:T(8,128)(2,1)} %param.13) | data formatting | bytes 4915200 | tf_op jit(solution)/shard_map/convert_element_type | solution.py:530
  42.2 41.7 %gather_req.1 = bf16[4,16,512,128]{3,2,1,0:T(8,128)(2,1)S(1)} custom-call(bf16[4,512,128]{2,1,0:T(8,128)(2,1)S(1)} %bitcast.112), custom_call_target="tpu_custom_call" | custom-call | tf_op jit(solution)/shard_map/gather_req/pallas_call | solution.py:377
  83.9 3.2 copy-done.1
  93.6 14.4 %all-to-all-start.1 = ((bf16[2,16,32,100]{3,2,0,1:T(8,128)(2,1)}), bf16[2,16,32,100]{3,2,0,1:T(8,128)(2,1)}, u32[]{:S(2)}, u32[]{:S(2)}) async-start(bf16[2,16,32,100]{3,2,0,1:T(8,128)(2,1)} %copy.93), calls=%async_computation.2 | async-start | bytes 524288 | tf_op jit(solution)/shard_map/all_to_all | solution.py:520
  109.6 3.4 %copy-done.2 = bf16[4,16,512,128]{3,2,1,0:T(8,128)(2,1)S(1)} copy-done((bf16[4,16,512,128]{3,2,1,0:T(8,128)(2,1)S(1)}, bf16[4,16,512,128]{3,2,1,0:T(8,128)(2,1)}, u32[]{:S(2)}) %copy-start.2) | copy-done | bytes 8388632
  113.0 12.8 %attend.2.x_ref = bf16[256,128]{1,0:T(8,128)(2,1)S(1)} custom-call(s32[2]{0:T(128)S(1)} %get-tuple-element.112.groups, s32[2]{0:T(128)S(1)} %and_select_fusion.lengths, bf16[2,256,128]{2,1,0:T(8,128)(2,1)S(1)} %bitcast.113, bf16[2,256,128]{2,1,0:T(8,128)(2,1)S(1)} %bitcast.111, bf16[4,8192,128]{2,1,0:T(8,128)(2,1)S(1)} %bitcast.105), custom_call_target="tpu_custom_call" | custom-call | tf_op jit(solution)/shard_map/attend/pallas_call | solution.py:485
  125.8 22.9 %gather_blk_1.1 = bf16[8,2,256,128]{3,2,1,0:T(8,128)(2,1)S(1)} custom-call(bf16[256,128]{1,0:T(8,128)(2,1)S(1)} %attend.2.x_ref), custom_call_target="tpu_custom_call" | custom-call | tf_op jit(solution)/shard_map/gather_blk_1/pallas_call | solution.py:137
  152.4 5.4 %fusion.73 = (f32[512]{0:T(512)S(1)}, f32[512,1600]{1,0:T(8,128)S(1)}) fusion(bf16[512,1024]{0,1:T(8,128)(2,1)S(1)} %bitcast.116, bf16[1,1024,1600]{2,1,0:T(8,128)(2,1)} %all-gather.3.cloned.1.call-done, f32[2,256,1600]{2,1,0:T(8,128)} %copy.83), kind=kOutput, calls=%fused_computation.138 | convolution fusion | flops 1679359488 | bytes 10881024 | tf_op jit(solution)/shard_map/dot_general | solution.py:544
  160.1 4.5 %convolution_convert_fusion.1 = bf16[512,1600]{0,1:T(8,128)(2,1)S(1)} fusion(bf16[400,1600]{1,0:T(8,128)(2,1)S(1)} %copy-done, bf16[1600,400]{0,1:T(8,128)(2,1)} %param.17, f32[512,1600]{1,0:T(8,128)} %copy-done.10, f32[512]{0:T(512)S(1)} %add_rsqrt_fusion.2, f32[512]{0:T(512)S(1)} %broadcast_multiply_fusion.3), kind=kOutput, calls=%fused_computation.44 | convolution fusion | flops 1315840000 | bytes 7479296 | tf_op jit(solution)/shard_map/dot_general | solution.py:549
  164.6 2.5 copy.87
  168.6 43.2 %reduce_blk_2.1 = bf16[8,2,32,1600]{3,2,1,0:T(8,128)(2,1)S(1)} custom-call(bf16[8,2,32,1600]{3,2,1,0:T(8,128)(2,1)S(1)} %bitcast.107, f32[32,1600]{1,0:T(8,128)S(1)} %constant_dynamic-slice_fusion.4.middle, bf16[32,1600]{1,0:T(8,128)(2,1)S(1)} %squeeze.24.fresh, s32[32,1]{1,0:T(8,128)S(1)} %copy.96.accept), custom_call_target="tpu_custom_call" | custom-call | tf_op jit(solution)/shard_map/reduce_blk_2/pallas_call | solution.py:248
  215.3 3.4 %copy-done.3 = bf16[4,16,512,128]{3,2,1,0:T(8,128)(2,1)S(1)} copy-done((bf16[4,16,512,128]{3,2,1,0:T(8,128)(2,1)S(1)}, bf16[4,16,512,128]{3,2,1,0:T(8,128)(2,1)}, u32[]{:S(2)}) %copy-start.3) | copy-done | bytes 8388632
  218.7 12.8 %attend.3.x_ref = bf16[256,128]{1,0:T(8,128)(2,1)S(1)} custom-call(s32[2]{0:T(128)S(1)} %get-tuple-element.112.groups, s32[2]{0:T(128)S(1)} %and_select_fusion.lengths, bf16[2,256,128]{2,1,0:T(8,128)(2,1)S(1)} %bitcast.114, bf16[2,256,128]{2,1,0:T(8,128)(2,1)S(1)} %bitcast.110, bf16[4,8192,128]{2,1,0:T(8,128)(2,1)S(1)} %bitcast.106), custom_call_target="tpu_custom_call" | custom-call | tf_op jit(solution)/shard_map/attend/pallas_call | solution.py:485
  231.5 20.8 %gather_blk_3.1 = bf16[8,2,256,128]{3,2,1,0:T(8,128)(2,1)S(1)} custom-call(bf16[256,128]{1,0:T(8,128)(2,1)S(1)} %attend.3.x_ref), custom_call_target="tpu_custom_call" | custom-call | tf_op jit(solution)/shard_map/gather_blk_3/pallas_call | solution.py:137
  255.5 2.5 copy.98
  262.9 5.3 %convolution_convert_fusion = bf16[512,1600]{0,1:T(8,128)(2,1)} fusion(bf16[400,1600]{1,0:T(8,128)(2,1)S(1)} %copy-done, bf16[1600,400]{0,1:T(8,128)(2,1)S(1)} %copy-done.17, f32[512,1600]{1,0:T(8,128)} %copy-done.11, f32[512]{0:T(512)S(1)} %add_rsqrt_fusion.1, f32[512]{0:T(512)S(1)} %broadcast_multiply_fusion.2), kind=kOutput, calls=%fused_computation.43 | convolution fusion | flops 1315840000 | bytes 7479296 | tf_op jit(solution)/shard_map/dot_general | solution.py:549
  268.2 2.7 copy.100
  271.0 41.7 %reduce_blk_4.1 = bf16[8,2,32,1600]{3,2,1,0:T(8,128)(2,1)S(1)} custom-call(bf16[8,2,32,1600]{3,2,1,0:T(8,128)(2,1)S(1)} %bitcast.108, f32[32,1600]{1,0:T(8,128)S(1)} %constant_dynamic-slice_fusion.1.middle, bf16[32,1600]{1,0:T(8,128)(2,1)S(1)} %squeeze.26.fresh, s32[32,1]{1,0:T(8,128)S(1)} %copy.102.accept), custom_call_target="tpu_custom_call" | custom-call | tf_op jit(solution)/shard_map/reduce_blk_4/pallas_call | solution.py:248
  313.8 3.6 %copy.103 = bf16[2,256,1600]{1,2,0:T(8,128)(2,1)} copy(bf16[2,256,1600]{2,1,0:T(8,128)(2,1)} %bitcast.109) | data formatting | bytes 3276800 | tf_op jit(solution)/shard_map/reshape;reshape | solution.py:558
  (111 shorter events, 37.5 us)
Async XLA Ops:
  7.4 152.7 %copy-start = (bf16[400,1600]{1,0:T(8,128)(2,1)S(1)}, bf16[400,1600]{1,0:T(8,128)(2,1)}, u32[]{:S(2)}) copy-start(bf16[400,1600]{1,0:T(8,128)(2,1)} %param.18) | copy-start | bytes 3840004
  11.4 21.0 %copy-start.13 = (bf16[3141,100]{0,1:T(8,128)(2,1)S(1)}, bf16[3141,100]{0,1:T(8,128)(2,1)}, u32[]{:S(2)}) copy-start(bf16[3141,100]{0,1:T(8,128)(2,1)} %param.19) | copy-start | bytes 1884604
  18.7 13.7 %all-to-all-start = ((bf16[16,128,100]{1,2,0:T(8,128)(2,1)}), bf16[16,128,100]{1,2,0:T(8,128)(2,1)S(1)}, u32[]{:S(2)}, u32[]{:S(2)}) async-start(bf16[16,128,100]{1,2,0:T(8,128)(2,1)} %broadcast_select_fusion.1), calls=%async_computation.1 | async-start | bytes 851968 | tf_op jit(solution)/shard_map/all_to_all | solution.py:414
  37.0 4.4 %copy-start.9 = (bf16[2,256,1600]{1,2,0:T(8,128)(2,1)S(1)}, bf16[2,256,1600]{1,2,0:T(8,128)(2,1)}, u32[]{:S(2)}) copy-start(bf16[2,256,1600]{1,2,0:T(8,128)(2,1)} %param.13) | copy-start | bytes 4915204
  37.0 115.3 %all-gather.3.cloned.1.call-start = ((), (), s32[]{:S(2)}) async-start(), calls=%async_computation.4 | async-start | bytes 3620864 | tf_op jit(solution)/shard_map/all_gather | solution.py:517
  37.6 4.6 %copy-start.7 = (bf16[4,512,1,128]{3,1,2,0:T(8,128)(2,1)S(1)}, bf16[4,512,1,128]{3,1,2,0:T(8,128)(2,1)}, u32[]{:S(2)}) copy-start(bf16[4,512,1,128]{3,1,2,0:T(8,128)(2,1)} %param.14) | copy-start | bytes 1572868
  42.2 44.9 %copy-start.16 = (s32[32]{0:T(128)S(1)}, s32[32]{0:T(128)}, u32[]{:S(2)}) copy-start(s32[32]{0:T(128)} %param.20) | copy-start | bytes 388
  42.2 45.0 %copy-start.8 = (s32[4]{0:T(128)S(1)}, s32[4]{0:T(128)}, u32[]{:S(2)}) copy-start(s32[4]{0:T(128)} %param.21) | copy-start | bytes 52
  83.9 3.2 copy-start.1
  87.1 3.1 copy-start.18
  93.6 57.3 %all-to-all-start.1 = ((bf16[2,16,32,100]{3,2,0,1:T(8,128)(2,1)}), bf16[2,16,32,100]{3,2,0,1:T(8,128)(2,1)}, u32[]{:S(2)}, u32[]{:S(2)}) async-start(bf16[2,16,32,100]{3,2,0,1:T(8,128)(2,1)} %copy.93), calls=%async_computation.2 | async-start | bytes 524288 | tf_op jit(solution)/shard_map/all_to_all | solution.py:520
  109.6 3.4 %copy-start.2 = (bf16[4,16,512,128]{3,2,1,0:T(8,128)(2,1)S(1)}, bf16[4,16,512,128]{3,2,1,0:T(8,128)(2,1)}, u32[]{:S(2)}) copy-start(bf16[4,16,512,128]{3,2,1,0:T(8,128)(2,1)} %copy-done.1) | copy-start | bytes 25165828
  148.7 1.9 copy-start.15
  157.8 1.8 copy-start.10
  167.1 1.5 copy-start.4
  212.9 1.1 copy-start.14
  215.3 3.4 %copy-start.3 = (bf16[4,16,512,128]{3,2,1,0:T(8,128)(2,1)S(1)}, bf16[4,16,512,128]{3,2,1,0:T(8,128)(2,1)}, u32[]{:S(2)}) copy-start(bf16[4,16,512,128]{3,2,1,0:T(8,128)(2,1)} %copy-done.1) | copy-start | bytes 25165828
  252.3 1.0 copy-start.6
  255.5 2.7 copy-start.12
  260.6 1.7 copy-start.11
  260.6 2.3 copy-start.17
  312.6 1.2 copy-start.5
Sparse Core Ops, SparseCore 1:
  39.4 96.3 all-gather.2

commit v3 on v0

v3 whole, which is shorter than its diff:
```python
import functools

import jax
import jax.numpy as jnp
from jax import lax
from jax.experimental import pallas as pl
from jax.experimental.pallas import tpu as pltpu
from jax.sharding import PartitionSpec as P

PASSES = 2
MESH = pl.DeviceIdType.MESH
NEG = -1e30


def layer_norm(values):
    centre = values - jnp.mean(values, -1, keepdims=True)
    spread = jnp.mean(centre * centre, -1, keepdims=True)
    return centre * lax.rsqrt(spread + 1e-05)


class Net:
    def __init__(self):
        self.blk = lax.axis_index("blk")
        self.z = self.blk // 2
        self.x = self.blk % 2
        self.right = self.ring(1) * 2 + self.x
        self.left = self.ring(-1) * 2 + self.x
        self.pair = self.z * 2 + 1 - self.x
        self.started = []

    def ring(self, offset):
        return lax.rem(self.z + 8 + offset, 8)

    def greet(self, axis="blk", others=None):
        barrier = pltpu.get_barrier_semaphore()
        others = (self.right, self.left, self.pair) if others is None else others
        for other in others:
            pl.semaphore_signal(barrier, inc=1, device_id={axis: other}, device_id_type=MESH)
        pl.semaphore_wait(barrier, len(others))

    def copy_of(self, src, dst, sems, slot, other, axis):
        return pltpu.make_async_remote_copy(
            src_ref=src,
            dst_ref=dst,
            send_sem=sems[0].at[slot],
            recv_sem=sems[1].at[slot],
            device_id={axis: other},
            device_id_type=MESH,
        )

    def send(self, src, dst, sems, slot, other, axis="blk"):
        copy = self.copy_of(src, dst, sems, slot, other, axis)
        copy.start()
        self.started.append(copy)

    def arrived(self, dst, sems, slot):
        self.copy_of(dst, dst, sems, slot, self.pair, "blk").wait_recv()

    def finish(self):
        for copy in self.started:
            copy.wait_send()


def sem_pair(count):
    return [pltpu.SemaphoreType.DMA((count,)), pltpu.SemaphoreType.DMA((count,))]


def whole(count):
    return [pl.BlockSpec(memory_space=pltpu.VMEM)] * count


RING_A, RING_B, RING_C, RING_D = 0, 4, 7, 10
RING_SLOTS = 14


def ring_begin(net, out, sems, half, high):
    piece = out.at[net.z, half : 2 * half] if high else out.at[net.z, 0:half]
    net.send(piece, piece, sems, RING_B if high else RING_A, net.right)
    net.send(piece, piece, sems, RING_D if high else RING_C, net.left)


def ring_rest(net, out, sems, half):
    def take(offset, high, slot, last, target):
        at = net.ring(offset)
        piece = out.at[at, half : 2 * half] if high else out.at[at, 0:half]
        net.arrived(piece, sems, slot)
        if not last:
            net.send(piece, piece, sems, slot + 1, target)

    for step in range(1, 5):
        take(-step, False, RING_A + step - 1, step == 4, net.right)
        take(step, True, RING_D + step - 1, step == 4, net.left)
        if step < 4:
            take(-step, True, RING_B + step - 1, step == 3, net.right)
            take(step, False, RING_C + step - 1, step == 3, net.left)


def heads_kernel(heads, *refs, with_fresh):
    if with_fresh:
        picked, out, mine, peer, copy_sem, *sem_refs = refs
    else:
        out, peer, *sem_refs = refs
    net = Net()
    ring_sems, pair_sems = tuple(sem_refs[0:2]), tuple(sem_refs[2:4])
    half = heads.shape[1] // 2
    if with_fresh:
        net.greet(others=[lax.rem(net.blk + step, 16) for step in range(1, 16)])
    else:
        net.greet()
    parts = (slice(0, half), slice(half, 2 * half))
    for part, rows in enumerate(parts):
        net.send(heads.at[1 - net.x, rows], peer.at[rows], pair_sems, part, net.pair)
    if with_fresh:
        fresh_sems = tuple(sem_refs[4:6])
        keep = pltpu.make_async_copy(picked.at[net.blk], mine.at[net.blk], copy_sem)
        keep.start()
    for part, rows in enumerate(parts):
        net.arrived(peer.at[rows], pair_sems, part)
        out[net.z, rows] = heads[net.x, rows] + peer[rows]
        ring_begin(net, out, ring_sems, half, part == 1)
    if with_fresh:
        for step in range(1, 16):
            other = lax.rem(net.blk + step, 16)
            net.send(picked.at[other], mine.at[net.blk], fresh_sems, step - 1, other)
    ring_rest(net, out, ring_sems, half)
    if with_fresh:
        for step in range(1, 16):
            net.arrived(mine.at[lax.rem(net.blk + 16 - step, 16)], fresh_sems, step - 1)
        keep.wait()
    net.finish()


def gather_heads(heads, picked, collective_id):
    _, rows, lanes = heads.shape
    with_fresh = picked is not None
    shape = jax.ShapeDtypeStruct((8, rows, lanes), heads.dtype)
    scratch = [pltpu.VMEM((rows, lanes), heads.dtype)]
    sems = sem_pair(RING_SLOTS) + sem_pair(2)
    if with_fresh:
        scratch = scratch + [pltpu.SemaphoreType.DMA]
        sems = sems + sem_pair(15)
        shapes = (shape, jax.ShapeDtypeStruct(picked.shape, picked.dtype))
        operands = (heads, picked)
    else:
        shapes, operands = (shape,), (heads,)
    return pl.pallas_call(
        functools.partial(heads_kernel, with_fresh=with_fresh),
        out_shape=shapes,
        in_specs=whole(len(operands)),
        out_specs=tuple(whole(len(shapes))),
        scratch_shapes=scratch + sems,
        compiler_params=pltpu.CompilerParams(
            collective_id=collective_id, has_side_effects=True, vmem_limit_bytes=16 << 20
        ),
        name=f"gather_heads_{collective_id}",
    )(*operands)


def mlp_kernel(
    every_head, current, w_out, w_fc, w_proj, w_fc_b, w_proj_b, w_fc_c, w_proj_c, grown, my_middle,
    head_rows, middle,
):
    f32, bf16 = jnp.float32, jnp.bfloat16
    for z in range(8):
        head_rows[:, 128 * z : 128 * (z + 1)] = every_head[z]
    middle[...] = current[...].astype(f32) + jnp.dot(
        head_rows[...], w_out[...], preferred_element_type=f32
    )
    share = my_middle.shape[0]
    start = pl.multiple_of(lax.axis_index("blk") // 2 * share, share)
    my_middle[...] = middle[pl.ds(start, share), :]
    normed = layer_norm(middle[...]).astype(bf16)

    def hidden(weights):
        raw = jnp.dot(normed, weights[...], preferred_element_type=f32)
        return jax.nn.gelu(raw, approximate=True).astype(bf16)

    def back(rows, weights):
        return jnp.dot(rows, weights[...], preferred_element_type=f32)

    first, second, third = hidden(w_fc), hidden(w_fc_b), hidden(w_fc_c)
    grown[...] = (back(first, w_proj) + back(second, w_proj_b) + back(third, w_proj_c)).astype(bf16)


def mlp(every_head, current, weights):
    rows, width = current.shape
    return pl.pallas_call(
        mlp_kernel,
        out_shape=(
            jax.ShapeDtypeStruct((rows, width), jnp.bfloat16),
            jax.ShapeDtypeStruct((rows // 8, width), jnp.float32),
        ),
        in_specs=whole(2 + len(weights)),
        out_specs=tuple(whole(2)),
        scratch_shapes=[
            pltpu.VMEM((rows, 8 * every_head.shape[2]), jnp.bfloat16),
            pltpu.VMEM((rows, width), jnp.float32),
        ],
        compiler_params=pltpu.CompilerParams(vmem_limit_bytes=40 << 20),
        name="mlp",
    )(every_head, current, *weights)


def project(rows_f32, weights):
    bf16 = jnp.bfloat16
    normed = layer_norm(rows_f32).astype(bf16)
    got = jnp.dot(normed, weights, preferred_element_type=jnp.float32).astype(bf16)
    lane = lax.broadcasted_iota(jnp.int32, (1, got.shape[1]), 1)
    return (got.astype(jnp.float32) * jnp.where(lane < 128, 0.125, 1.0)).astype(bf16)


def reduce_kernel(part, middle, fresh, accept, *refs, last):
    if last:
        out, *refs = refs
    else:
        w_own, w_pair, out, qkv, stage, *refs = refs
    right_low, right_high, left_low, left_high, *sem_refs = refs
    net = Net()
    sems, gather_sems = tuple(sem_refs[0:2]), tuple(sem_refs[2:4])
    half = part.shape[1] // 2
    f32, bf16 = jnp.float32, jnp.bfloat16
    low, high = slice(0, half), slice(half, 2 * half)
    net.greet()

    def begin(buf, rows, slot, offset, target):
        net.send(part.at[net.ring(offset), rows], buf.at[0], sems, slot, target)

    def hand_on(buf, rows, slot, step, offset, target):
        piece = buf.at[step]
        net.arrived(piece, sems, slot + step)
        total = piece[...].astype(f32) + part[net.ring(offset), rows].astype(f32)
        buf[step] = total.astype(bf16)
        net.send(piece, buf.at[step + 1], sems, slot + step + 1, target)

    begin(right_low, low, RING_A, 4, net.right)
    begin(left_high, high, RING_D, -4, net.left)
    begin(right_high, high, RING_B, 3, net.right)
    begin(left_low, low, RING_C, -3, net.left)
    for step in range(3):
        hand_on(right_low, low, RING_A, step, 3 - step, net.right)
        hand_on(left_high, high, RING_D, step, step - 3, net.left)
        if step < 2:
            hand_on(right_high, high, RING_B, step, 2 - step, net.right)
            hand_on(left_low, low, RING_C, step, step - 2, net.left)

    def close(rows, from_left, from_right):
        total = part[net.z, rows].astype(f32) + from_left.astype(f32) + from_right.astype(f32)
        layer_out = (middle[rows] + total).astype(bf16)
        return jnp.where(accept[rows] == 1, fresh[rows], layer_out)

    net.arrived(left_low.at[2], sems, RING_C + 2)
    net.arrived(right_low.at[3], sems, RING_A + 3)
    result = close(low, right_low[3], left_low[2])
    if last:
        out[net.x, net.z, low] = result
        gather_begin_low(net, out, gather_sems, half)
    else:
        out[net.z, low] = result
        ring_begin(net, out, gather_sems, half, False)
    net.arrived(right_high.at[2], sems, RING_B + 2)
    net.arrived(left_high.at[3], sems, RING_D + 3)
    result = close(high, right_high[2], left_high[3])
    if last:
        out[net.x, net.z, high] = result
        gather_begin_high(net, out, gather_sems, half)
        gather_rest(net, out, gather_sems, half)
    else:
        out[net.z, high] = result
        ring_begin(net, out, gather_sems, half, True)
        ring_rest(net, out, gather_sems, half)
        swap_sems = tuple(sem_refs[4:6])
        rows_f32 = out[...].reshape(8 * 2 * half, out.shape[2]).astype(f32)
        stage[...] = project(rows_f32, w_pair[...])
        net.send(stage, qkv.at[net.x], swap_sems, 0, net.pair)
        qkv[net.x] = project(rows_f32, w_own[...])
        net.arrived(qkv.at[1 - net.x], swap_sems, 0)
    net.finish()


def reduce_blk(part, middle, fresh, accept, w_pair, collective_id):
    blocks, rows, width = part.shape
    bf16 = jnp.bfloat16
    last = w_pair is None
    block = (rows // 2, width)
    rings = [pltpu.VMEM((count,) + block, bf16) for count in (4, 3, 3, 4)]
    operands = (part, middle, fresh, accept)
    if last:
        shapes = (jax.ShapeDtypeStruct((2,) + part.shape, bf16),)
        sems = sem_pair(RING_SLOTS) + sem_pair(GATHER_SLOTS)
    else:
        operands = operands + w_pair
        columns = w_pair[0].shape[1]
        shapes = (
            jax.ShapeDtypeStruct(part.shape, bf16),
            jax.ShapeDtypeStruct((2, blocks * rows, columns), bf16),
        )
        rings = [pltpu.VMEM((blocks * rows, columns), bf16)] + rings
        sems = sem_pair(RING_SLOTS) + sem_pair(RING_SLOTS) + sem_pair(1)
    return pl.pallas_call(
        functools.partial(reduce_kernel, last=last),
        out_shape=shapes,
        in_specs=whole(len(operands)),
        out_specs=tuple(whole(len(shapes))),
        scratch_shapes=rings + sems,
        compiler_params=pltpu.CompilerParams(
            collective_id=collective_id, has_side_effects=True, vmem_limit_bytes=40 << 20
        ),
        name=f"reduce_blk_{collective_id}",
    )(*operands)


R_A, R_B, R_O, L_A, L_B, L_O, X_A, X_B = 0, 4, 8, 12, 16, 20, 24, 25
GATHER_SLOTS = 33


def gather_begin_low(net, out, sems, half):
    low = out.at[net.x, net.z, 0:half]
    net.send(low, low, sems, R_A + 0, net.right)
    net.send(low, low, sems, L_A + 0, net.left)
    net.send(low, low, sems, X_A, net.pair)


def gather_begin_high(net, out, sems, half):
    high = out.at[net.x, net.z, half : 2 * half]
    net.send(high, high, sems, R_B + 0, net.right)
    net.send(high, high, sems, L_B + 0, net.left)
    net.send(high, high, sems, X_B + 0, net.pair)


def gather_rest(net, out, sems, half):
    other = 1 - net.x
    peer_low = out.at[other, net.z, 0:half]
    net.arrived(peer_low, sems, X_A)
    net.send(peer_low, peer_low, sems, R_O + 0, net.right)
    net.send(peer_low, peer_low, sems, L_O + 0, net.left)
    for step in range(1, 5):
        before, after = net.ring(-step), net.ring(step)
        piece = out.at[net.x, before, 0:half]
        net.arrived(piece, sems, R_A + step - 1)
        if step < 4:
            net.send(piece, piece, sems, R_A + step, net.right)
        piece = out.at[net.x, after, half : 2 * half]
        net.arrived(piece, sems, L_B + step - 1)
        if step < 4:
            net.send(piece, piece, sems, L_B + step, net.left)
        net.send(piece, piece, sems, X_B + (step if step < 4 else 7), net.pair)
        piece = out.at[other, after, 0:half]
        net.arrived(piece, sems, L_O + step - 1)
        if step < 4:
            net.send(piece, piece, sems, L_O + step, net.left)
        if step < 4:
            piece = out.at[net.x, after, 0:half]
            net.arrived(piece, sems, L_A + step - 1)
            if step < 3:
                net.send(piece, piece, sems, L_A + step, net.left)
            piece = out.at[net.x, before, half : 2 * half]
            net.arrived(piece, sems, R_B + step - 1)
            if step < 3:
                net.send(piece, piece, sems, R_B + step, net.right)
            net.send(piece, piece, sems, X_B + 3 + step, net.pair)
            piece = out.at[other, before, 0:half]
            net.arrived(piece, sems, R_O + step - 1)
            if step < 3:
                net.send(piece, piece, sems, R_O + step, net.right)
    for slot, offset in ((0, 0), (1, 1), (2, 2), (3, 3), (7, 4), (4, -1), (5, -2), (6, -3)):
        net.arrived(out.at[other, net.ring(offset), half : 2 * half], sems, X_B + slot)


PIECES = (0, 2, 1, 3)


def start_kernel(
    own, w_own, sent, out, w_all, got, copy_sems, send_sems, recv_sems, send_w, recv_w, send_f, recv_f
):
    net = Net()
    me = lax.axis_index("req")
    y, x, core = me // 4, (me // 2) % 2, me % 2

    def device(step, other_x, other_core=False):
        return (
            lax.rem(y + 4 + step, 4) * 4
            + (1 - x if other_x else x) * 2
            + (1 - core if other_core else core)
        )

    up, down, side, twin = device(1, 0), device(-1, 0), device(0, 1), device(0, 0, True)
    barrier = pltpu.get_barrier_semaphore()
    for step in range(1, 16):
        other = lax.rem(me + step, 16)
        pl.semaphore_signal(barrier, inc=1, device_id={"req": other}, device_id_type=MESH)
    for other in (net.right, net.left, net.pair):
        pl.semaphore_signal(barrier, inc=1, device_id={"blk": other}, device_id_type=MESH)
    pl.semaphore_wait(barrier, 18)
    w_sems, f_sems = (send_w, recv_w), (send_f, recv_f)
    started = []

    def copy_of(src, dst, slot, other):
        return pltpu.make_async_remote_copy(
            src_ref=src,
            dst_ref=dst,
            send_sem=send_sems.at[slot],
            recv_sem=recv_sems.at[slot],
            device_id={"req": other},
            device_id_type=MESH,
        )

    def send(src, dst, slot, other):
        copy = copy_of(src, dst, slot, other)
        copy.start()
        started.append(copy)

    def arrived(dst, slot):
        copy_of(dst, dst, slot, twin).wait_recv()

    U0, D0, SIDE, U1, D1, UF0, UF1, DF0, DF1, TWIN = 0, 4, 8, 12, 16, 20, 22, 24, 26, 28
    places = {(0, 0): 0, (0, 1): 1, (-1, 0): 2, (1, 0): 3, (-1, 1): 4, (1, 1): 5, (2, 0): 6, (2, 1): 7}

    def share(step, other_x, g):
        piece = out.at[g, device(step, other_x)]
        send(piece, piece, TWIN + 4 * places[(step, other_x)] + g, twin)

    for g in PIECES:
        dst = out.at[g, me]
        send(own.at[g], dst, U0 + g, up)
        send(own.at[g], dst, D0 + g, down)
        send(own.at[g], dst, SIDE + g, side)
    RO, LO, RQ, LQ, PX = 0, 4, 7, 10, 14
    w_mine, w_peer = w_all.at[net.z, net.x], w_all.at[net.z, 1 - net.x]
    net.send(w_own, w_mine, w_sems, PX, net.pair)
    net.send(w_own, w_mine, w_sems, RO, net.right)
    net.send(w_own, w_mine, w_sems, LO, net.left)
    for step in range(1, 16):
        other = lax.rem(me + step, 16)
        net.send(sent.at[other], got.at[me], f_sems, step - 1, other, "req")
    keeps = [
        pltpu.make_async_copy(own, out.at[:, me], copy_sems.at[0]),
        pltpu.make_async_copy(w_own, w_mine, copy_sems.at[1]),
        pltpu.make_async_copy(sent.at[me], got.at[me], copy_sems.at[2]),
    ]
    for keep in keeps:
        keep.start()

    def w_peer_begin():
        net.arrived(w_peer, w_sems, PX)
        net.send(w_peer, w_peer, w_sems, RQ, net.right)
        net.send(w_peer, w_peer, w_sems, LQ, net.left)

    def w_step(step, parity, slot_r, slot_l, last_r, last_l):
        if step < last_r:
            piece = w_all.at[net.ring(-1 - step), parity]
            net.arrived(piece, w_sems, slot_r + step)
            if step < last_r - 1:
                net.send(piece, piece, w_sems, slot_r + step + 1, net.right)
        if step < last_l:
            piece = w_all.at[net.ring(1 + step), parity]
            net.arrived(piece, w_sems, slot_l + step)
            if step < last_l - 1:
                net.send(piece, piece, w_sems, slot_l + step + 1, net.left)

    def w_mine_step(step):
        w_step(step, net.x, RO, LO, 4, 3)

    def w_peer_step(step):
        w_step(step, 1 - net.x, RQ, LQ, 3, 4)

    w_order = iter(
        [w_peer_begin, lambda: w_mine_step(0), lambda: w_peer_step(0), lambda: w_mine_step(1),
         lambda: w_peer_step(1), lambda: w_mine_step(2), lambda: w_peer_step(2)]
    )
    for g in PIECES:
        send(own.at[g], out.at[g, me], TWIN + g, twin)

    def from_below(g, other_x, base, forward):
        piece = out.at[g, device(-1, other_x)]
        arrived(piece, base + g)
        if g < 2:
            send(piece, piece, forward + g, up)
        share(-1, other_x, g)

    def from_above(g, other_x, base, forward):
        piece = out.at[g, device(1, other_x)]
        arrived(piece, base + g)
        if g >= 2:
            send(piece, piece, forward + g - 2, down)
        share(1, other_x, g)

    def from_far(g, other_x):
        piece = out.at[g, device(2, other_x)]
        if g < 2:
            arrived(piece, (UF1 if other_x else UF0) + g)
        else:
            arrived(piece, (DF1 if other_x else DF0) + g - 2)
        share(2, other_x, g)

    for g in PIECES:
        piece = out.at[g, side]
        arrived(piece, SIDE + g)
        send(piece, piece, U1 + g, up)
        send(piece, piece, D1 + g, down)
        share(0, 1, g)
        from_below(g, 0, U0, UF0)
        from_above(g, 0, D0, DF0)
        next(w_order)()
    for g in PIECES:
        from_far(g, 0)
        from_below(g, 1, U1, UF1)
        from_above(g, 1, D1, DF1)
        next(w_order, lambda: None)()
    for g in PIECES:
        from_far(g, 1)
    for (step, other_x), place in places.items():
        for g in PIECES:
            arrived(out.at[g, device(step, other_x, True)], TWIN + 4 * place + g)
    w_mine_step(3)
    w_peer_step(3)
    for step in range(1, 16):
        net.arrived(got.at[lax.rem(me + 16 - step, 16)], f_sems, step - 1)
    for keep in keeps:
        keep.wait()
    for copy in started:
        copy.wait_send()
    net.finish()


def start_gathers(own, w_own, sent, collective_id):
    groups = own.shape[0]
    anywhere = pl.BlockSpec(memory_space=pl.ANY)
    return pl.pallas_call(
        start_kernel,
        out_shape=(
            jax.ShapeDtypeStruct((groups, 16) + own.shape[1:], own.dtype),
            jax.ShapeDtypeStruct((8, 2) + w_own.shape, w_own.dtype),
            jax.ShapeDtypeStruct(sent.shape, sent.dtype),
        ),
        in_specs=[anywhere] * 3,
        out_specs=(anywhere,) * 3,
        scratch_shapes=[pltpu.SemaphoreType.DMA((3,))] + sem_pair(60) + sem_pair(15) + sem_pair(15),
        compiler_params=pltpu.CompilerParams(
            collective_id=collective_id, has_side_effects=True, vmem_limit_bytes=4 << 20
        ),
        name="start_gathers",
    )(own, w_own, sent)


SLOTS = 128


class Fresh:
    def __init__(self, embed_table, new_ids, req_index):
        self.table, self.req_index = embed_table, req_index
        passes = new_ids.shape[0]
        by_device = new_ids.reshape(passes, 16, 2, 8, -1)
        self.ids = jnp.transpose(by_device, (1, 3, 2, 0, 4)).reshape(16, -1)
        count = self.ids.shape[1]
        places = jnp.arange(count)
        self.earlier = (places[:, None] < places[None, :]).astype(jnp.bfloat16)

    def ranks(self, inside):
        got = jnp.dot(inside.astype(jnp.bfloat16), self.earlier, preferred_element_type=jnp.float32)
        return got.astype(jnp.int32)

    def sent(self):
        vocab_dev = self.table.shape[0]
        relative = self.ids - self.req_index * vocab_dev
        inside = (relative >= 0) & (relative < vocab_dev)
        rank = jnp.where(inside, self.ranks(inside), -1)
        chosen = rank[:, None, :] == jnp.arange(SLOTS)[None, :, None]
        wanted = jnp.sum(jnp.where(chosen, relative[:, None, :], 0), -1)
        rows = jnp.take(self.table, wanted, axis=0)
        return jnp.pad(rows, ((0, 0), (0, 0), (0, 128 - rows.shape[2])))

    def picked(self, got):
        vocab_dev, columns = self.table.shape
        mine = lax.dynamic_index_in_dim(self.ids, self.req_index, 0, keepdims=True)
        owners = jnp.arange(16)[:, None]
        theirs = mine - owners * vocab_dev
        inside = (theirs >= 0) & (theirs < vocab_dev)
        place = jnp.sum(jnp.where(inside, owners * SLOTS + self.ranks(inside), 0), 0)
        quick = jnp.take(got.reshape(16 * SLOTS, -1), jnp.minimum(place, 16 * SLOTS - 1), axis=0)

        owner = self.ids // vocab_dev
        asked = jnp.sum((owner[:, None, :] == owners[None]).astype(jnp.int32), -1)
        crowded = jnp.max(asked) > SLOTS

        def dense():
            relative = (self.ids - self.req_index * vocab_dev).reshape(-1)
            here = (relative >= 0) & (relative < vocab_dev)
            looked = jnp.take(self.table, jnp.clip(relative, 0, vocab_dev - 1), axis=0)
            looked = jnp.where(here[:, None], looked, jnp.zeros((), jnp.bfloat16))
            summed = lax.psum_scatter(looked, "req", scatter_dimension=0, tiled=True)
            return jnp.pad(summed, ((0, 0), (0, 128 - columns)))

        chosen = lax.cond(crowded, dense, lambda: quick)
        return chosen.reshape(16, -1, chosen.shape[1])


def attend_kernel(groups, lengths, rows_or_qkv, *refs, span, first):
    if first:
        weights, cache, out = refs
        qkv = project(rows_or_qkv[0].astype(jnp.float32), weights[...])
    else:
        cache, out = refs
        qkv = rows_or_qkv[0]
    length = lengths[pl.program_id(0)]
    q, own_block = qkv[:, 0:128], qkv[:, 128:256]
    f32 = jnp.float32

    def scores_of(keys):
        return lax.dot_general(q, keys, (((1,), (1,)), ((), ())), preferred_element_type=f32)

    def weigh(weights, values):
        return jnp.dot(weights.astype(jnp.bfloat16), values, preferred_element_type=f32)

    scores = scores_of(own_block)
    top = jnp.max(scores, -1, keepdims=True)
    weights = jnp.exp(scores - top)
    total = jnp.sum(weights, -1, keepdims=True)
    mixed = weigh(weights, own_block)

    def visit(index, carried):
        top, total, mixed = carried
        start = pl.multiple_of(index * span, span)
        block = cache[0, pl.ds(start, span), :]
        position = start + lax.broadcasted_iota(jnp.int32, (1, span), 1)
        bias = jnp.where(position < length, 0.0, NEG).astype(f32)
        scores = scores_of(block) + bias
        raised = jnp.maximum(top, jnp.max(scores, -1, keepdims=True))
        shrink = jnp.exp(top - raised)
        weights = jnp.exp(scores - raised)
        total = total * shrink + jnp.sum(weights, -1, keepdims=True)
        return raised, total, mixed * shrink + weigh(weights, block)

    blocks = (length + span - 1) // span
    top, total, mixed = lax.fori_loop(0, blocks, visit, (top, total, mixed))
    head = mixed / total
    parity = lax.axis_index("blk") % 2
    lane = lax.broadcasted_iota(jnp.int32, (1, 128), 1)
    moved = jnp.where(parity == 0, pltpu.roll(head, 64, 1), head)
    out[0] = jnp.where(lane // 64 == parity, moved, 0.0).astype(out.dtype)


def attend(rows_or_qkv, weights, cache, groups, lengths):
    requests, rows, width = rows_or_qkv.shape
    size = cache.shape[1]
    first = weights is not None
    in_specs = [pl.BlockSpec((1, rows, width), lambda r, g, n: (r, 0, 0))]
    operands = (rows_or_qkv,)
    if first:
        in_specs.append(pl.BlockSpec(weights.shape, lambda r, g, n: (0, 0)))
        operands = operands + (weights,)
    in_specs.append(pl.BlockSpec((1, size, 128), lambda r, g, n: (g[r], 0, 0)))
    return pl.pallas_call(
        functools.partial(attend_kernel, span=1024, first=first),
        out_shape=jax.ShapeDtypeStruct((requests, rows, 128), jnp.bfloat16),
        grid_spec=pltpu.PrefetchScalarGridSpec(
            num_scalar_prefetch=2,
            grid=(requests,),
            in_specs=in_specs,
            out_specs=pl.BlockSpec((1, rows, 128), lambda r, g, n: (r, 0, 0)),
        ),
        compiler_params=pltpu.CompilerParams(vmem_limit_bytes=40 << 20),
        name="attend",
    )(groups, lengths, *operands, cache)


def shards(
    tokens, cache_kv, w_qkv, w_out, w_fc, w_proj, embed_table, group_ids, cache_len, accept, new_ids
):
    req_index = lax.axis_index("req")
    blk_index = lax.axis_index("blk")
    z, x, core = blk_index // 2, blk_index % 2, req_index % 2
    requests, rows, width = tokens.shape
    kv_width = cache_kv.shape[3]
    head_dim = kv_width // 2
    share = rows // 8
    my_groups = lax.dynamic_slice_in_dim(group_ids, req_index * requests, requests)
    lengths = jnp.take(cache_len, my_groups)
    pairs = [(index, index ^ 1) for index in range(16)]
    hidden = w_fc.shape[1] // 2
    w_fc_half = lax.dynamic_slice_in_dim(w_fc, core * hidden, hidden, 1)
    w_proj_half = lax.dynamic_slice_in_dim(w_proj, core * hidden, hidden, 0)
    w_fc_b, w_proj_b = (lax.ppermute(half, "blk", pairs) for half in (w_fc_half, w_proj_half))
    w_fc_c, w_proj_c = (lax.ppermute(half, "req", pairs) for half in (w_fc_b, w_proj_b))
    w_qkv = w_qkv[:, 0, :]
    w_own = jnp.concatenate(
        [w_qkv[:, :head_dim], jnp.zeros_like(w_qkv[:, :head_dim]), w_qkv[:, head_dim:]], 1
    )
    w_other = lax.ppermute(w_own, "blk", pairs)

    asked = Fresh(embed_table, new_ids, req_index)
    every_cache, w_out_all, got = start_gathers(cache_kv[:, :, 0, :], w_out[0], asked.sent(), 1)
    every_cache = every_cache.reshape(cache_kv.shape[0], -1, kv_width)
    w_out_all = w_out_all.reshape(16 * head_dim, width)
    my_accept = lax.dynamic_index_in_dim(accept, x, 1, keepdims=False)
    my_accept = lax.dynamic_slice_in_dim(my_accept, z * share, share, 1)[..., None]
    weights = (w_out_all, w_fc, w_proj, w_fc_b, w_proj_b, w_fc_c, w_proj_c)

    heads = attend(tokens, w_own, every_cache, my_groups, lengths)
    every_head, mine = gather_heads(heads, asked.picked(got), 2)
    columns = embed_table.shape[1]
    mine = jnp.transpose(mine[:, :, :columns], (1, 0, 2)).reshape(PASSES, share, width)
    current = lax.dynamic_index_in_dim(tokens, x, 0, keepdims=False)
    for pass_index in range(PASSES):
        last = pass_index == PASSES - 1
        grown, my_middle = mlp(every_head, current, weights)
        done = reduce_blk(
            grown.reshape(8, share, width),
            my_middle,
            mine[pass_index],
            my_accept[pass_index],
            None if last else (w_own, w_other),
            3 + 2 * pass_index,
        )
        if last:
            return done[0].reshape(requests, rows, width)
        current = done[0].reshape(rows, width)
        heads = attend(done[1], None, every_cache, my_groups, lengths)
        (every_head,) = gather_heads(heads, None, 4 + 2 * pass_index)


def solution(mesh):
    return jax.shard_map(
        shards,
        mesh=mesh,
        in_specs=(
            P("req", None, None),
            P(None, "req", "blk", None),
            P(None, "blk", None),
            P("blk", None, None),
            P(None, "blk"),
            P("blk", None),
            P("req", "blk"),
            P(),
            P(),
            P(None, "req", None),
            P(),
        ),
        out_specs=P("req", None, None),
        check_vma=False,
    )
```

time: 971 us -> 307 us (0.32)
  waiting for transfers between devices: 744 us -> 11.5 us
  Pallas kernels: 0 us -> 210 us
  matrix products: 72.2 us -> 1.34 us
  local copies, waits for them, and re-layouts: 103 us -> 56.8 us
  other arithmetic: 33.7 us -> 4.89 us
    psum x4 -> x0, waiting for transfers between devices: 578 us -> none  [the longest x2 297 us: shards(): lax.psum(partial_terms.astype(jnp.bfloat16), 'blk').astype(jnp.float32)]
    pallas_call x0 -> x9, Pallas kernels: none -> 210 us  [the longest x2 72.4 us: reduce_blk(): pl.pallas_call(functools.partial(reduce_kernel, last=last), out_shape=sha...]
    unnamed x8 -> x0, waiting for transfers between devices: 88.3 us -> none
    all_gather x2 -> x0, waiting for transfers between devices: 77.3 us -> none  [the longest x1 77 us: shards(): fresh_rows = lax.all_gather(picked, 'blk', axis=3, tiled=True)]
    dot_general x42 -> x2, matrix products: 72.2 us -> 1.34 us  [ranks(): jnp.dot(inside.astype(jnp.bfloat16), self.earlier, preferred_element_type...]
    gather x5 -> x2, local copies, waits for them, and re-layouts: 79.5 us -> 10.2 us  [the longest x1 6.17 us: sent(): rows = jnp.take(self.table, wanted, axis=0)]
    reduce_sum x26 -> x3, other arithmetic: 20.1 us -> 1.53 us  [the longest x1 1.08 us: sent(): wanted = jnp.sum(jnp.where(chosen, relative[:, None, :], 0), -1)]
    unnamed x32 -> x54, local copies, waits for them, and re-layouts: 5.13 us -> 21.6 us
  transfers between devices with their start and end apart: 7 -> 5, of which waited for: 7 -> 1; matrix products, arithmetic and copies ran while one was open for 16% -> 15% of each run, Pallas kernels for 0% -> 34%
where the time goes in v3:
time: 307 us; the launch traced here: 303 us
  Pallas kernels  210 us (68%)
  local copies, waits for them, and re-layouts  56.8 us (19%)
  between operations  14.4 us (5%)
  waiting for transfers between devices  11.5 us (4%)
  other arithmetic  4.89 us (2%)
  starting transfers between devices  3.31 us (1%)
    pallas_call x2, Pallas kernels, reduce_blk(): pl.pallas_call(functools.partial(reduce_kernel, last=last), out_shape=sha...  72.4 us
    pallas_call x1, Pallas kernels, start_gathers(): pl.pallas_call(start_kernel, out_shape=(jax.ShapeDtypeStruct((groups, 16)...  58.2 us
    pallas_call x2, Pallas kernels, gather_heads(): pl.pallas_call(functools.partial(heads_kernel, with_fresh=with_fresh), ou...  40.3 us
    pallas_call x2, Pallas kernels, attend(): pl.pallas_call(functools.partial(attend_kernel, span=1024, first=first),...  28.9 us
    unnamed x54, local copies, waits for them, and re-layouts  21.6 us
    ppermute x2, waiting for transfers between devices, shards(): lax.ppermute(half, 'blk', pairs)  11.5 us
    pallas_call x2, Pallas kernels, mlp(): pl.pallas_call(mlp_kernel, out_shape=(jax.ShapeDtypeStruct((rows, width),...  10.5 us
    gather x1, local copies, waits for them, and re-layouts, sent(): rows = jnp.take(self.table, wanted, axis=0)  6.17 us
  transfers between devices with their start and end apart: 5, of which 1 were waited for; matrix products, arithmetic and copies ran while one was open for 15% of the time, Pallas kernels for 34%

profile of v3, /device:TPU:12, one launch (start us, length us, event | category | flops | bytes accessed | tf_op | source)
XLA Modules:
  0.0 302.8 jit_solution(17938746879484209609)
XLA Ops:
  6.5 2.0 constant_dynamic-slice_fusion.1
  9.8 2.0 constant_dynamic-slice_fusion
  21.0 6.2 %gather_fusion.3 = bf16[2048,100]{1,0:T(8,128)(2,1)S(1)} fusion(bf16[3141,100]{1,0:T(8,128)(2,1)S(1)} %copy.59, s32[2048]{0:T(1024)S(1)} %fusion.14), kind=kCustom, calls=%fused_computation.3 | custom fusion | bytes 827392 | tf_op jit(solution)/shard_map/jit(_take)/gather | solution.py:569
  29.5 11.5 %collective-permute-done.1.w_proj_b = bf16[200,1600]{1,0:T(8,128)(2,1)} collective-permute-done((bf16[200,1600]{1,0:T(8,128)(2,1)}, bf16[200,1600]{1,0:T(8,128)(2,1)}, u32[]{:S(2)}, u32[]{:S(2)}) %collective-permute-start.1) | collective-permute-done | bytes 640032 | tf_op jit(solution)/shard_map/ppermute | solution.py:682
  41.3 2.7 copy.60.rows_or_qkv
  44.1 2.7 copy.63.w_fc
  46.8 2.0 pad.8.sent
  50.1 2.2 copy.62
  55.3 58.2 %start_gathers.1 = (bf16[4,16,512,128]{3,2,1,0:T(8,128)(2,1)S(1)}, bf16[8,2,64,1600]{3,2,1,0:T(8,128)(2,1)S(1)}, bf16[16,128,128]{2,1,0:T(8,128)(2,1)}) custom-call(bf16[4,512,128]{2,1,0:T(8,128)(2,1)S(1)} %bitcast.51, bf16[64,1600]{1,0:T(8,128)(2,1)S(1)} %bitcast.52, bf16[16,128,128]{2,1,0:T(8,128)(2,1)S(1)} %copy-done.12), custom_call_target="tpu_custom_call" | custom-call | tf_op jit(solution)/shard_map/start_gathers/pallas_call | solution.py:528
  115.2 16.2 %attend.2.heads = bf16[2,256,128]{2,1,0:T(8,128)(2,1)S(1)} custom-call(s32[2]{0:T(128)S(1)} %get-tuple-element.115.groups, s32[2]{0:T(128)S(1)} %and_select_fusion.lengths, bf16[2,256,1600]{2,1,0:T(8,128)(2,1)S(1)} %copy.60.rows_or_qkv, bf16[1600,256]{1,0:T(8,128)(2,1)} %pad_maximum_fusion.refs_0_, bf16[4,8192,128]{2,1,0:T(8,128)(2,1)S(1)} %bitcast.42), custom_call_target="tpu_custom_call" | custom-call | tf_op jit(solution)/shard_map/attend/pallas_call | solution.py:652
  131.4 4.6 %conditional.1 = (bf16[16,64,128]{2,1,0:T(8,128)(2,1)S(1)}) conditional(s32[]{:T(128)} %convert_element_type.21, (s32[16]{0:T(128)S(1)}, s32[16,1024]{1,0:T(8,128)S(1)}, pred[16,1024]{1,0:T(8,128)(4,1)S(1)}, s32[16,1024]{1,0:T(8,128)S(1)}, bf16[16,128,128]{2,1,0:T(8,128)(2,1)}) %tuple.36, (s32[]{:T(128)}, s32[16,1024]{1,0:T(8,128)}, ...), branch_computations={%region_3.5_spmd, %region_5.7_spmd} | conditional | flops 3538945 | bytes 27266070 | solution.py:593
  131.6 4.0 %gather_fusion = bf16[1024,128]{1,0:T(8,128)(2,1)S(1)} fusion(bf16[2048,128]{1,0:T(8,128)(2,1)} %bitcast, s32[1024]{0:T(1024)S(1)} %fusion), kind=kCustom, calls=%fused_computation | custom fusion | bytes 528384 | tf_op jit(solution)/shard_map/jit(_take)/gather | solution.py:579
  136.1 22.8 %gather_heads_2.1 = (bf16[8,256,128]{2,1,0:T(8,128)(2,1)S(1)}, bf16[16,64,128]{2,1,0:T(8,128)(2,1)S(1)}) custom-call(bf16[2,256,128]{2,1,0:T(8,128)(2,1)S(1)} %attend.2.heads, bf16[16,64,128]{2,1,0:T(8,128)(2,1)S(1)} %get-tuple-element.124.refs_0_), custom_call_target="tpu_custom_call" | custom-call | tf_op jit(solution)/shard_map/gather_heads_2/pallas_call | solution.py:146
  167.1 2.3 copy.64.w_fc_b
  169.5 2.3 copy.65.w_fc_c
  171.8 2.0 copy-done.4
  177.2 5.2 %mlp.2 = (bf16[256,1600]{1,0:T(8,128)(2,1)S(1)}, f32[32,1600]{1,0:T(8,128)S(1)}) custom-call(bf16[8,256,128]{2,1,0:T(8,128)(2,1)S(1)} %copy-done.14, bf16[256,1600]{1,0:T(8,128)(2,1)S(1)} %bitcast.47, bf16[1024,1600]{1,0:T(8,128)(2,1)S(1)} %bitcast.44, bf16[1600,400]{1,0:T(8,128)(2,1)S(1)} %copy.63.w_fc, bf16[400,1600]{1,0:T(8,128)(2,1)S(1)} %copy-done.6, ...), custom_call_target="tpu_custom_call" | custom-call | tf_op jit(solution)/shard_map/mlp/pallas_call | solution.py:187
  182.4 37.6 %reduce_blk_3.1 = (bf16[8,32,1600]{2,1,0:T(8,128)(2,1)S(1)}, bf16[2,256,256]{2,1,0:T(8,128)(2,1)S(1)}) custom-call(bf16[8,32,1600]{2,1,0:T(8,128)(2,1)S(1)} %bitcast.49, f32[32,1600]{1,0:T(8,128)S(1)} %get-tuple-element.96.middle, bf16[32,1600]{1,0:T(8,128)(2,1)S(1)} %copy-done.16, s32[32,1]{1,0:T(8,128)S(1)} %copy.67.accept, ...), custom_call_target="tpu_custom_call" | custom-call | tf_op jit(solution)/shard_map/reduce_blk_3/pallas_call | solution.py:299
  220.0 3.4 %copy-done.2 = bf16[4,16,512,128]{3,2,1,0:T(8,128)(2,1)S(1)} copy-done((bf16[4,16,512,128]{3,2,1,0:T(8,128)(2,1)S(1)}, bf16[4,16,512,128]{3,2,1,0:T(8,128)(2,1)}, u32[]{:S(2)}) %copy-start.2) | copy-done | bytes 8388632
  223.4 12.8 %attend.3.heads = bf16[2,256,128]{2,1,0:T(8,128)(2,1)S(1)} custom-call(s32[2]{0:T(128)S(1)} %get-tuple-element.115.groups, s32[2]{0:T(128)S(1)} %and_select_fusion.lengths, bf16[2,256,256]{2,1,0:T(8,128)(2,1)S(1)} %get-tuple-element.98.rows_or_qkv, bf16[4,8192,128]{2,1,0:T(8,128)(2,1)S(1)} %bitcast.43), custom_call_target="tpu_custom_call" | custom-call | tf_op jit(solution)/shard_map/attend/pallas_call | solution.py:652
  236.1 17.5 %gather_heads_4.1.every_head = bf16[8,256,128]{2,1,0:T(8,128)(2,1)S(1)} custom-call(bf16[2,256,128]{2,1,0:T(8,128)(2,1)S(1)} %attend.3.heads), custom_call_target="tpu_custom_call" | custom-call | tf_op jit(solution)/shard_map/gather_heads_4/pallas_call | solution.py:146
  253.7 5.3 %mlp.3 = (bf16[256,1600]{1,0:T(8,128)(2,1)S(1)}, f32[32,1600]{1,0:T(8,128)S(1)}) custom-call(bf16[8,256,128]{2,1,0:T(8,128)(2,1)S(1)} %gather_heads_4.1.every_head, bf16[256,1600]{1,0:T(8,128)(2,1)S(1)} %bitcast.48, bf16[1024,1600]{1,0:T(8,128)(2,1)S(1)} %bitcast.45, bf16[1600,400]{1,0:T(8,128)(2,1)S(1)} %copy.63.w_fc, bf16[400,1600]{1,0:T(8,128)(2,1)S(1)} %copy-done.6, ...), custom_call_target="tpu_custom_call" | custom-call | tf_op jit(solution)/shard_map/mlp/pallas_call | solution.py:187
  258.9 34.8 %reduce_blk_5.1 = bf16[2,8,32,1600]{3,2,1,0:T(8,128)(2,1)S(1)} custom-call(bf16[8,32,1600]{2,1,0:T(8,128)(2,1)S(1)} %bitcast.50, f32[32,1600]{1,0:T(8,128)S(1)} %get-tuple-element.101.middle, bf16[32,1600]{1,0:T(8,128)(2,1)S(1)} %copy-done.17, s32[32,1]{1,0:T(8,128)S(1)} %copy.72.accept), custom_call_target="tpu_custom_call" | custom-call | tf_op jit(solution)/shard_map/reduce_blk_5/pallas_call | solution.py:299
  293.7 2.2 copy.73
  (101 shorter events, 30.4 us)
Async XLA Ops:
  6.5 13.8 %copy-start = (s32[4]{0:T(128)S(1)}, s32[4]{0:T(128)}, u32[]{:S(2)}) copy-start(s32[4]{0:T(128)} %param.21) | copy-start | bytes 52
  6.5 10.0 %copy-start.22 = (s32[2,32,256]{2,1,0:T(8,128)S(1)}, s32[2,32,256]{2,1,0:T(8,128)}, u32[]{:S(2)}) copy-start(s32[2,32,256]{2,1,0:T(8,128)} %param.23) | copy-start | bytes 196612
  8.6 9.8 %copy-start.24 = (s32[32]{0:T(128)S(1)}, s32[32]{0:T(128)}, u32[]{:S(2)}) copy-start(s32[32]{0:T(128)} %param.20) | copy-start | bytes 388
  8.6 20.8 %collective-permute-start = (bf16[1600,200]{0,1:T(8,128)(2,1)}, bf16[1600,200]{0,1:T(8,128)(2,1)}, u32[]{:S(2)}, u32[]{:S(2)}) collective-permute-start(bf16[1600,200]{0,1:T(8,128)(2,1)} %constant_dynamic-slice_fusion.1), channel_id=1, source_target_pairs={{0,1},{1,0},{2,3},{3,2},{4,5},{5,4},{6,7},{7,6},{8,9},{9,8},{10,11... | collective-permute-start | bytes 1920008 | tf_op jit(solution)/shard_map/ppermute | solution.py:682
  11.7 8.2 %copy-start.20 = (bf16[3141,100]{0,1:T(8,128)(2,1)S(1)}, bf16[3141,100]{0,1:T(8,128)(2,1)}, u32[]{:S(2)}) copy-start(bf16[3141,100]{0,1:T(8,128)(2,1)} %param.19) | copy-start | bytes 1884604
  11.7 29.2 %collective-permute-start.1 = (bf16[200,1600]{1,0:T(8,128)(2,1)}, bf16[200,1600]{1,0:T(8,128)(2,1)}, u32[]{:S(2)}, u32[]{:S(2)}) collective-permute-start(bf16[200,1600]{1,0:T(8,128)(2,1)} %constant_dynamic-slice_fusion), channel_id=1, source_target_pairs={{0,1},{1,0},{2,3},{3,2},{4,5},{5,4},{6,7},{7,6},{8,9},{9,8},{10,11... | collective-permute-start | bytes 1920008 | tf_op jit(solution)/shard_map/ppermute | solution.py:682
  15.3 167.0 %collective-permute-start.4 = (bf16[1600,256]{1,0:T(8,128)(2,1)}, bf16[1600,256]{1,0:T(8,128)(2,1)}, u32[]{:S(2)}, u32[]{:S(2)}) collective-permute-start(bf16[1600,256]{1,0:T(8,128)(2,1)} %pad_maximum_fusion.refs_0_), channel_id=1, source_target_pairs={{0,1},{1,0},{2,3},{3,2},{4,5},{5,4},{6,7},{7,6},{8,9},{9,8},{10,11... | collective-permute-start | bytes 2457608 | tf_op jit(solution)/shard_map/ppermute | solution.py:688
  17.2 10.0 %copy-start.21 = (s32[16,1024]{1,0:T(8,128)}, s32[16,1024]{1,0:T(8,128)S(1)}, u32[]{:S(2)}) copy-start(s32[16,1024]{1,0:T(8,128)S(1)} %reshape.165) | copy-start | bytes 196612
  18.2 9.0 %copy-start.19 = (bf16[2,256,1600]{1,2,0:T(8,128)(2,1)S(1)}, bf16[2,256,1600]{1,2,0:T(8,128)(2,1)}, u32[]{:S(2)}) copy-start(bf16[2,256,1600]{1,2,0:T(8,128)(2,1)} %param.13) | copy-start | bytes 4915204
  29.4 140.1 %collective-permute-start.2 = (bf16[1600,200]{0,1:T(8,128)(2,1)}, bf16[1600,200]{0,1:T(8,128)(2,1)}, u32[]{:S(2)}, u32[]{:S(2)}) collective-permute-start(bf16[1600,200]{0,1:T(8,128)(2,1)} %collective-permute-done), channel_id=1, source_target_pairs={{0,16},{16,0},{32,48},{48,32},{64,80},{80,64},{96,112},{112,96},{1... | collective-permute-start | bytes 1920008 | tf_op jit(solution)/shard_map/ppermute | solution.py:683
  41.0 130.8 %collective-permute-start.3 = (bf16[200,1600]{1,0:T(8,128)(2,1)}, bf16[200,1600]{1,0:T(8,128)(2,1)}, u32[]{:S(2)}, u32[]{:S(2)}) collective-permute-start(bf16[200,1600]{1,0:T(8,128)(2,1)} %collective-permute-done.1.w_proj_b), channel_id=1, source_target_pairs={{0,16},{16,0},{32,48},{48,32},{64,80},{80,64},{96,112},{112,96},{1... | collective-permute-start | bytes 1920008 | tf_op jit(solution)/shard_map/ppermute | solution.py:683
  113.5 1.7 copy-start.3
  115.2 16.2 %copy-start.1 = (bf16[4,16,512,128]{3,2,1,0:T(8,128)(2,1)}, bf16[4,16,512,128]{3,2,1,0:T(8,128)(2,1)S(1)}, u32[]{:S(2)}) copy-start(bf16[4,16,512,128]{3,2,1,0:T(8,128)(2,1)S(1)} %get-tuple-element.91) | copy-start | bytes 25165828
  115.2 16.2 %copy-start.23 = (s32[16,1024]{1,0:T(8,128)S(1)}, s32[16,1024]{1,0:T(8,128)}, u32[]{:S(2)}) copy-start(s32[16,1024]{1,0:T(8,128)} %fusion.5) | copy-start | bytes 196612
  136.0 35.7 %copy-start.6 = (bf16[400,1600]{1,0:T(8,128)(2,1)S(1)}, bf16[400,1600]{1,0:T(8,128)(2,1)}, u32[]{:S(2)}) copy-start(bf16[400,1600]{1,0:T(8,128)(2,1)} %w_proj.3) | copy-start | bytes 3840004
  159.7 12.1 %copy-start.14 = (bf16[8,256,128]{2,1,0:T(8,128)(2,1)S(1)}, bf16[8,256,128]{2,1,0:T(8,128)(2,1)}, u32[]{:S(2)}) copy-start(bf16[8,256,128]{2,1,0:T(8,128)(2,1)} %copy-done.13) | copy-start | bytes 1572868
  171.7 2.0 copy-start.4
  176.0 1.2 copy-start.11
  177.2 5.2 %copy-start.16 = (bf16[32,1600]{1,0:T(8,128)(2,1)S(1)}, bf16[32,1600]{1,0:T(8,128)(2,1)}, u32[]{:S(2)}) copy-start(bf16[32,1600]{1,0:T(8,128)(2,1)} %squeeze.31.fresh) | copy-start | bytes 307204
  220.0 3.4 %copy-start.2 = (bf16[4,16,512,128]{3,2,1,0:T(8,128)(2,1)S(1)}, bf16[4,16,512,128]{3,2,1,0:T(8,128)(2,1)}, u32[]{:S(2)}) copy-start(bf16[4,16,512,128]{3,2,1,0:T(8,128)(2,1)} %copy-done.1) | copy-start | bytes 25165828
  223.4 30.3 %copy-start.5 = (bf16[8,2,64,1600]{3,2,1,0:T(8,128)(2,1)S(1)}, bf16[8,2,64,1600]{3,2,1,0:T(8,128)(2,1)}, u32[]{:S(2)}) copy-start(bf16[8,2,64,1600]{3,2,1,0:T(8,128)(2,1)} %copy-done.3) | copy-start | bytes 9830404
  223.4 30.3 %copy-start.8 = (bf16[1600,200]{1,0:T(8,128)(2,1)S(1)}, bf16[1600,200]{1,0:T(8,128)(2,1)}, u32[]{:S(2)}) copy-start(bf16[1600,200]{1,0:T(8,128)(2,1)} %copy.64.w_fc_b) | copy-start | bytes 1920004
  223.4 30.3 %copy-start.10 = (bf16[1600,200]{1,0:T(8,128)(2,1)S(1)}, bf16[1600,200]{1,0:T(8,128)(2,1)}, u32[]{:S(2)}) copy-start(bf16[1600,200]{1,0:T(8,128)(2,1)} %copy.65.w_fc_c) | copy-start | bytes 1920004
  253.6 5.3 %copy-start.17 = (bf16[32,1600]{1,0:T(8,128)(2,1)S(1)}, bf16[32,1600]{1,0:T(8,128)(2,1)}, u32[]{:S(2)}) copy-start(bf16[32,1600]{1,0:T(8,128)(2,1)} %squeeze.33.fresh) | copy-start | bytes 307204
  (6 other events, 6.1 us)

commit v4 on v3

--- a/solution.py
+++ b/solution.py
@@ -95,95 +95,64 @@
             take(step, False, RING_C + step - 1, step == 3, net.left)
 
 
-def heads_kernel(heads, *refs, with_fresh):
-    if with_fresh:
-        picked, out, mine, peer, copy_sem, *sem_refs = refs
-    else:
-        out, peer, *sem_refs = refs
+def heads_kernel(heads, out, peer, *sem_refs):
     net = Net()
     ring_sems, pair_sems = tuple(sem_refs[0:2]), tuple(sem_refs[2:4])
     half = heads.shape[1] // 2
-    if with_fresh:
-        net.greet(others=[lax.rem(net.blk + step, 16) for step in range(1, 16)])
-    else:
-        net.greet()
+    net.greet()
     parts = (slice(0, half), slice(half, 2 * half))
     for part, rows in enumerate(parts):
         net.send(heads.at[1 - net.x, rows], peer.at[rows], pair_sems, part, net.pair)
-    if with_fresh:
-        fresh_sems = tuple(sem_refs[4:6])
-        keep = pltpu.make_async_copy(picked.at[net.blk], mine.at[net.blk], copy_sem)
-        keep.start()
     for part, rows in enumerate(parts):
         net.arrived(peer.at[rows], pair_sems, part)
         out[net.z, rows] = heads[net.x, rows] + peer[rows]
         ring_begin(net, out, ring_sems, half, part == 1)
-    if with_fresh:
-        for step in range(1, 16):
-            other = lax.rem(net.blk + step, 16)
-            net.send(picked.at[other], mine.at[net.blk], fresh_sems, step - 1, other)
     ring_rest(net, out, ring_sems, half)
-    if with_fresh:
-        for step in range(1, 16):
-            net.arrived(mine.at[lax.rem(net.blk + 16 - step, 16)], fresh_sems, step - 1)
-        keep.wait()
     net.finish()
 
 
-def gather_heads(heads, picked, collective_id):
+def gather_heads(heads, collective_id):
     _, rows, lanes = heads.shape
-    with_fresh = picked is not None
-    shape = jax.ShapeDtypeStruct((8, rows, lanes), heads.dtype)
-    scratch = [pltpu.VMEM((rows, lanes), heads.dtype)]
-    sems = sem_pair(RING_SLOTS) + sem_pair(2)
-    if with_fresh:
-        scratch = scratch + [pltpu.SemaphoreType.DMA]
-        sems = sems + sem_pair(15)
-        shapes = (shape, jax.ShapeDtypeStruct(picked.shape, picked.dtype))
-        operands = (heads, picked)
-    else:
-        shapes, operands = (shape,), (heads,)
     return pl.pallas_call(
-        functools.partial(heads_kernel, with_fresh=with_fresh),
-        out_shape=shapes,
-        in_specs=whole(len(operands)),
-        out_specs=tuple(whole(len(shapes))),
-        scratch_shapes=scratch + sems,
+        heads_kernel,
+        out_shape=jax.ShapeDtypeStruct((8, rows, lanes), heads.dtype),
+        in_specs=whole(1),
+        out_specs=whole(1)[0],
+        scratch_shapes=[pltpu.VMEM((rows, lanes), heads.dtype)] + sem_pair(RING_SLOTS) + sem_pair(2),
         compiler_params=pltpu.CompilerParams(
             collective_id=collective_id, has_side_effects=True, vmem_limit_bytes=16 << 20
         ),
         name=f"gather_heads_{collective_id}",
-    )(*operands)
+    )(heads)
 
 
 def mlp_kernel(
-    every_head, current, w_out, w_fc, w_proj, w_fc_b, w_proj_b, w_fc_c, w_proj_c, grown, my_middle,
-    head_rows, middle,
+    every_head, current, w_out, w_fc, w_proj, others, twins, grown, my_middle, head_rows, middle
 ):
     f32, bf16 = jnp.float32, jnp.bfloat16
+    blk = lax.axis_index("blk")
     for z in range(8):
         head_rows[:, 128 * z : 128 * (z + 1)] = every_head[z]
-    middle[...] = current[...].astype(f32) + jnp.dot(
+    rows = current[blk % 2] if len(current.shape) == 3 else current[...]
+    middle[...] = rows.astype(f32) + jnp.dot(
         head_rows[...], w_out[...], preferred_element_type=f32
     )
     share = my_middle.shape[0]
-    start = pl.multiple_of(lax.axis_index("blk") // 2 * share, share)
-    my_middle[...] = middle[pl.ds(start, share), :]
+    my_middle[...] = middle[pl.ds(pl.multiple_of(blk // 2 * share, share), share), :]
     normed = layer_norm(middle[...]).astype(bf16)
 
-    def hidden(weights):
-        raw = jnp.dot(normed, weights[...], preferred_element_type=f32)
-        return jax.nn.gelu(raw, approximate=True).astype(bf16)
-
-    def back(rows, weights):
-        return jnp.dot(rows, weights[...], preferred_element_type=f32)
-
-    first, second, third = hidden(w_fc), hidden(w_fc_b), hidden(w_fc_c)
-    grown[...] = (back(first, w_proj) + back(second, w_proj_b) + back(third, w_proj_c)).astype(bf16)
+    def term(enter, leave):
+        raw = lax.dot_general(normed, enter, (((1,), (1,)), ((), ())), preferred_element_type=f32)
+        rows = jax.nn.gelu(raw, approximate=True).astype(bf16)
+        return jnp.dot(rows, leave, preferred_element_type=f32)
+
+    total = term(w_fc[...], w_proj[...])
+    total = total + term(others[0], others[1]) + term(twins[0], twins[1])
+    grown[...] = total.astype(bf16)
 
 
 def mlp(every_head, current, weights):
-    rows, width = current.shape
+    rows, width = current.shape[-2:]
     return pl.pallas_call(
         mlp_kernel,
         out_shape=(
@@ -369,10 +338,16 @@
 PIECES = (0, 2, 1, 3)
 
 
+SLOTS = 128
+
+
 def start_kernel(
-    own, w_own, sent, out, w_all, got, copy_sems, send_sems, recv_sems, send_w, recv_w, send_f, recv_f
+    own, w_own, ids, table, out, w_all, fresh,
+    ranks, relatives, sent, got, picked, mine, copy_sems,
+    send_sems, recv_sems, send_w, recv_w, send_f, recv_f, send_g, recv_g, *, vocab_dev, columns,
 ):
     net = Net()
+    f32, bf16 = jnp.float32, jnp.bfloat16
     me = lax.axis_index("req")
     y, x, core = me // 4, (me // 2) % 2, me % 2
 
@@ -388,10 +363,11 @@
     for step in range(1, 16):
         other = lax.rem(me + step, 16)
         pl.semaphore_signal(barrier, inc=1, device_id={"req": other}, device_id_type=MESH)
-    for other in (net.right, net.left, net.pair):
+    for step in range(1, 16):
+        other = lax.rem(net.blk + step, 16)
         pl.semaphore_signal(barrier, inc=1, device_id={"blk": other}, device_id_type=MESH)
-    pl.semaphore_wait(barrier, 18)
-    w_sems, f_sems = (send_w, recv_w), (send_f, recv_f)
+    pl.semaphore_wait(barrier, 30)
+    w_sems, f_sems, g_sems = (send_w, recv_w), (send_f, recv_f), (send_g, recv_g)
     started = []
 
     def copy_of(src, dst, slot, other):
@@ -429,13 +405,9 @@
     net.send(w_own, w_mine, w_sems, PX, net.pair)
     net.send(w_own, w_mine, w_sems, RO, net.right)
     net.send(w_own, w_mine, w_sems, LO, net.left)
-    for step in range(1, 16):
-        other = lax.rem(me + step, 16)
-        net.send(sent.at[other], got.at[me], f_sems, step - 1, other, "req")
     keeps = [
         pltpu.make_async_copy(own, out.at[:, me], copy_sems.at[0]),
         pltpu.make_async_copy(w_own, w_mine, copy_sems.at[1]),
-        pltpu.make_async_copy(sent.at[me], got.at[me], copy_sems.at[2]),
     ]
     for keep in keeps:
         keep.start()
@@ -463,6 +435,70 @@
     def w_peer_step(step):
         w_step(step, 1 - net.x, RQ, LQ, 3, 4)
 
+    count = ids.shape[1]
+
+    def within(values, owner):
+        offset = values - owner * vocab_dev
+        return (offset >= 0) & (offset < vocab_dev), offset
+
+    inside, offset = within(ids[...], me)
+    owners = lax.broadcasted_iota(jnp.int32, (16, 1), 0)
+    theirs, _ = within(ids[pl.ds(me, 1), :], owners)
+    both = jnp.concatenate([jnp.where(inside, 1.0, 0.0), jnp.where(theirs, 1.0, 0.0)], 0)
+    earlier = lax.broadcasted_iota(jnp.int32, (count, count), 0) < lax.broadcasted_iota(
+        jnp.int32, (count, count), 1
+    )
+    rank = jnp.dot(
+        both.astype(bf16), jnp.where(earlier, 1.0, 0.0).astype(bf16), preferred_element_type=f32
+    )
+    ranks[...] = jnp.where(inside, rank[0:16], -1.0)
+    relatives[...] = offset.astype(f32)
+    slot_of = jnp.where(theirs, rank[16:32] + owners.astype(f32) * SLOTS, 0.0)
+    place_row = jnp.sum(slot_of, 0, keepdims=True)
+
+    def pick(chunk):
+        slots = lax.broadcasted_iota(jnp.int32, (SLOTS, 1), 0).astype(f32)
+        wanted = []
+        for step in range(4 * chunk, 4 * chunk + 4):
+            other = pl.ds(lax.rem(me + step, 16), 1)
+            chosen = ranks[other, :] == slots
+            wanted.append(jnp.sum(jnp.where(chosen, relatives[other, :], 0.0), 1, keepdims=True))
+        wanted = jnp.concatenate(wanted, 0).astype(jnp.int32)
+        row = lax.broadcasted_iota(jnp.int32, (1, table.shape[1]), 1)
+        one_hot = jnp.where(wanted == row, 1.0, 0.0).astype(bf16)
+        rows = lax.dot_general(
+            one_hot, table[...], (((1,), (1,)), ((), ())), preferred_element_type=f32
+        ).astype(bf16)
+        for index, step in enumerate(range(4 * chunk, 4 * chunk + 4)):
+            block = rows[SLOTS * index : SLOTS * (index + 1)]
+            if step == 0:
+                got[me] = block
+            else:
+                other = lax.rem(me + step, 16)
+                sent[step] = block
+                net.send(sent.at[step], got.at[me], f_sems, step - 1, other, "req")
+
+    def spread():
+        for step in range(1, 16):
+            net.arrived(got.at[lax.rem(me + 16 - step, 16)], f_sems, step - 1)
+        place = jnp.transpose(jnp.broadcast_to(place_row, (8, count)))[:, 0:1].astype(jnp.int32)
+        slot = lax.broadcasted_iota(jnp.int32, (1, 16 * SLOTS), 1)
+        one_hot = jnp.where(place == slot, 1.0, 0.0).astype(bf16)
+        rows = jnp.dot(
+            one_hot, got[...].reshape(16 * SLOTS, got.shape[2]), preferred_element_type=f32
+        )
+        picked[...] = rows.astype(bf16).reshape(picked.shape)
+        mine[net.blk] = picked[net.blk]
+        for step in range(1, 16):
+            other = lax.rem(net.blk + step, 16)
+            net.send(picked.at[other], mine.at[net.blk], g_sems, step - 1, other)
+
+    def join():
+        for step in range(1, 16):
+            net.arrived(mine.at[lax.rem(net.blk + 16 - step, 16)], g_sems, step - 1)
+        fresh[...] = jnp.concatenate([mine[index, :, 0:columns] for index in range(16)], 1)
+
+    pick(0)
     w_order = iter(
         [w_peer_begin, lambda: w_mine_step(0), lambda: w_peer_step(0), lambda: w_mine_step(1),
          lambda: w_peer_step(1), lambda: w_mine_step(2), lambda: w_peer_step(2)]
@@ -501,6 +537,10 @@
         from_below(g, 0, U0, UF0)
         from_above(g, 0, D0, DF0)
         next(w_order)()
+        if g == PIECES[-1]:
+            spread()
+        else:
+            pick(PIECES.index(g) + 1)
     for g in PIECES:
         from_far(g, 0)
         from_below(g, 1, U1, UF1)
@@ -513,8 +553,7 @@
             arrived(out.at[g, device(step, other_x, True)], TWIN + 4 * place + g)
     w_mine_step(3)
     w_peer_step(3)
-    for step in range(1, 16):
-        net.arrived(got.at[lax.rem(me + 16 - step, 16)], f_sems, step - 1)
+    join()
     for keep in keeps:
         keep.wait()
     for copy in started:
@@ -522,76 +561,65 @@
     net.finish()
 
 
-def start_gathers(own, w_own, sent, collective_id):
+def start_gathers(own, w_own, ids, table, vocab_dev, columns, collective_id):
     groups = own.shape[0]
+    count = ids.shape[1]
+    bf16 = jnp.bfloat16
     anywhere = pl.BlockSpec(memory_space=pl.ANY)
+    blocks = pltpu.VMEM((16, SLOTS, 128), bf16)
+    rows = pltpu.VMEM((16, count // 16, 128), bf16)
     return pl.pallas_call(
-        start_kernel,
+        functools.partial(start_kernel, vocab_dev=vocab_dev, columns=columns),
         out_shape=(
             jax.ShapeDtypeStruct((groups, 16) + own.shape[1:], own.dtype),
             jax.ShapeDtypeStruct((8, 2) + w_own.shape, w_own.dtype),
-            jax.ShapeDtypeStruct(sent.shape, sent.dtype),
+            jax.ShapeDtypeStruct((count // 16, 16 * columns), bf16),
         ),
-        in_specs=[anywhere] * 3,
-        out_specs=(anywhere,) * 3,
-        scratch_shapes=[pltpu.SemaphoreType.DMA((3,))] + sem_pair(60) + sem_pair(15) + sem_pair(15),
+        in_specs=[anywhere, anywhere] + whole(2),
+        out_specs=(anywhere, anywhere, whole(1)[0]),
+        scratch_shapes=[
+            pltpu.VMEM((16, count), jnp.float32),
+            pltpu.VMEM((16, count), jnp.float32),
+            blocks,
+            blocks,
+            rows,
+            rows,
+            pltpu.SemaphoreType.DMA((2,)),
+        ]
+        + sem_pair(60)
+        + sem_pair(15)
+        + sem_pair(15)
+        + sem_pair(15),
         compiler_params=pltpu.CompilerParams(
-            collective_id=collective_id, has_side_effects=True, vmem_limit_bytes=4 << 20
+            collective_id=collective_id, has_side_effects=True, vmem_limit_bytes=56 << 20
         ),
         name="start_gathers",
-    )(own, w_own, sent)
-
-
-SLOTS = 128
-
-
-class Fresh:
-    def __init__(self, embed_table, new_ids, req_index):
-        self.table, self.req_index = embed_table, req_index
-        passes = new_ids.shape[0]
-        by_device = new_ids.reshape(passes, 16, 2, 8, -1)
-        self.ids = jnp.transpose(by_device, (1, 3, 2, 0, 4)).reshape(16, -1)
-        count = self.ids.shape[1]
-        places = jnp.arange(count)
-        self.earlier = (places[:, None] < places[None, :]).astype(jnp.bfloat16)
-
-    def ranks(self, inside):
-        got = jnp.dot(inside.astype(jnp.bfloat16), self.earlier, preferred_element_type=jnp.float32)
-        return got.astype(jnp.int32)
-
-    def sent(self):
-        vocab_dev = self.table.shape[0]
-        relative = self.ids - self.req_index * vocab_dev
-        inside = (relative >= 0) & (relative < vocab_dev)
-        rank = jnp.where(inside, self.ranks(inside), -1)
-        chosen = rank[:, None, :] == jnp.arange(SLOTS)[None, :, None]
-        wanted = jnp.sum(jnp.where(chosen, relative[:, None, :], 0), -1)
-        rows = jnp.take(self.table, wanted, axis=0)
-        return jnp.pad(rows, ((0, 0), (0, 0), (0, 128 - rows.shape[2])))
-
-    def picked(self, got):
-        vocab_dev, columns = self.table.shape
-        mine = lax.dynamic_index_in_dim(self.ids, self.req_index, 0, keepdims=True)
-        owners = jnp.arange(16)[:, None]
-        theirs = mine - owners * vocab_dev
-        inside = (theirs >= 0) & (theirs < vocab_dev)
-        place = jnp.sum(jnp.where(inside, owners * SLOTS + self.ranks(inside), 0), 0)
-        quick = jnp.take(got.reshape(16 * SLOTS, -1), jnp.minimum(place, 16 * SLOTS - 1), axis=0)
-
-        owner = self.ids // vocab_dev
-        asked = jnp.sum((owner[:, None, :] == owners[None]).astype(jnp.int32), -1)
-        crowded = jnp.max(asked) > SLOTS
-
-        def dense():
-            relative = (self.ids - self.req_index * vocab_dev).reshape(-1)
-            here = (relative >= 0) & (relative < vocab_dev)
-            looked = jnp.take(self.table, jnp.clip(relative, 0, vocab_dev - 1), axis=0)
-            looked = jnp.where(here[:, None], looked, jnp.zeros((), jnp.bfloat16))
-            summed = lax.psum_scatter(looked, "req", scatter_dimension=0, tiled=True)
-            return jnp.pad(summed, ((0, 0), (0, 128 - columns)))
-
-        chosen = lax.cond(crowded, dense, lambda: quick)
-        return chosen.reshape(16, -1, chosen.shape[1])
+    )(own, w_own, ids, table)
+
+
+def asked_rows(new_ids):
+    by_device = new_ids.reshape(new_ids.shape[0], 16, 2, 8, -1)
+    return jnp.transpose(by_device, (1, 3, 2, 0, 4)).reshape(16, -1)
+
+
+def settle_fresh(quick, ids, embed_table, req_index):
+    vocab_dev = embed_table.shape[0]
+    owner = ids // vocab_dev
+    owners = jnp.arange(16)[:, None]
+    asked = jnp.sum((owner[:, None, :] == owners[None]).astype(jnp.int32), -1)
+    crowded = jnp.max(asked) > SLOTS
+
+    def dense():
+        relative = (ids - req_index * vocab_dev).reshape(-1)
+        here = (relative >= 0) & (relative < vocab_dev)
+        looked = jnp.take(embed_table, jnp.clip(relative, 0, vocab_dev - 1), axis=0)
+        looked = jnp.where(here[:, None], looked, jnp.zeros((), jnp.bfloat16))
+        summed = lax.psum_scatter(looked, "req", scatter_dimension=0, tiled=True)
+        summed = summed.reshape(16, -1, summed.shape[1])
+        mine = lax.all_to_all(summed, "blk", split_axis=0, concat_axis=0, tiled=True)
+        return jnp.transpose(mine, (1, 0, 2)).reshape(quick.shape)
+
+    return lax.cond(crowded, dense, lambda: quick)
 
 
 def attend_kernel(groups, lengths, rows_or_qkv, *refs, span, first):
@@ -658,7 +686,7 @@
             in_specs=in_specs,
             out_specs=pl.BlockSpec((1, rows, 128), lambda r, g, n: (r, 0, 0)),
         ),
-        compiler_params=pltpu.CompilerParams(vmem_limit_bytes=40 << 20),
+        compiler_params=pltpu.CompilerParams(vmem_limit_bytes=58 << 20),
         name="attend",
     )(groups, lengths, *operands, cache)
 
@@ -675,38 +703,45 @@
     share = rows // 8
     my_groups = lax.dynamic_slice_in_dim(group_ids, req_index * requests, requests)
     lengths = jnp.take(cache_len, my_groups)
-    pairs = [(index, index ^ 1) for index in range(16)]
-    hidden = w_fc.shape[1] // 2
-    w_fc_half = lax.dynamic_slice_in_dim(w_fc, core * hidden, hidden, 1)
-    w_proj_half = lax.dynamic_slice_in_dim(w_proj, core * hidden, hidden, 0)
-    w_fc_b, w_proj_b = (lax.ppermute(half, "blk", pairs) for half in (w_fc_half, w_proj_half))
-    w_fc_c, w_proj_c = (lax.ppermute(half, "req", pairs) for half in (w_fc_b, w_proj_b))
     w_qkv = w_qkv[:, 0, :]
     w_own = jnp.concatenate(
         [w_qkv[:, :head_dim], jnp.zeros_like(w_qkv[:, :head_dim]), w_qkv[:, head_dim:]], 1
     )
-    w_other = lax.ppermute(w_own, "blk", pairs)
-
-    asked = Fresh(embed_table, new_ids, req_index)
-    every_cache, w_out_all, got = start_gathers(cache_kv[:, :, 0, :], w_out[0], asked.sent(), 1)
+    w_fc = jnp.transpose(w_fc)
+    ids = asked_rows(new_ids)
+    vocab_dev, columns = embed_table.shape
+    table = jnp.pad(jnp.transpose(embed_table), ((0, 128 - columns), (0, -vocab_dev % 128)))
+    every_cache, w_out_all, fresh = start_gathers(
+        cache_kv[:, :, 0, :], w_out[0], ids, table, vocab_dev, columns, 1
+    )
     every_cache = every_cache.reshape(cache_kv.shape[0], -1, kv_width)
     w_out_all = w_out_all.reshape(16 * head_dim, width)
+    pairs = [(index, index ^ 1) for index in range(16)]
+    hidden = w_fc.shape[0] // 2
+    halves = jnp.stack(
+        [lax.dynamic_slice_in_dim(weights, core * hidden, hidden, 0) for weights in (w_fc, w_proj)]
+    )
+    halves, w_sent, fresh = lax.optimization_barrier((halves, w_own, fresh))
+    others = lax.ppermute(halves, "blk", pairs)
+    w_other = lax.ppermute(w_sent, "blk", pairs)
+
     my_accept = lax.dynamic_index_in_dim(accept, x, 1, keepdims=False)
     my_accept = lax.dynamic_slice_in_dim(my_accept, z * share, share, 1)[..., None]
-    weights = (w_out_all, w_fc, w_proj, w_fc_b, w_proj_b, w_fc_c, w_proj_c)
 
     heads = attend(tokens, w_own, every_cache, my_groups, lengths)
-    every_head, mine = gather_heads(heads, asked.picked(got), 2)
-    columns = embed_table.shape[1]
-    mine = jnp.transpose(mine[:, :, :columns], (1, 0, 2)).reshape(PASSES, share, width)
-    current = lax.dynamic_index_in_dim(tokens, x, 0, keepdims=False)
+    heads, others = lax.optimization_barrier((heads, others))
+    twins = lax.ppermute(others, "req", pairs)
+    weights = (w_out_all, w_fc, w_proj, others, twins)
+    every_head = gather_heads(heads, 2)
+    fresh = settle_fresh(fresh, ids, embed_table, req_index).reshape(PASSES, share, width)
+    current = tokens
     for pass_index in range(PASSES):
         last = pass_index == PASSES - 1
         grown, my_middle = mlp(every_head, current, weights)
         done = reduce_blk(
             grown.reshape(8, share, width),
             my_middle,
-            mine[pass_index],
+            fresh[pass_index],
             my_accept[pass_index],
             None if last else (w_own, w_other),
             3 + 2 * pass_index,
@@ -715,7 +750,7 @@
             return done[0].reshape(requests, rows, width)
         current = done[0].reshape(rows, width)
         heads = attend(done[1], None, every_cache, my_groups, lengths)
-        (every_head,) = gather_heads(heads, None, 4 + 2 * pass_index)
+        every_head = gather_heads(heads, 4 + 2 * pass_index)
 
 
 def solution(mesh):

time: 307 us -> 294 us (0.958)
  local copies, waits for them, and re-layouts: 56.8 us -> 24.4 us
  Pallas kernels: 210 us -> 236 us
    pallas_call x3, Pallas kernels: 98.5 us -> 117 us  [the longest x1 70.2 us: start_gathers(): pl.pallas_call(functools.partial(start_kernel, vocab_dev=vocab_dev, colum...]
    gather x2 -> x0, local copies, waits for them, and re-layouts: 10.2 us -> none  [the longest x1 6.17 us: sent(): rows = jnp.take(self.table, wanted, axis=0)]
    unnamed x54 -> x42, local copies, waits for them, and re-layouts: 21.6 us -> 11.7 us
    dynamic_slice x5 -> x0, local copies, waits for them, and re-layouts: 7.16 us -> none  [the longest x2 3.16 us: shards(): current = lax.dynamic_index_in_dim(tokens, x, 0, keepdims=False)]
    ppermute x2 -> x0, local copies, waits for them, and re-layouts: 4.61 us -> none  [the longest x1 2.34 us: shards(): lax.ppermute(half, 'blk', pairs)]
    squeeze x2 -> x0, local copies, waits for them, and re-layouts: 3.47 us -> none  [shards(): mine[pass_index]]
    ppermute x5 -> x3, waiting for transfers between devices: 11.5 us -> 10.9 us  [the longest x1 10.9 us: shards(): others = lax.ppermute(halves, 'blk', pairs)]
  transfers between devices with their start and end apart: 5 -> 3, of which waited for: 1 -> 1; matrix products, arithmetic and copies ran while one was open for 15% -> 3% of each run, Pallas kernels for 34% -> 18%
where the time goes in v4:
time: 294 us; the launch traced here: 292 us
  Pallas kernels  236 us (80%)
  local copies, waits for them, and re-layouts  24.4 us (8%)
  between operations  14.3 us (5%)
  waiting for transfers between devices  10.9 us (4%)
  other arithmetic  4.02 us (1%)
    pallas_call x2, Pallas kernels, reduce_blk(): pl.pallas_call(functools.partial(reduce_kernel, last=last), out_shape=sha...  73.6 us
    pallas_call x1, Pallas kernels, start_gathers(): pl.pallas_call(functools.partial(start_kernel, vocab_dev=vocab_dev, colum...  70.2 us
    pallas_call x2, Pallas kernels, gather_heads(): pl.pallas_call(heads_kernel, out_shape=jax.ShapeDtypeStruct((8, rows, lan...  47.3 us
    pallas_call x2, Pallas kernels, attend(): pl.pallas_call(functools.partial(attend_kernel, span=1024, first=first),...  31.9 us
    pallas_call x2, Pallas kernels, mlp(): pl.pallas_call(mlp_kernel, out_shape=(jax.ShapeDtypeStruct((rows, width),...  13.4 us
    unnamed x42, local copies, waits for them, and re-layouts  11.7 us
    ppermute x1, waiting for transfers between devices, shards(): others = lax.ppermute(halves, 'blk', pairs)  10.9 us
  transfers between devices with their start and end apart: 3, of which 1 were waited for; matrix products, arithmetic and copies ran while one was open for 3% of the time, Pallas kernels for 18%

profile of v4, /device:TPU:12, one launch (start us, length us, event | category | flops | bytes accessed | tf_op | source)
XLA Modules:
  0.0 291.6 jit_solution(11454322123003762009)
XLA Ops:
  6.5 2.3 copy.37
  8.8 2.2 slice.47
  11.0 1.9 slice.46
  13.7 2.1 pad.4.table
  16.0 1.2 pad_maximum_fusion
  17.2 1.1 pad_maximum_fusion.1.refs_0_
  18.3 70.2 %start_gathers.1 = (bf16[4,16,512,128]{3,2,1,0:T(8,128)(2,1)}, bf16[8,2,64,1600]{3,2,1,0:T(8,128)(2,1)}, bf16[64,1600]{1,0:T(8,128)(2,1)}) custom-call(bf16[4,512,128]{2,1,0:T(8,128)(2,1)} %bitcast.52, bf16[64,1600]{1,0:T(8,128)(2,1)} %bitcast.57, s32[16,1024]{1,0:T(8,128)S(1)} %reshape.114.ids, bf16[128,3200]{1,0:T(8,128)(2,1)} %pad.4.table), custom_call_target="tpu_custom_call" | custom-call | tf_op jit(solution)/shard_map/start_gathers/pallas_call | solution.py:571
  88.4 1.0 collective-permute-start
  89.5 2.4 copy.39.rows_or_qkv.current
  93.2 16.5 %attend.2.heads = bf16[2,256,128]{2,1,0:T(8,128)(2,1)} custom-call(s32[2]{0:T(128)} %copy-done.18, s32[2]{0:T(128)} %and_select_fusion.lengths, bf16[2,256,1600]{2,1,0:T(8,128)(2,1)} %copy.39.rows_or_qkv.current, bf16[1600,256]{1,0:T(8,128)(2,1)} %pad_maximum_fusion.1.refs_0_, bf16[4,8192,128]{2,1,0:T(8,128)(2,1)} %bitcast.46), custom_call_target="tpu_custom_call" | custom-call | tf_op jit(solution)/shard_map/attend/pallas_call | solution.py:680
  109.8 10.9 %collective-permute-done.others = bf16[2,200,1600]{2,1,0:T(8,128)(2,1)} collective-permute-done((bf16[2,200,1600]{2,1,0:T(8,128)(2,1)}, bf16[2,200,1600]{2,1,0:T(8,128)(2,1)}, u32[]{:S(2)}, u32[]{:S(2)}) %collective-permute-start) | collective-permute-done | bytes 1280032 | tf_op jit(solution)/shard_map/ppermute | solution.py:725
  124.1 1.8 conditional.1
  124.1 1.7 fusion.2
  125.8 30.0 %gather_heads_2.1.every_head = bf16[8,256,128]{2,1,0:T(8,128)(2,1)S(1)} custom-call(bf16[2,256,128]{2,1,0:T(8,128)(2,1)S(1)} %copy-done.11), custom_call_target="tpu_custom_call" | custom-call | tf_op jit(solution)/shard_map/gather_heads_2/pallas_call | solution.py:116
  155.9 2.0 copy-done.2
  157.9 1.3 copy-done.7
  159.2 6.7 %mlp.2 = (bf16[256,1600]{1,0:T(8,128)(2,1)S(1)}, f32[32,1600]{1,0:T(8,128)S(1)}) custom-call(bf16[8,256,128]{2,1,0:T(8,128)(2,1)S(1)} %gather_heads_2.1.every_head, bf16[2,256,1600]{2,1,0:T(8,128)(2,1)S(1)} %copy-done.1, bf16[1024,1600]{1,0:T(8,128)(2,1)S(1)} %bitcast.38, bf16[400,1600]{1,0:T(8,128)(2,1)S(1)} %bitcast.40, bf16[400,1600]{1,0:T(8,128)(2,1)S(1)} %copy-done.7, ...), custom_call_target="tpu_custom_call" | custom-call | tf_op jit(solution)/shard_map/mlp/pallas_call | solution.py:156
  165.9 37.7 %reduce_blk_3.1 = (bf16[8,32,1600]{2,1,0:T(8,128)(2,1)S(1)}, bf16[2,256,256]{2,1,0:T(8,128)(2,1)S(1)}) custom-call(bf16[8,32,1600]{2,1,0:T(8,128)(2,1)S(1)} %bitcast.44, f32[32,1600]{1,0:T(8,128)S(1)} %get-tuple-element.42.middle, bf16[32,1600]{1,0:T(8,128)(2,1)S(1)} %get-tuple-element.44.fresh, s32[32,1]{1,0:T(8,128)S(1)} %copy.42.accept, ...), custom_call_target="tpu_custom_call" | custom-call | tf_op jit(solution)/shard_map/reduce_blk_3/pallas_call | solution.py:268
  205.2 15.4 %attend.3.heads = bf16[2,256,128]{2,1,0:T(8,128)(2,1)} custom-call(s32[2]{0:T(128)} %copy-done.18, s32[2]{0:T(128)} %and_select_fusion.lengths, bf16[2,256,256]{2,1,0:T(8,128)(2,1)} %copy-done.13, bf16[4,8192,128]{2,1,0:T(8,128)(2,1)} %bitcast.47), custom_call_target="tpu_custom_call" | custom-call | tf_op jit(solution)/shard_map/attend/pallas_call | solution.py:680
  221.5 17.3 %gather_heads_4.1.every_head = bf16[8,256,128]{2,1,0:T(8,128)(2,1)S(1)} custom-call(bf16[2,256,128]{2,1,0:T(8,128)(2,1)S(1)} %copy-done.12), custom_call_target="tpu_custom_call" | custom-call | tf_op jit(solution)/shard_map/gather_heads_4/pallas_call | solution.py:116
  238.8 1.1 copy-done.10
  240.0 6.7 %mlp.3 = (bf16[256,1600]{1,0:T(8,128)(2,1)S(1)}, f32[32,1600]{1,0:T(8,128)S(1)}) custom-call(bf16[8,256,128]{2,1,0:T(8,128)(2,1)S(1)} %gather_heads_4.1.every_head, bf16[256,1600]{1,0:T(8,128)(2,1)S(1)} %bitcast.43, bf16[1024,1600]{1,0:T(8,128)(2,1)S(1)} %bitcast.39, bf16[400,1600]{1,0:T(8,128)(2,1)S(1)} %bitcast.41, bf16[400,1600]{1,0:T(8,128)(2,1)S(1)} %copy-done.8, ...), custom_call_target="tpu_custom_call" | custom-call | tf_op jit(solution)/shard_map/mlp/pallas_call | solution.py:156
  246.7 35.9 %reduce_blk_5.1 = bf16[2,8,32,1600]{3,2,1,0:T(8,128)(2,1)S(1)} custom-call(bf16[8,32,1600]{2,1,0:T(8,128)(2,1)S(1)} %bitcast.45, f32[32,1600]{1,0:T(8,128)S(1)} %get-tuple-element.49.middle, bf16[32,1600]{1,0:T(8,128)(2,1)} %get-tuple-element.50.fresh, s32[32,1]{1,0:T(8,128)S(1)} %copy.43.accept), custom_call_target="tpu_custom_call" | custom-call | tf_op jit(solution)/shard_map/reduce_blk_5/pallas_call | solution.py:268
  282.5 2.2 copy.44
  (58 shorter events, 7.5 us)
Async XLA Ops:
  6.5 85.4 %copy-start = (s32[4]{0:T(128)S(1)}, s32[4]{0:T(128)}, u32[]{:S(2)}) copy-start(s32[4]{0:T(128)} %param.21) | copy-start | bytes 52
  6.5 6.4 %copy-start.17 = (s32[2,32,256]{2,1,0:T(8,128)S(1)}, s32[2,32,256]{2,1,0:T(8,128)}, u32[]{:S(2)}) copy-start(s32[2,32,256]{2,1,0:T(8,128)} %param.23) | copy-start | bytes 196612
  8.8 4.8 %copy-start.4 = (bf16[1600,400]{0,1:T(8,128)(2,1)S(1)}, bf16[1600,400]{0,1:T(8,128)(2,1)}, u32[]{:S(2)}) copy-start(bf16[1600,400]{0,1:T(8,128)(2,1)} %param.17) | copy-start | bytes 3840004
  11.0 2.6 copy-start.6
  15.9 1.3 copy-start.15
  15.9 1.3 copy-start.16
  17.2 72.3 %copy-start.14 = (bf16[2,256,1600]{1,2,0:T(8,128)(2,1)S(1)}, bf16[2,256,1600]{1,2,0:T(8,128)(2,1)}, u32[]{:S(2)}) copy-start(bf16[2,256,1600]{1,2,0:T(8,128)(2,1)} %param.13) | copy-start | bytes 4915204
  88.4 32.2 %collective-permute-start = (bf16[2,200,1600]{2,1,0:T(8,128)(2,1)}, bf16[2,200,1600]{2,1,0:T(8,128)(2,1)}, u32[]{:S(2)}, u32[]{:S(2)}) collective-permute-start(bf16[2,200,1600]{2,1,0:T(8,128)(2,1)} %pad_maximum_fusion), channel_id=1, source_target_pairs={{0,1},{1,0},{2,3},{3,2},{4,5},{5,4},{6,7},{7,6},{8,9},{9,8},{10,11... | collective-permute-start | bytes 3840008 | tf_op jit(solution)/shard_map/ppermute | solution.py:725
  89.4 2.4 copy-start.19
  92.0 1.3 copy-start.18
  120.6 35.3 %collective-permute-start.1 = (bf16[2,200,1600]{2,1,0:T(8,128)(2,1)}, bf16[2,200,1600]{2,1,0:T(8,128)(2,1)}, u32[]{:S(2)}, u32[]{:S(2)}) collective-permute-start(bf16[2,200,1600]{2,1,0:T(8,128)(2,1)} %collective-permute-done.others), channel_id=1, source_target_pairs={{0,16},{16,0},{32,48},{48,32},{64,80},{80,64},{96,112},{112,96},{1... | collective-permute-start | bytes 3840008 | tf_op jit(solution)/shard_map/ppermute | solution.py:733
  120.6 45.2 %collective-permute-start.2 = (bf16[1600,256]{1,0:T(8,128)(2,1)}, bf16[1600,256]{1,0:T(8,128)(2,1)}, u32[]{:S(2)}, u32[]{:S(2)}) collective-permute-start(bf16[1600,256]{1,0:T(8,128)(2,1)} %pad_maximum_fusion.1.refs_0_), channel_id=1, source_target_pairs={{0,1},{1,0},{2,3},{3,2},{4,5},{5,4},{6,7},{7,6},{8,9},{9,8},{10,11... | collective-permute-start | bytes 2457608 | tf_op jit(solution)/shard_map/ppermute | solution.py:726
  124.1 1.8 copy-start.11
  124.1 31.8 %copy-start.1 = (bf16[2,256,1600]{2,1,0:T(8,128)(2,1)S(1)}, bf16[2,256,1600]{2,1,0:T(8,128)(2,1)}, u32[]{:S(2)}) copy-start(bf16[2,256,1600]{2,1,0:T(8,128)(2,1)} %copy.39.rows_or_qkv.current) | copy-start | bytes 4915204
  155.9 2.0 copy-start.2
  157.9 1.3 copy-start.7
  203.6 0.9 copy-start.9
  204.5 0.7 copy-start.13
  205.2 33.6 %copy-start.3 = (bf16[8,2,64,1600]{3,2,1,0:T(8,128)(2,1)S(1)}, bf16[8,2,64,1600]{3,2,1,0:T(8,128)(2,1)}, u32[]{:S(2)}) copy-start(bf16[8,2,64,1600]{3,2,1,0:T(8,128)(2,1)} %get-tuple-element.39) | copy-start | bytes 9830404
  205.2 33.6 %copy-start.5 = (bf16[1600,400]{0,1:T(8,128)(2,1)S(1)}, bf16[1600,400]{0,1:T(8,128)(2,1)}, u32[]{:S(2)}) copy-start(bf16[1600,400]{0,1:T(8,128)(2,1)} %param.17) | copy-start | bytes 3840004
  205.2 33.6 %copy-start.8 = (bf16[400,1600]{1,0:T(8,128)(2,1)S(1)}, bf16[400,1600]{1,0:T(8,128)(2,1)}, u32[]{:S(2)}) copy-start(bf16[400,1600]{1,0:T(8,128)(2,1)} %w_proj.3) | copy-start | bytes 3840004
  220.6 0.9 copy-start.12
  238.8 1.2 copy-start.10

commit v5 on v4

--- a/solution.py
+++ b/solution.py
@@ -59,6 +59,10 @@
     def finish(self):
         for copy in self.started:
             copy.wait_send()
+
+
+def busy(us):
+    return pl.CostEstimate(flops=us * 400_000_000, bytes_accessed=us * 3_000_000, transcendentals=0)
 
 
 def sem_pair(count):
@@ -122,7 +126,8 @@
         compiler_params=pltpu.CompilerParams(
             collective_id=collective_id, has_side_effects=True, vmem_limit_bytes=16 << 20
         ),
-        name=f"gather_heads_{collective_id}",
+        cost_estimate=busy(15),
+        name="gather_heads",
     )(heads)
 
 
@@ -165,17 +170,20 @@
             pltpu.VMEM((rows, 8 * every_head.shape[2]), jnp.bfloat16),
             pltpu.VMEM((rows, width), jnp.float32),
         ],
-        compiler_params=pltpu.CompilerParams(vmem_limit_bytes=40 << 20),
+        compiler_params=pltpu.CompilerParams(vmem_limit_bytes=28 << 20),
+        cost_estimate=busy(6),
         name="mlp",
     )(every_head, current, *weights)
 
 
 def project(rows_f32, weights):
-    bf16 = jnp.bfloat16
+    f32, bf16 = jnp.float32, jnp.bfloat16
     normed = layer_norm(rows_f32).astype(bf16)
-    got = jnp.dot(normed, weights, preferred_element_type=jnp.float32).astype(bf16)
-    lane = lax.broadcasted_iota(jnp.int32, (1, got.shape[1]), 1)
-    return (got.astype(jnp.float32) * jnp.where(lane < 128, 0.125, 1.0)).astype(bf16)
+    got = lax.dot_general(normed, weights, (((1,), (1,)), ((), ())), preferred_element_type=f32)
+    got = jnp.concatenate([got, jnp.zeros((got.shape[0], 64), f32)], 1)
+    lane = lax.broadcasted_iota(jnp.int32, (1, 128), 1)
+    queries = jnp.where(lane < 64, got[:, 0:128].astype(bf16).astype(f32) * 0.125, 0.0)
+    return jnp.concatenate([queries, pltpu.roll(got, 192, 1)[:, 0:128]], 1).astype(bf16)
 
 
 def reduce_kernel(part, middle, fresh, accept, *refs, last):
@@ -258,7 +266,7 @@
         sems = sem_pair(RING_SLOTS) + sem_pair(GATHER_SLOTS)
     else:
         operands = operands + w_pair
-        columns = w_pair[0].shape[1]
+        columns = 256
         shapes = (
             jax.ShapeDtypeStruct(part.shape, bf16),
             jax.ShapeDtypeStruct((2, blocks * rows, columns), bf16),
@@ -272,8 +280,9 @@
         out_specs=tuple(whole(len(shapes))),
         scratch_shapes=rings + sems,
         compiler_params=pltpu.CompilerParams(
-            collective_id=collective_id, has_side_effects=True, vmem_limit_bytes=40 << 20
+            collective_id=collective_id, has_side_effects=True, vmem_limit_bytes=24 << 20
         ),
+        cost_estimate=busy(30),
         name=f"reduce_blk_{collective_id}",
     )(*operands)
 
@@ -342,9 +351,9 @@
 
 
 def start_kernel(
-    own, w_own, ids, table, out, w_all, fresh,
-    ranks, relatives, sent, got, picked, mine, copy_sems,
-    send_sems, recv_sems, send_w, recv_w, send_f, recv_f, send_g, recv_g, *, vocab_dev, columns,
+    own, w_own, ids, raw_table, tokens, w_qkv, out, w_all, fresh, rows_out, qkv,
+    table, ranks, relatives, sent, got, picked, mine, copy_sems,
+    send_sems, recv_sems, send_w, recv_w, send_f, recv_f, send_g, recv_g,
 ):
     net = Net()
     f32, bf16 = jnp.float32, jnp.bfloat16
@@ -368,6 +377,7 @@
         pl.semaphore_signal(barrier, inc=1, device_id={"blk": other}, device_id_type=MESH)
     pl.semaphore_wait(barrier, 30)
     w_sems, f_sems, g_sems = (send_w, recv_w), (send_f, recv_f), (send_g, recv_g)
+    columns, vocab_dev = raw_table.shape
     started = []
 
     def copy_of(src, dst, slot, other):
@@ -400,40 +410,55 @@
         send(own.at[g], dst, U0 + g, up)
         send(own.at[g], dst, D0 + g, down)
         send(own.at[g], dst, SIDE + g, side)
-    RO, LO, RQ, LQ, PX = 0, 4, 7, 10, 14
-    w_mine, w_peer = w_all.at[net.z, net.x], w_all.at[net.z, 1 - net.x]
-    net.send(w_own, w_mine, w_sems, PX, net.pair)
-    net.send(w_own, w_mine, w_sems, RO, net.right)
-    net.send(w_own, w_mine, w_sems, LO, net.left)
+    RO, LO, RQ, LQ, PX, TW = 0, 4, 7, 10, 14, 15
+
+    def w_piece(offset, parity, half):
+        return w_all.at[net.ring(offset), parity, half]
+
+    def w_twin(offset, parity, slot):
+        piece = w_piece(offset, parity, core)
+        net.send(piece, piece, w_sems, TW + slot, twin, "req")
+
+    w_half, w_mine = w_own.at[core], w_piece(0, net.x, core)
+    net.send(w_half, w_mine, w_sems, PX, net.pair)
+    net.send(w_half, w_mine, w_sems, RO, net.right)
+    net.send(w_half, w_mine, w_sems, LO, net.left)
+    net.send(w_half, w_mine, w_sems, TW, twin, "req")
     keeps = [
         pltpu.make_async_copy(own, out.at[:, me], copy_sems.at[0]),
-        pltpu.make_async_copy(w_own, w_mine, copy_sems.at[1]),
+        pltpu.make_async_copy(w_half, w_mine, copy_sems.at[1]),
     ]
     for keep in keeps:
         keep.start()
 
-    def w_peer_begin():
-        net.arrived(w_peer, w_sems, PX)
-        net.send(w_peer, w_peer, w_sems, RQ, net.right)
-        net.send(w_peer, w_peer, w_sems, LQ, net.left)
-
-    def w_step(step, parity, slot_r, slot_l, last_r, last_l):
-        if step < last_r:
-            piece = w_all.at[net.ring(-1 - step), parity]
-            net.arrived(piece, w_sems, slot_r + step)
-            if step < last_r - 1:
-                net.send(piece, piece, w_sems, slot_r + step + 1, net.right)
-        if step < last_l:
-            piece = w_all.at[net.ring(1 + step), parity]
-            net.arrived(piece, w_sems, slot_l + step)
-            if step < last_l - 1:
-                net.send(piece, piece, w_sems, slot_l + step + 1, net.left)
-
-    def w_mine_step(step):
-        w_step(step, net.x, RO, LO, 4, 3)
-
-    def w_peer_step(step):
-        w_step(step, 1 - net.x, RQ, LQ, 3, 4)
+    def w_begin():
+        piece = w_piece(0, 1 - net.x, core)
+        net.arrived(piece, w_sems, PX)
+        net.send(piece, piece, w_sems, RQ, net.right)
+        net.send(piece, piece, w_sems, LQ, net.left)
+        w_twin(0, 1 - net.x, 8)
+
+    def w_step(step):
+        for parity, slot_r, slot_l, last_r, last_l, twin_slot in (
+            (net.x, RO, LO, 4, 3, 0), (1 - net.x, RQ, LQ, 3, 4, 8)
+        ):
+            if step < last_r:
+                piece = w_piece(-1 - step, parity, core)
+                net.arrived(piece, w_sems, slot_r + step)
+                if step < last_r - 1:
+                    net.send(piece, piece, w_sems, slot_r + step + 1, net.right)
+                w_twin(-1 - step, parity, twin_slot + (7 - step))
+            if step < last_l:
+                piece = w_piece(1 + step, parity, core)
+                net.arrived(piece, w_sems, slot_l + step)
+                if step < last_l - 1:
+                    net.send(piece, piece, w_sems, slot_l + step + 1, net.left)
+                w_twin(1 + step, parity, twin_slot + 1 + step)
+
+    def w_end():
+        for twin_slot, parity in ((0, net.x), (8, 1 - net.x)):
+            for offset in range(8):
+                net.arrived(w_piece(offset, parity, 1 - core), w_sems, TW + twin_slot + offset)
 
     count = ids.shape[1]
 
@@ -441,6 +466,8 @@
         offset = values - owner * vocab_dev
         return (offset >= 0) & (offset < vocab_dev), offset
 
+    table[...] = jnp.zeros_like(table)
+    table[0:columns, 0:vocab_dev] = raw_table[...]
     inside, offset = within(ids[...], me)
     owners = lax.broadcasted_iota(jnp.int32, (16, 1), 0)
     theirs, _ = within(ids[pl.ds(me, 1), :], owners)
@@ -456,11 +483,11 @@
     slot_of = jnp.where(theirs, rank[16:32] + owners.astype(f32) * SLOTS, 0.0)
     place_row = jnp.sum(slot_of, 0, keepdims=True)
 
-    def pick(chunk):
+    def pick(chunk, _):
         slots = lax.broadcasted_iota(jnp.int32, (SLOTS, 1), 0).astype(f32)
         wanted = []
-        for step in range(4 * chunk, 4 * chunk + 4):
-            other = pl.ds(lax.rem(me + step, 16), 1)
+        for step in range(4):
+            other = pl.ds(lax.rem(me + 4 * chunk + step, 16), 1)
             chosen = ranks[other, :] == slots
             wanted.append(jnp.sum(jnp.where(chosen, relatives[other, :], 0.0), 1, keepdims=True))
         wanted = jnp.concatenate(wanted, 0).astype(jnp.int32)
@@ -469,14 +496,14 @@
         rows = lax.dot_general(
             one_hot, table[...], (((1,), (1,)), ((), ())), preferred_element_type=f32
         ).astype(bf16)
-        for index, step in enumerate(range(4 * chunk, 4 * chunk + 4)):
-            block = rows[SLOTS * index : SLOTS * (index + 1)]
-            if step == 0:
-                got[me] = block
-            else:
-                other = lax.rem(me + step, 16)
-                sent[step] = block
-                net.send(sent.at[step], got.at[me], f_sems, step - 1, other, "req")
+        sent[pl.ds(4 * chunk, 4)] = rows.reshape(4, SLOTS, rows.shape[1])
+        return 0
+
+    def send_picked():
+        got[me] = sent[0]
+        for step in range(1, 16):
+            other = lax.rem(me + step, 16)
+            net.send(sent.at[step], got.at[me], f_sems, step - 1, other, "req")
 
     def spread():
         for step in range(1, 16):
@@ -498,11 +525,14 @@
             net.arrived(mine.at[lax.rem(net.blk + 16 - step, 16)], g_sems, step - 1)
         fresh[...] = jnp.concatenate([mine[index, :, 0:columns] for index in range(16)], 1)
 
-    pick(0)
-    w_order = iter(
-        [w_peer_begin, lambda: w_mine_step(0), lambda: w_peer_step(0), lambda: w_mine_step(1),
-         lambda: w_peer_step(1), lambda: w_mine_step(2), lambda: w_peer_step(2)]
-    )
+    def first_qkv(request, _):
+        rows_f32 = jnp.transpose(tokens[request].astype(f32))
+        rows_out[request] = rows_f32.astype(bf16)
+        qkv[request] = project(rows_f32, w_qkv[...])
+        return 0
+
+    lax.fori_loop(0, 4, pick, 0)
+    send_picked()
     for g in PIECES:
         send(own.at[g], out.at[g, me], TWIN + g, twin)
 
@@ -536,24 +566,26 @@
         share(0, 1, g)
         from_below(g, 0, U0, UF0)
         from_above(g, 0, D0, DF0)
-        next(w_order)()
+        if g == PIECES[0]:
+            w_begin()
+        else:
+            w_step(PIECES.index(g) - 1)
         if g == PIECES[-1]:
             spread()
-        else:
-            pick(PIECES.index(g) + 1)
     for g in PIECES:
         from_far(g, 0)
         from_below(g, 1, U1, UF1)
         from_above(g, 1, D1, DF1)
-        next(w_order, lambda: None)()
+        if g == PIECES[0]:
+            w_step(3)
+            lax.fori_loop(0, 2, first_qkv, 0)
     for g in PIECES:
         from_far(g, 1)
     for (step, other_x), place in places.items():
         for g in PIECES:
             arrived(out.at[g, device(step, other_x, True)], TWIN + 4 * place + g)
-    w_mine_step(3)
-    w_peer_step(3)
     join()
+    w_end()
     for keep in keeps:
         keep.wait()
     for copy in started:
@@ -561,40 +593,45 @@
     net.finish()
 
 
-def start_gathers(own, w_own, ids, table, vocab_dev, columns, collective_id):
+def start_gathers(own, w_own, ids, table, tokens, w_qkv, collective_id):
     groups = own.shape[0]
     count = ids.shape[1]
+    columns, vocab_dev = table.shape
+    requests, width, rows = tokens.shape
     bf16 = jnp.bfloat16
-    anywhere = pl.BlockSpec(memory_space=pl.ANY)
     blocks = pltpu.VMEM((16, SLOTS, 128), bf16)
-    rows = pltpu.VMEM((16, count // 16, 128), bf16)
+    asked = pltpu.VMEM((16, count // 16, 128), bf16)
     return pl.pallas_call(
-        functools.partial(start_kernel, vocab_dev=vocab_dev, columns=columns),
+        start_kernel,
         out_shape=(
             jax.ShapeDtypeStruct((groups, 16) + own.shape[1:], own.dtype),
             jax.ShapeDtypeStruct((8, 2) + w_own.shape, w_own.dtype),
             jax.ShapeDtypeStruct((count // 16, 16 * columns), bf16),
+            jax.ShapeDtypeStruct((requests, rows, width), bf16),
+            jax.ShapeDtypeStruct((requests, rows, 256), bf16),
         ),
-        in_specs=[anywhere, anywhere] + whole(2),
-        out_specs=(anywhere, anywhere, whole(1)[0]),
+        in_specs=[pl.BlockSpec(memory_space=pl.ANY)] * 2 + whole(4),
+        out_specs=(pl.BlockSpec(memory_space=pl.ANY),) * 2 + tuple(whole(3)),
         scratch_shapes=[
+            pltpu.VMEM((128, -(-vocab_dev // 128) * 128), bf16),
             pltpu.VMEM((16, count), jnp.float32),
             pltpu.VMEM((16, count), jnp.float32),
             blocks,
             blocks,
-            rows,
-            rows,
+            asked,
+            asked,
             pltpu.SemaphoreType.DMA((2,)),
         ]
         + sem_pair(60)
-        + sem_pair(15)
+        + sem_pair(31)
         + sem_pair(15)
         + sem_pair(15),
         compiler_params=pltpu.CompilerParams(
-            collective_id=collective_id, has_side_effects=True, vmem_limit_bytes=56 << 20
+            collective_id=collective_id, has_side_effects=True, vmem_limit_bytes=40 << 20
         ),
+        cost_estimate=busy(45),
         name="start_gathers",
-    )(own, w_own, ids, table)
+    )(own, w_own, ids, table, tokens, w_qkv)
 
 
 def asked_rows(new_ids):
@@ -614,7 +651,10 @@
         here = (relative >= 0) & (relative < vocab_dev)
         looked = jnp.take(embed_table, jnp.clip(relative, 0, vocab_dev - 1), axis=0)
         looked = jnp.where(here[:, None], looked, jnp.zeros((), jnp.bfloat16))
-        summed = lax.psum_scatter(looked, "req", scatter_dimension=0, tiled=True)
+        looked = lax.all_to_all(
+            looked.reshape(16, -1, looked.shape[1]), "req", split_axis=0, concat_axis=0, tiled=True
+        )
+        summed = jnp.sum(looked.astype(jnp.float32), 0).astype(jnp.bfloat16)
         summed = summed.reshape(16, -1, summed.shape[1])
         mine = lax.all_to_all(summed, "blk", split_axis=0, concat_axis=0, tiled=True)
         return jnp.transpose(mine, (1, 0, 2)).reshape(quick.shape)
@@ -622,15 +662,9 @@
     return lax.cond(crowded, dense, lambda: quick)
 
 
-def attend_kernel(groups, lengths, rows_or_qkv, *refs, span, first):
-    if first:
-        weights, cache, out = refs
-        qkv = project(rows_or_qkv[0].astype(jnp.float32), weights[...])
-    else:
-        cache, out = refs
-        qkv = rows_or_qkv[0]
+def attend_kernel(groups, lengths, qkv, cache, out, *, span):
     length = lengths[pl.program_id(0)]
-    q, own_block = qkv[:, 0:128], qkv[:, 128:256]
+    q, own_block = qkv[0, :, 0:128], qkv[0, :, 128:256]
     f32 = jnp.float32
 
     def scores_of(keys):
@@ -644,22 +678,16 @@
     weights = jnp.exp(scores - top)
     total = jnp.sum(weights, -1, keepdims=True)
     mixed = weigh(weights, own_block)
-
-    def visit(index, carried):
-        top, total, mixed = carried
-        start = pl.multiple_of(index * span, span)
-        block = cache[0, pl.ds(start, span), :]
+    for start in range(0, cache.shape[1], span):
+        block = cache[0, start : start + span, :]
         position = start + lax.broadcasted_iota(jnp.int32, (1, span), 1)
-        bias = jnp.where(position < length, 0.0, NEG).astype(f32)
-        scores = scores_of(block) + bias
+        scores = scores_of(block) + jnp.where(position < length, 0.0, NEG).astype(f32)
         raised = jnp.maximum(top, jnp.max(scores, -1, keepdims=True))
         shrink = jnp.exp(top - raised)
         weights = jnp.exp(scores - raised)
         total = total * shrink + jnp.sum(weights, -1, keepdims=True)
-        return raised, total, mixed * shrink + weigh(weights, block)
-
-    blocks = (length + span - 1) // span
-    top, total, mixed = lax.fori_loop(0, blocks, visit, (top, total, mixed))
+        mixed = mixed * shrink + weigh(weights, block)
+        top = raised
     head = mixed / total
     parity = lax.axis_index("blk") % 2
     lane = lax.broadcasted_iota(jnp.int32, (1, 128), 1)
@@ -667,28 +695,25 @@
     out[0] = jnp.where(lane // 64 == parity, moved, 0.0).astype(out.dtype)
 
 
-def attend(rows_or_qkv, weights, cache, groups, lengths):
-    requests, rows, width = rows_or_qkv.shape
+def attend(qkv, cache, groups, lengths):
+    requests, rows, width = qkv.shape
     size = cache.shape[1]
-    first = weights is not None
-    in_specs = [pl.BlockSpec((1, rows, width), lambda r, g, n: (r, 0, 0))]
-    operands = (rows_or_qkv,)
-    if first:
-        in_specs.append(pl.BlockSpec(weights.shape, lambda r, g, n: (0, 0)))
-        operands = operands + (weights,)
-    in_specs.append(pl.BlockSpec((1, size, 128), lambda r, g, n: (g[r], 0, 0)))
     return pl.pallas_call(
-        functools.partial(attend_kernel, span=1024, first=first),
+        functools.partial(attend_kernel, span=min(2048, size)),
         out_shape=jax.ShapeDtypeStruct((requests, rows, 128), jnp.bfloat16),
         grid_spec=pltpu.PrefetchScalarGridSpec(
             num_scalar_prefetch=2,
             grid=(requests,),
-            in_specs=in_specs,
+            in_specs=[
+                pl.BlockSpec((1, rows, width), lambda r, g, n: (r, 0, 0)),
+                pl.BlockSpec((1, size, 128), lambda r, g, n: (g[r], 0, 0)),
+            ],
             out_specs=pl.BlockSpec((1, rows, 128), lambda r, g, n: (r, 0, 0)),
         ),
         compiler_params=pltpu.CompilerParams(vmem_limit_bytes=58 << 20),
+        cost_estimate=busy(11),
         name="attend",
-    )(groups, lengths, *operands, cache)
+    )(groups, lengths, qkv, cache)
 
 
 def shards(
@@ -703,38 +728,30 @@
     share = rows // 8
     my_groups = lax.dynamic_slice_in_dim(group_ids, req_index * requests, requests)
     lengths = jnp.take(cache_len, my_groups)
-    w_qkv = w_qkv[:, 0, :]
-    w_own = jnp.concatenate(
-        [w_qkv[:, :head_dim], jnp.zeros_like(w_qkv[:, :head_dim]), w_qkv[:, head_dim:]], 1
-    )
+    w_own = jnp.transpose(w_qkv[:, 0, :])
     w_fc = jnp.transpose(w_fc)
-    ids = asked_rows(new_ids)
-    vocab_dev, columns = embed_table.shape
-    table = jnp.pad(jnp.transpose(embed_table), ((0, 128 - columns), (0, -vocab_dev % 128)))
-    every_cache, w_out_all, fresh = start_gathers(
-        cache_kv[:, :, 0, :], w_out[0], ids, table, vocab_dev, columns, 1
-    )
-    every_cache = every_cache.reshape(cache_kv.shape[0], -1, kv_width)
-    w_out_all = w_out_all.reshape(16 * head_dim, width)
     pairs = [(index, index ^ 1) for index in range(16)]
     hidden = w_fc.shape[0] // 2
     halves = jnp.stack(
         [lax.dynamic_slice_in_dim(weights, core * hidden, hidden, 0) for weights in (w_fc, w_proj)]
     )
-    halves, w_sent, fresh = lax.optimization_barrier((halves, w_own, fresh))
     others = lax.ppermute(halves, "blk", pairs)
-    w_other = lax.ppermute(w_sent, "blk", pairs)
+    w_other = lax.ppermute(w_own, "blk", pairs)
+    ids = asked_rows(new_ids)
+    every_cache, all_w_out, fresh, current, qkv = start_gathers(
+        cache_kv[:, :, 0, :], w_out.reshape(2, head_dim // 2, width), ids, jnp.transpose(embed_table), jnp.transpose(tokens, (0, 2, 1)), w_own, 1
+    )
+    all_w_out = all_w_out.reshape(16 * head_dim, width)
+    every_cache = every_cache.reshape(cache_kv.shape[0], -1, kv_width)
+    others, w_other, fresh = lax.optimization_barrier((others, w_other, fresh))
+    twins = lax.ppermute(others, "req", pairs)
+    weights = (all_w_out, w_fc, w_proj, others, twins)
 
     my_accept = lax.dynamic_index_in_dim(accept, x, 1, keepdims=False)
     my_accept = lax.dynamic_slice_in_dim(my_accept, z * share, share, 1)[..., None]
-
-    heads = attend(tokens, w_own, every_cache, my_groups, lengths)
-    heads, others = lax.optimization_barrier((heads, others))
-    twins = lax.ppermute(others, "req", pairs)
-    weights = (w_out_all, w_fc, w_proj, others, twins)
+    heads = attend(qkv, every_cache, my_groups, lengths)
     every_head = gather_heads(heads, 2)
     fresh = settle_fresh(fresh, ids, embed_table, req_index).reshape(PASSES, share, width)
-    current = tokens
     for pass_index in range(PASSES):
         last = pass_index == PASSES - 1
         grown, my_middle = mlp(every_head, current, weights)
@@ -749,8 +766,8 @@
         if last:
             return done[0].reshape(requests, rows, width)
         current = done[0].reshape(rows, width)
-        heads = attend(done[1], None, every_cache, my_groups, lengths)
-        every_head = gather_heads(heads, 4 + 2 * pass_index)
+        heads = attend(done[1], every_cache, my_groups, lengths)
+        every_head = gather_heads(heads, 2)
 
 
 def solution(mesh):

time: 294 us -> 262 us (0.89)
  between operations: 14.3 us -> 0.84 us
  waiting for transfers between devices: 10.9 us -> 0.01 us
  Pallas kernels: 236 us -> 232 us
    ppermute x1, waiting for transfers between devices: 10.9 us -> 0.01 us  [shards(): others = lax.ppermute(halves, 'blk', pairs)]
    pallas_call x2, Pallas kernels: 47.3 us -> 37.7 us  [gather_heads(): pl.pallas_call(heads_kernel, out_shape=jax.ShapeDtypeStruct((8, rows, lan...]
    pallas_call x3, Pallas kernels: 102 us -> 107 us  [the longest x1 85.6 us: start_gathers(): pl.pallas_call(start_kernel, out_shape=(jax.ShapeDtypeStruct((groups, 16)...]
    slice x2 -> x0, local copies, waits for them, and re-layouts: 4.1 us -> none  [the longest x1 2.2 us: shards(): w_qkv[:, head_dim:]]
    unnamed x42 -> x44, local copies, waits for them, and re-layouts: 11.7 us -> 14.9 us
  transfers between devices with their start and end apart: 3 -> 3, of which waited for: 1 -> 0; matrix products, arithmetic and copies ran while one was open for 3% -> 3% of each run, Pallas kernels for 18% -> 45%
where the time goes in v5:
time: 262 us; the launch traced here: 261 us
  Pallas kernels  232 us (89%)
  local copies, waits for them, and re-layouts  22.2 us (8%)
  other arithmetic  2.96 us (1%)
  starting transfers between devices  2.93 us (1%)
    pallas_call x1, Pallas kernels, start_gathers(): pl.pallas_call(start_kernel, out_shape=(jax.ShapeDtypeStruct((groups, 16)...  85.6 us
    pallas_call x2, Pallas kernels, reduce_blk(): pl.pallas_call(functools.partial(reduce_kernel, last=last), out_shape=sha...  73.6 us
    pallas_call x2, Pallas kernels, gather_heads(): pl.pallas_call(heads_kernel, out_shape=jax.ShapeDtypeStruct((8, rows, lan...  37.7 us
    pallas_call x2, Pallas kernels, attend(): pl.pallas_call(functools.partial(attend_kernel, span=min(2048, size)), ou...  21.6 us
    unnamed x44, local copies, waits for them, and re-layouts  14.9 us
    pallas_call x2, Pallas kernels, mlp(): pl.pallas_call(mlp_kernel, out_shape=(jax.ShapeDtypeStruct((rows, width),...  13.4 us
  transfers between devices with their start and end apart: 3, of which 0 were waited for; matrix products, arithmetic and copies ran while one was open for 3% of the time, Pallas kernels for 45%

profile of v5, /device:TPU:12, one launch (start us, length us, event | category | flops | bytes accessed | tf_op | source)
XLA Modules:
  0.0 260.9 jit_solution(3665701324120992950)
XLA Ops:
  0.0 1.2 collective-permute-start.1
  1.2 1.1 dynamic-slice_bitcast_fusion.1
  2.4 1.2 pad_maximum_fusion
  5.2 1.4 copy-done.10
  6.6 1.1 copy-done.11
  7.7 1.0 copy-done.13
  8.7 0.9 copy-done.14
  9.6 85.6 %start_gathers.1 = (bf16[4,16,512,128]{3,2,1,0:T(8,128)(2,1)}, bf16[8,2,2,32,1600]{4,3,2,1,0:T(8,128)(2,1)S(1)}, bf16[64,1600]{1,0:T(8,128)(2,1)}, bf16[2,256,16...) custom-call(bf16[4,512,128]{2,1,0:T(8,128)(2,1)S(1)} %bitcast.48, bf16[2,32,1600]{2,1,0:T(8,128)(2,1)S(1)} %bitcast.49, ...), custom_call_target="tpu_custom_call" | custom-call | flops 17999998976 | bytes 135000000 | tf_op jit(solution)/shard_map/start_gathers/pallas_call | solution.py:604
  95.2 1.2 copy-done.6
  102.0 10.7 %attend.2.heads = bf16[2,256,128]{2,1,0:T(8,128)(2,1)} custom-call(s32[2]{0:T(128)} %copy-done.21, s32[2]{0:T(128)} %and_select_fusion.lengths, bf16[2,256,256]{2,1,0:T(8,128)(2,1)} %copy-done.15, bf16[4,8192,128]{2,1,0:T(8,128)(2,1)} %bitcast.58), custom_call_target="tpu_custom_call" | custom-call | flops 4400000000 | bytes 33000000 | tf_op jit(solution)/shard_map/attend/pallas_call | solution.py:701
  113.6 19.9 %gather_heads.2.every_head = bf16[8,256,128]{2,1,0:T(8,128)(2,1)S(1)} custom-call(bf16[2,256,128]{2,1,0:T(8,128)(2,1)S(1)} %copy-done.18), custom_call_target="tpu_custom_call" | custom-call | flops 6000000000 | bytes 45000000 | tf_op jit(solution)/shard_map/gather_heads/pallas_call | solution.py:120
  134.4 1.6 conditional.1
  134.4 1.6 fusion.2
  136.0 1.3 copy-done.1
  137.3 1.3 copy-done.4
  138.7 1.5 copy-done.7
  140.1 1.0 copy-done.9
  141.2 6.7 %mlp.2 = (bf16[256,1600]{1,0:T(8,128)(2,1)S(1)}, f32[32,1600]{1,0:T(8,128)S(1)}) custom-call(bf16[8,256,128]{2,1,0:T(8,128)(2,1)S(1)} %copy-done.9, bf16[2,256,1600]{2,1,0:T(8,128)(2,1)S(1)} %copy-done.7, bf16[1024,1600]{1,0:T(8,128)(2,1)S(1)} %bitcast.36, bf16[400,1600]{1,0:T(8,128)(2,1)S(1)} %bitcast.38, bf16[400,1600]{1,0:T(8,128)(2,1)S(1)} %copy-done.4, ...), custom_call_target="tpu_custom_call" | custom-call | flops 2400000000 | bytes 18000000 | tf_op jit(solution)/shard_map/mlp/pallas_call | solution.py:161
  147.9 37.3 %reduce_blk_3.1 = (bf16[8,32,1600]{2,1,0:T(8,128)(2,1)S(1)}, bf16[2,256,256]{2,1,0:T(8,128)(2,1)S(1)}) custom-call(bf16[8,32,1600]{2,1,0:T(8,128)(2,1)S(1)} %bitcast.44, f32[32,1600]{1,0:T(8,128)S(1)} %get-tuple-element.42.middle, bf16[32,1600]{1,0:T(8,128)(2,1)} %get-tuple-element.44.fresh, s32[32,1]{1,0:T(8,128)S(1)} %copy.56.accept, ...), custom_call_target="tpu_custom_call" | custom-call | flops 12000000000 | bytes 90000000 | tf_op jit(solution)/shard_map/reduce_blk_3/pallas_call | solution.py:276
  185.9 10.9 %attend.3.heads = bf16[2,256,128]{2,1,0:T(8,128)(2,1)} custom-call(s32[2]{0:T(128)} %copy-done.21, s32[2]{0:T(128)} %and_select_fusion.lengths, bf16[2,256,256]{2,1,0:T(8,128)(2,1)} %copy-done.16, bf16[4,8192,128]{2,1,0:T(8,128)(2,1)} %bitcast.59), custom_call_target="tpu_custom_call" | custom-call | flops 4400000000 | bytes 33000000 | tf_op jit(solution)/shard_map/attend/pallas_call | solution.py:701
  197.8 17.8 %gather_heads.3.every_head = bf16[8,256,128]{2,1,0:T(8,128)(2,1)S(1)} custom-call(bf16[2,256,128]{2,1,0:T(8,128)(2,1)S(1)} %copy-done.17), custom_call_target="tpu_custom_call" | custom-call | flops 6000000000 | bytes 45000000 | tf_op jit(solution)/shard_map/gather_heads/pallas_call | solution.py:120
  215.6 6.7 %mlp.3 = (bf16[256,1600]{1,0:T(8,128)(2,1)S(1)}, f32[32,1600]{1,0:T(8,128)S(1)}) custom-call(bf16[8,256,128]{2,1,0:T(8,128)(2,1)S(1)} %gather_heads.3.every_head, bf16[256,1600]{1,0:T(8,128)(2,1)S(1)} %bitcast.41, bf16[1024,1600]{1,0:T(8,128)(2,1)S(1)} %bitcast.37, bf16[400,1600]{1,0:T(8,128)(2,1)S(1)} %bitcast.39, bf16[400,1600]{1,0:T(8,128)(2,1)S(1)} %copy-done.5, ...), custom_call_target="tpu_custom_call" | custom-call | flops 2400000000 | bytes 18000000 | tf_op jit(solution)/shard_map/mlp/pallas_call | solution.py:161
  222.3 36.3 %reduce_blk_5.1 = bf16[2,8,32,1600]{3,2,1,0:T(8,128)(2,1)S(1)} custom-call(bf16[8,32,1600]{2,1,0:T(8,128)(2,1)S(1)} %bitcast.43, f32[32,1600]{1,0:T(8,128)S(1)} %get-tuple-element.49.middle, bf16[32,1600]{1,0:T(8,128)(2,1)} %get-tuple-element.50.fresh, s32[32,1]{1,0:T(8,128)S(1)} %copy.57.accept), custom_call_target="tpu_custom_call" | custom-call | flops 12000000000 | bytes 90000000 | tf_op jit(solution)/shard_map/reduce_blk_5/pallas_call | solution.py:276
  258.6 2.2 copy.58
  (54 shorter events, 9.9 us)
Async XLA Ops:
  0.0 100.8 %copy-start = (s32[4]{0:T(128)S(1)}, s32[4]{0:T(128)}, u32[]{:S(2)}) copy-start(s32[4]{0:T(128)} %param.21) | copy-start | bytes 52
  0.0 2.3 copy-start.3
  0.0 99.9 %collective-permute-start.1 = (bf16[192,1600]{1,0:T(8,128)(2,1)}, bf16[192,1600]{1,0:T(8,128)(2,1)}, u32[]{:S(2)}, u32[]{:S(2)}) collective-permute-start(bf16[192,1600]{1,0:T(8,128)(2,1)} %bitcast.45), channel_id=1, source_target_pairs={{0,1},{1,0},{2,3},{3,2},{4,5},{5,4},{6,7},{7,6},{8,9},{9,8},{10,11... | collective-permute-start | bytes 1843208 | tf_op jit(solution)/shard_map/ppermute | solution.py:739
  2.4 2.1 copy-start.19
  3.7 96.2 %collective-permute-start = (bf16[2,200,1600]{2,1,0:T(8,128)(2,1)}, bf16[2,200,1600]{2,1,0:T(8,128)(2,1)}, u32[]{:S(2)}, u32[]{:S(2)}) collective-permute-start(bf16[2,200,1600]{2,1,0:T(8,128)(2,1)} %pad_maximum_fusion), channel_id=1, source_target_pairs={{0,1},{1,0},{2,3},{3,2},{4,5},{5,4},{6,7},{7,6},{8,9},{9,8},{10,11... | collective-permute-start | bytes 3840008 | tf_op jit(solution)/shard_map/ppermute | solution.py:738
  5.2 1.4 copy-start.10
  6.6 1.1 copy-start.11
  7.7 1.0 copy-start.13
  8.7 0.9 copy-start.14
  9.6 90.2 %copy-start.20 = (s32[32]{0:T(128)S(1)}, s32[32]{0:T(128)}, u32[]{:S(2)}) copy-start(s32[32]{0:T(128)} %param.20) | copy-start | bytes 388
  95.2 1.2 copy-start.6
  96.4 0.7 copy-start.15
  99.9 2.1 copy-start.21
  99.9 36.1 %collective-permute-start.2 = (bf16[2,200,1600]{2,1,0:T(8,128)(2,1)}, bf16[2,200,1600]{2,1,0:T(8,128)(2,1)}, u32[]{:S(2)}, u32[]{:S(2)}) collective-permute-start(bf16[2,200,1600]{2,1,0:T(8,128)(2,1)} %collective-permute-done.others), channel_id=1, source_target_pairs={{0,16},{16,0},{32,48},{48,32},{64,80},{80,64},{96,112},{112,96},{1... | collective-permute-start | bytes 3840008 | tf_op jit(solution)/shard_map/ppermute | solution.py:747
  112.7 0.9 copy-start.18
  133.5 0.8 copy-start.8
  136.0 1.3 copy-start.1
  137.3 1.3 copy-start.4
  138.7 1.5 copy-start.7
  140.1 1.0 copy-start.9
  141.2 6.8 %copy-start.12 = (bf16[1600,1,192]{0,2,1:T(8,128)(2,1)S(1)}, bf16[1600,1,192]{0,2,1:T(8,128)(2,1)}, u32[]{:S(2)}) copy-start(bf16[1600,1,192]{0,2,1:T(8,128)(2,1)} %param.15) | copy-start | bytes 1843204
  196.9 0.9 copy-start.17
  197.8 17.8 %copy-start.2 = (bf16[1600,400]{0,1:T(8,128)(2,1)S(1)}, bf16[1600,400]{0,1:T(8,128)(2,1)}, u32[]{:S(2)}) copy-start(bf16[1600,400]{0,1:T(8,128)(2,1)} %param.17) | copy-start | bytes 3840004
  197.8 17.8 %copy-start.5 = (bf16[400,1600]{1,0:T(8,128)(2,1)S(1)}, bf16[400,1600]{1,0:T(8,128)(2,1)}, u32[]{:S(2)}) copy-start(bf16[400,1600]{1,0:T(8,128)(2,1)} %w_proj.3) | copy-start | bytes 3840004
  (1 other events, 0.7 us)

commit v6 on v5

--- a/solution.py
+++ b/solution.py
@@ -99,11 +99,8 @@
             take(step, False, RING_C + step - 1, step == 3, net.left)
 
 
-def heads_kernel(heads, out, peer, *sem_refs):
-    net = Net()
-    ring_sems, pair_sems = tuple(sem_refs[0:2]), tuple(sem_refs[2:4])
+def swap_heads(net, heads, peer, out, ring_sems, pair_sems):
     half = heads.shape[1] // 2
-    net.greet()
     parts = (slice(0, half), slice(half, 2 * half))
     for part, rows in enumerate(parts):
         net.send(heads.at[1 - net.x, rows], peer.at[rows], pair_sems, part, net.pair)
@@ -112,68 +109,25 @@
         out[net.z, rows] = heads[net.x, rows] + peer[rows]
         ring_begin(net, out, ring_sems, half, part == 1)
     ring_rest(net, out, ring_sems, half)
-    net.finish()
-
-
-def gather_heads(heads, collective_id):
-    _, rows, lanes = heads.shape
-    return pl.pallas_call(
-        heads_kernel,
-        out_shape=jax.ShapeDtypeStruct((8, rows, lanes), heads.dtype),
-        in_specs=whole(1),
-        out_specs=whole(1)[0],
-        scratch_shapes=[pltpu.VMEM((rows, lanes), heads.dtype)] + sem_pair(RING_SLOTS) + sem_pair(2),
-        compiler_params=pltpu.CompilerParams(
-            collective_id=collective_id, has_side_effects=True, vmem_limit_bytes=16 << 20
-        ),
-        cost_estimate=busy(15),
-        name="gather_heads",
-    )(heads)
-
-
-def mlp_kernel(
-    every_head, current, w_out, w_fc, w_proj, others, twins, grown, my_middle, head_rows, middle
-):
+
+
+def mlp(net, every_head, current, w_out, w_mlp, w_mlp_pair, head_rows, middle):
     f32, bf16 = jnp.float32, jnp.bfloat16
-    blk = lax.axis_index("blk")
     for z in range(8):
         head_rows[:, 128 * z : 128 * (z + 1)] = every_head[z]
-    rows = current[blk % 2] if len(current.shape) == 3 else current[...]
-    middle[...] = rows.astype(f32) + jnp.dot(
+    middle[...] = current[...].astype(f32) + jnp.dot(
         head_rows[...], w_out[...], preferred_element_type=f32
     )
-    share = my_middle.shape[0]
-    my_middle[...] = middle[pl.ds(pl.multiple_of(blk // 2 * share, share), share), :]
     normed = layer_norm(middle[...]).astype(bf16)
 
-    def term(enter, leave):
-        raw = lax.dot_general(normed, enter, (((1,), (1,)), ((), ())), preferred_element_type=f32)
+    def term(weights):
+        raw = lax.dot_general(
+            normed, weights[0], (((1,), (1,)), ((), ())), preferred_element_type=f32
+        )
         rows = jax.nn.gelu(raw, approximate=True).astype(bf16)
-        return jnp.dot(rows, leave, preferred_element_type=f32)
-
-    total = term(w_fc[...], w_proj[...])
-    total = total + term(others[0], others[1]) + term(twins[0], twins[1])
-    grown[...] = total.astype(bf16)
-
-
-def mlp(every_head, current, weights):
-    rows, width = current.shape[-2:]
-    return pl.pallas_call(
-        mlp_kernel,
-        out_shape=(
-            jax.ShapeDtypeStruct((rows, width), jnp.bfloat16),
-            jax.ShapeDtypeStruct((rows // 8, width), jnp.float32),
-        ),
-        in_specs=whole(2 + len(weights)),
-        out_specs=tuple(whole(2)),
-        scratch_shapes=[
-            pltpu.VMEM((rows, 8 * every_head.shape[2]), jnp.bfloat16),
-            pltpu.VMEM((rows, width), jnp.float32),
-        ],
-        compiler_params=pltpu.CompilerParams(vmem_limit_bytes=28 << 20),
-        cost_estimate=busy(6),
-        name="mlp",
-    )(every_head, current, *weights)
+        return jnp.dot(rows, weights[1], preferred_element_type=f32)
+
+    return (term(w_mlp) + term(w_mlp_pair)).astype(bf16)
 
 
 def project(rows_f32, weights):
@@ -186,18 +140,37 @@
     return jnp.concatenate([queries, pltpu.roll(got, 192, 1)[:, 0:128]], 1).astype(bf16)
 
 
-def reduce_kernel(part, middle, fresh, accept, *refs, last):
+def pass_kernel(heads, fresh, accept, current_in, *refs, last):
+    net = Net()
+    current_in = current_in.at[net.x] if len(current_in.shape) == 3 else current_in
+    loads = 4 if last else 6
+    sources, refs = (current_in,) + tuple(refs[0 : loads - 1]), refs[loads - 1 :]
     if last:
         out, *refs = refs
     else:
-        w_own, w_pair, out, qkv, stage, *refs = refs
+        out, qkv, stage, *refs = refs
+    held, refs = refs[0:loads], refs[loads:]
+    load_sems, peer, every_head, head_rows, middle_all, part, *refs = refs
     right_low, right_high, left_low, left_high, *sem_refs = refs
-    net = Net()
-    sems, gather_sems = tuple(sem_refs[0:2]), tuple(sem_refs[2:4])
+    copies = [
+        pltpu.make_async_copy(source, place, load_sems.at[index])
+        for index, (source, place) in enumerate(zip(sources, held))
+    ]
+    current, w_out, w_mlp, w_mlp_pair = held[0:4]
+    sems, gather_sems, head_sems, pair_sems, swap_sems = (
+        tuple(sem_refs[index : index + 2]) for index in range(0, 10, 2)
+    )
     half = part.shape[1] // 2
     f32, bf16 = jnp.float32, jnp.bfloat16
     low, high = slice(0, half), slice(half, 2 * half)
+    for copy in copies:
+        copy.start()
     net.greet()
+    swap_heads(net, heads, peer, every_head, head_sems, pair_sems)
+    for copy in copies:
+        copy.wait()
+    grown = mlp(net, every_head, current, w_out, w_mlp, w_mlp_pair, head_rows, middle_all)
+    part[...] = grown.reshape(part.shape)
 
     def begin(buf, rows, slot, offset, target):
         net.send(part.at[net.ring(offset), rows], buf.at[0], sems, slot, target)
@@ -222,7 +195,8 @@
 
     def close(rows, from_left, from_right):
         total = part[net.z, rows].astype(f32) + from_left.astype(f32) + from_right.astype(f32)
-        layer_out = (middle[rows] + total).astype(bf16)
+        start = pl.multiple_of(net.z * 2 * half + rows.start, half)
+        layer_out = (middle_all[pl.ds(start, half), :] + total).astype(bf16)
         return jnp.where(accept[rows] == 1, fresh[rows], layer_out)
 
     net.arrived(left_low.at[2], sems, RING_C + 2)
@@ -245,8 +219,8 @@
         out[net.z, high] = result
         ring_begin(net, out, gather_sems, half, True)
         ring_rest(net, out, gather_sems, half)
-        swap_sems = tuple(sem_refs[4:6])
         rows_f32 = out[...].reshape(8 * 2 * half, out.shape[2]).astype(f32)
+        w_own, w_pair = held[4:6]
         stage[...] = project(rows_f32, w_pair[...])
         net.send(stage, qkv.at[net.x], swap_sems, 0, net.pair)
         qkv[net.x] = project(rows_f32, w_own[...])
@@ -254,36 +228,46 @@
     net.finish()
 
 
-def reduce_blk(part, middle, fresh, accept, w_pair, collective_id):
-    blocks, rows, width = part.shape
+def run_pass(heads, current, w_out, w_mlp, w_mlp_pair, fresh, accept, w_qkv_both, collective_id):
+    rows, width = current.shape[-2:]
+    lanes, share = heads.shape[2], rows // 8
     bf16 = jnp.bfloat16
-    last = w_pair is None
-    block = (rows // 2, width)
+    last = w_qkv_both is None
+    block = (share // 2, width)
+    operands = (heads, fresh, accept, current, w_out, w_mlp, w_mlp_pair)
+    if last:
+        shapes = (jax.ShapeDtypeStruct((2, 8, share, width), bf16),)
+        first, gather = [], GATHER_SLOTS
+    else:
+        operands = operands + w_qkv_both
+        shapes = (
+            jax.ShapeDtypeStruct((8, share, width), bf16),
+            jax.ShapeDtypeStruct((2, rows, 256), bf16),
+        )
+        first, gather = [pltpu.VMEM((rows, 256), bf16)], RING_SLOTS
+    held = [pltpu.VMEM(array.shape[-2:] if array is current else array.shape, bf16) for array in operands[3:]]
+    scratch = first + held + [pltpu.SemaphoreType.DMA((len(held),))] + [
+        pltpu.VMEM((rows, lanes), bf16),
+        pltpu.VMEM((8, rows, lanes), bf16),
+        pltpu.VMEM((rows, 8 * lanes), bf16),
+        pltpu.VMEM((rows, width), jnp.float32),
+        pltpu.VMEM((8, share, width), bf16),
+    ]
     rings = [pltpu.VMEM((count,) + block, bf16) for count in (4, 3, 3, 4)]
-    operands = (part, middle, fresh, accept)
-    if last:
-        shapes = (jax.ShapeDtypeStruct((2,) + part.shape, bf16),)
-        sems = sem_pair(RING_SLOTS) + sem_pair(GATHER_SLOTS)
-    else:
-        operands = operands + w_pair
-        columns = 256
-        shapes = (
-            jax.ShapeDtypeStruct(part.shape, bf16),
-            jax.ShapeDtypeStruct((2, blocks * rows, columns), bf16),
-        )
-        rings = [pltpu.VMEM((blocks * rows, columns), bf16)] + rings
-        sems = sem_pair(RING_SLOTS) + sem_pair(RING_SLOTS) + sem_pair(1)
+    sems = []
+    for count in (RING_SLOTS, gather, RING_SLOTS, 2, 1):
+        sems = sems + sem_pair(count)
     return pl.pallas_call(
-        functools.partial(reduce_kernel, last=last),
+        functools.partial(pass_kernel, last=last),
         out_shape=shapes,
-        in_specs=whole(len(operands)),
+        in_specs=whole(3) + [pl.BlockSpec(memory_space=pl.ANY)] * len(held),
         out_specs=tuple(whole(len(shapes))),
-        scratch_shapes=rings + sems,
+        scratch_shapes=scratch + rings + sems,
         compiler_params=pltpu.CompilerParams(
-            collective_id=collective_id, has_side_effects=True, vmem_limit_bytes=24 << 20
+            collective_id=collective_id, has_side_effects=True, vmem_limit_bytes=56 << 20
         ),
-        cost_estimate=busy(30),
-        name=f"reduce_blk_{collective_id}",
+        cost_estimate=busy(50),
+        name=f"pass_{collective_id}",
     )(*operands)
 
 
@@ -351,9 +335,9 @@
 
 
 def start_kernel(
-    own, w_own, ids, raw_table, tokens, w_qkv, out, w_all, fresh, rows_out, qkv,
-    table, ranks, relatives, sent, got, picked, mine, copy_sems,
-    send_sems, recv_sems, send_w, recv_w, send_f, recv_f, send_g, recv_g,
+    own, w_own, ids, raw_table, tokens_in, w_qkv_in, w_mlp, out, w_all, w_mlp_pair, w_qkv_pair, fresh, rows_out,
+    qkv, tokens, w_qkv, table, ranks, relatives, sent, got, picked, mine, copy_sems,
+    send_sems, recv_sems, send_w, recv_w, send_f, recv_f, send_g, recv_g, send_m, recv_m,
 ):
     net = Net()
     f32, bf16 = jnp.float32, jnp.bfloat16
@@ -375,8 +359,10 @@
     for step in range(1, 16):
         other = lax.rem(net.blk + step, 16)
         pl.semaphore_signal(barrier, inc=1, device_id={"blk": other}, device_id_type=MESH)
-    pl.semaphore_wait(barrier, 30)
-    w_sems, f_sems, g_sems = (send_w, recv_w), (send_f, recv_f), (send_g, recv_g)
+    cross = {"req": side, "blk": net.pair}
+    pl.semaphore_signal(barrier, inc=1, device_id=cross, device_id_type=MESH)
+    pl.semaphore_wait(barrier, 31)
+    w_sems, f_sems, g_sems, m_sems = (send_w, recv_w), (send_f, recv_f), (send_g, recv_g), (send_m, recv_m)
     columns, vocab_dev = raw_table.shape
     started = []
 
@@ -428,8 +414,44 @@
         pltpu.make_async_copy(own, out.at[:, me], copy_sems.at[0]),
         pltpu.make_async_copy(w_half, w_mine, copy_sems.at[1]),
     ]
-    for keep in keeps:
-        keep.start()
+    loads = [
+        pltpu.make_async_copy(tokens_in, tokens, copy_sems.at[2]),
+        pltpu.make_async_copy(w_qkv_in, w_qkv, copy_sems.at[3]),
+    ]
+    for copy in keeps + loads:
+        copy.start()
+
+    units, half_qkv = w_mlp.shape[1] // 5, w_qkv_pair.shape[0] // 2
+
+    def pair_pieces(which):
+        for index in range(5):
+            rows = pl.ds(index * units, units)
+            yield w_mlp.at[which, rows], w_mlp_pair.at[which, rows]
+        rows = pl.ds(pl.multiple_of(which * half_qkv, half_qkv), half_qkv)
+        yield w_qkv_in.at[rows], w_qkv_pair.at[rows]
+
+    def pair_send():
+        for slot, (src, dst) in enumerate(pair_pieces(core)):
+            where = {"blk": net.pair} if slot < 3 else cross
+            copy = pltpu.make_async_remote_copy(
+                src_ref=src,
+                dst_ref=dst,
+                send_sem=m_sems[0].at[slot],
+                recv_sem=m_sems[1].at[slot],
+                device_id=where,
+                device_id_type=MESH,
+            )
+            copy.start()
+            started.append(copy)
+
+    def pair_share():
+        for slot, (_, dst) in enumerate(pair_pieces(core)):
+            net.arrived(dst, m_sems, slot)
+            net.send(dst, dst, m_sems, 6 + slot, twin, "req")
+
+    def pair_end():
+        for slot, (_, dst) in enumerate(pair_pieces(1 - core)):
+            net.arrived(dst, m_sems, 6 + slot)
 
     def w_begin():
         piece = w_piece(0, 1 - net.x, core)
@@ -571,6 +593,7 @@
         else:
             w_step(PIECES.index(g) - 1)
         if g == PIECES[-1]:
+            pair_send()
             spread()
     for g in PIECES:
         from_far(g, 0)
@@ -578,14 +601,18 @@
         from_above(g, 1, D1, DF1)
         if g == PIECES[0]:
             w_step(3)
+            for load in loads:
+                load.wait()
             lax.fori_loop(0, 2, first_qkv, 0)
     for g in PIECES:
         from_far(g, 1)
     for (step, other_x), place in places.items():
         for g in PIECES:
             arrived(out.at[g, device(step, other_x, True)], TWIN + 4 * place + g)
+    pair_share()
     join()
     w_end()
+    pair_end()
     for keep in keeps:
         keep.wait()
     for copy in started:
@@ -593,7 +620,7 @@
     net.finish()
 
 
-def start_gathers(own, w_own, ids, table, tokens, w_qkv, collective_id):
+def start_gathers(own, w_own, ids, table, tokens, w_qkv, w_mlp, collective_id):
     groups = own.shape[0]
     count = ids.shape[1]
     columns, vocab_dev = table.shape
@@ -601,18 +628,23 @@
     bf16 = jnp.bfloat16
     blocks = pltpu.VMEM((16, SLOTS, 128), bf16)
     asked = pltpu.VMEM((16, count // 16, 128), bf16)
+    anywhere = [pl.BlockSpec(memory_space=pl.ANY)]
     return pl.pallas_call(
         start_kernel,
         out_shape=(
             jax.ShapeDtypeStruct((groups, 16) + own.shape[1:], own.dtype),
             jax.ShapeDtypeStruct((8, 2) + w_own.shape, w_own.dtype),
+            jax.ShapeDtypeStruct(w_mlp.shape, w_mlp.dtype),
+            jax.ShapeDtypeStruct(w_qkv.shape, w_qkv.dtype),
             jax.ShapeDtypeStruct((count // 16, 16 * columns), bf16),
             jax.ShapeDtypeStruct((requests, rows, width), bf16),
             jax.ShapeDtypeStruct((requests, rows, 256), bf16),
         ),
-        in_specs=[pl.BlockSpec(memory_space=pl.ANY)] * 2 + whole(4),
-        out_specs=(pl.BlockSpec(memory_space=pl.ANY),) * 2 + tuple(whole(3)),
+        in_specs=anywhere * 2 + whole(2) + anywhere * 3,
+        out_specs=tuple(anywhere * 4 + whole(3)),
         scratch_shapes=[
+            pltpu.VMEM(tokens.shape, bf16),
+            pltpu.VMEM(w_qkv.shape, bf16),
             pltpu.VMEM((128, -(-vocab_dev // 128) * 128), bf16),
             pltpu.VMEM((16, count), jnp.float32),
             pltpu.VMEM((16, count), jnp.float32),
@@ -620,18 +652,19 @@
             blocks,
             asked,
             asked,
-            pltpu.SemaphoreType.DMA((2,)),
+            pltpu.SemaphoreType.DMA((4,)),
         ]
         + sem_pair(60)
         + sem_pair(31)
         + sem_pair(15)
-        + sem_pair(15),
+        + sem_pair(15)
+        + sem_pair(12),
         compiler_params=pltpu.CompilerParams(
-            collective_id=collective_id, has_side_effects=True, vmem_limit_bytes=40 << 20
+            collective_id=collective_id, has_side_effects=True, vmem_limit_bytes=58 << 20
         ),
         cost_estimate=busy(45),
         name="start_gathers",
-    )(own, w_own, ids, table, tokens, w_qkv)
+    )(own, w_own, ids, table, tokens, w_qkv, w_mlp)
 
 
 def asked_rows(new_ids):
@@ -721,7 +754,7 @@
 ):
     req_index = lax.axis_index("req")
     blk_index = lax.axis_index("blk")
-    z, x, core = blk_index // 2, blk_index % 2, req_index % 2
+    z, x = blk_index // 2, blk_index % 2
     requests, rows, width = tokens.shape
     kv_width = cache_kv.shape[3]
     head_dim = kv_width // 2
@@ -729,45 +762,39 @@
     my_groups = lax.dynamic_slice_in_dim(group_ids, req_index * requests, requests)
     lengths = jnp.take(cache_len, my_groups)
     w_own = jnp.transpose(w_qkv[:, 0, :])
-    w_fc = jnp.transpose(w_fc)
-    pairs = [(index, index ^ 1) for index in range(16)]
-    hidden = w_fc.shape[0] // 2
-    halves = jnp.stack(
-        [lax.dynamic_slice_in_dim(weights, core * hidden, hidden, 0) for weights in (w_fc, w_proj)]
+    w_mlp = jnp.stack([jnp.transpose(w_fc), w_proj])
+    ids = asked_rows(new_ids)
+    every_cache, w_out_all, w_mlp_pair, w_other, fresh, current, qkv = start_gathers(
+        cache_kv[:, :, 0, :],
+        w_out.reshape(2, head_dim // 2, width),
+        ids,
+        jnp.transpose(embed_table),
+        jnp.transpose(tokens, (0, 2, 1)),
+        w_own,
+        w_mlp,
+        1,
     )
-    others = lax.ppermute(halves, "blk", pairs)
-    w_other = lax.ppermute(w_own, "blk", pairs)
-    ids = asked_rows(new_ids)
-    every_cache, all_w_out, fresh, current, qkv = start_gathers(
-        cache_kv[:, :, 0, :], w_out.reshape(2, head_dim // 2, width), ids, jnp.transpose(embed_table), jnp.transpose(tokens, (0, 2, 1)), w_own, 1
-    )
-    all_w_out = all_w_out.reshape(16 * head_dim, width)
+    w_out_all = w_out_all.reshape(16 * head_dim, width)
     every_cache = every_cache.reshape(cache_kv.shape[0], -1, kv_width)
-    others, w_other, fresh = lax.optimization_barrier((others, w_other, fresh))
-    twins = lax.ppermute(others, "req", pairs)
-    weights = (all_w_out, w_fc, w_proj, others, twins)
-
     my_accept = lax.dynamic_index_in_dim(accept, x, 1, keepdims=False)
     my_accept = lax.dynamic_slice_in_dim(my_accept, z * share, share, 1)[..., None]
-    heads = attend(qkv, every_cache, my_groups, lengths)
-    every_head = gather_heads(heads, 2)
     fresh = settle_fresh(fresh, ids, embed_table, req_index).reshape(PASSES, share, width)
     for pass_index in range(PASSES):
         last = pass_index == PASSES - 1
-        grown, my_middle = mlp(every_head, current, weights)
-        done = reduce_blk(
-            grown.reshape(8, share, width),
-            my_middle,
+        done = run_pass(
+            attend(qkv, every_cache, my_groups, lengths),
+            current,
+            w_out_all,
+            w_mlp,
+            w_mlp_pair,
             fresh[pass_index],
             my_accept[pass_index],
             None if last else (w_own, w_other),
-            3 + 2 * pass_index,
+            2 + pass_index,
         )
         if last:
             return done[0].reshape(requests, rows, width)
-        current = done[0].reshape(rows, width)
-        heads = attend(done[1], every_cache, my_groups, lengths)
-        every_head = gather_heads(heads, 2)
+        current, qkv = done[0].reshape(rows, width), done[1]
 
 
 def solution(mesh):

time: 262 us -> 220 us (0.84)
  Pallas kernels: 232 us -> 201 us
  local copies, waits for them, and re-layouts: 22.2 us -> 9.5 us
  starting transfers between devices: 2.93 us -> 0 us
  other arithmetic: 2.96 us -> 5.59 us
    pallas_call x1, Pallas kernels: 85.6 us -> 63.3 us  [start_gathers(): pl.pallas_call(start_kernel, out_shape=(jax.ShapeDtypeStruct((groups, 16)...]
    unnamed x44 -> x8, local copies, waits for them, and re-layouts: 14.9 us -> 0.02 us
    pallas_call x6 -> x2, Pallas kernels: 125 us -> 116 us  [run_pass(): pl.pallas_call(functools.partial(pass_kernel, last=last), out_shape=shape...]
    ppermute x3 -> x0, starting transfers between devices: 2.93 us -> none  [the longest x1 1.2 us: shards(): w_other = lax.ppermute(w_own, 'blk', pairs)]
  transfers between devices with their start and end apart: 3 -> 0, of which waited for: 0 -> 0; matrix products, arithmetic and copies ran while one was open for 3% -> 0% of each run, Pallas kernels for 45% -> 0%
where the time goes in v6:
time: 220 us; the launch traced here: 217 us
  Pallas kernels  201 us (91%)
  local copies, waits for them, and re-layouts  9.5 us (4%)
  other arithmetic  5.59 us (3%)
    pallas_call x2, Pallas kernels, run_pass(): pl.pallas_call(functools.partial(pass_kernel, last=last), out_shape=shape...  116 us
    pallas_call x1, Pallas kernels, start_gathers(): pl.pallas_call(start_kernel, out_shape=(jax.ShapeDtypeStruct((groups, 16)...  63.3 us
    pallas_call x2, Pallas kernels, attend(): pl.pallas_call(functools.partial(attend_kernel, span=min(2048, size)), ou...  21.6 us

profile of v6, /device:TPU:12, one launch (start us, length us, event | category | flops | bytes accessed | tf_op | source)
XLA Modules:
  0.0 216.8 jit_solution(16769929778093316046)
XLA Ops:
  0.0 0.0 copy-start
  0.0 0.8 compare_select_fusion.2
  0.9 0.0 copy-done
  0.9 0.6 gather_fusion.1
  1.5 0.5 and_select_fusion.lengths
  2.0 0.9 reshape.112
  3.0 0.2 copy.61
  3.2 0.3 reshape.113.ids
  3.5 0.0 copy-done.1
  3.5 3.2 %pad_maximum_fusion.w_mlp.refs_1_ = bf16[2,400,1600]{2,1,0:T(8,128)(2,1)} fusion(bf16[1,400,1600]{2,1,0:T(8,128)(2,1)S(1)} %bitcast.35, bf16[1,400,1600]{2,1,0:T(8,128)(2,1)} %bitcast.36), kind=kLoop, calls=%fused_computation.9 | loop fusion | flops 1280000 | bytes 5120000 | tf_op jit(solution)/shard_map/stack | solution.py:765
  6.7 0.0 copy-done.2
  6.7 63.3 %start_gathers.1 = (bf16[4,16,512,128]{3,2,1,0:T(8,128)(2,1)}, bf16[8,2,2,32,1600]{4,3,2,1,0:T(8,128)(2,1)}, bf16[2,400,1600]{2,1,0:T(8,128)(2,1)}, bf16[192,160...) custom-call(bf16[4,512,128]{2,1,0:T(8,128)(2,1)} %bitcast.45, ...), custom_call_target="tpu_custom_call" | custom-call | flops 17999998976 | bytes 135000000 | tf_op jit(solution)/shard_map/start_gathers/pallas_call | solution.py:632
  70.1 10.7 %attend.2.heads = bf16[2,256,128]{2,1,0:T(8,128)(2,1)} custom-call(s32[2]{0:T(128)} %copy-done.3, s32[2]{0:T(128)} %and_select_fusion.lengths, bf16[2,256,256]{2,1,0:T(8,128)(2,1)} %get-tuple-element.30.qkv, bf16[4,8192,128]{2,1,0:T(8,128)(2,1)} %bitcast.47), custom_call_target="tpu_custom_call" | custom-call | flops 4400000000 | bytes 33000000 | tf_op jit(solution)/shard_map/attend/pallas_call | solution.py:734
  80.8 0.4 convert_reduce_fusion
  81.2 0.6 reduce_max.9
  82.5 1.6 conditional.1
  82.5 1.6 fusion.1
  84.1 0.8 dynamic-slice_bitcast_fusion
  84.9 0.7 copy.56.accept
  85.6 59.8 %pass_2.1 = (bf16[8,32,1600]{2,1,0:T(8,128)(2,1)}, bf16[2,256,256]{2,1,0:T(8,128)(2,1)}) custom-call(bf16[2,256,128]{2,1,0:T(8,128)(2,1)} %attend.2.heads, bf16[32,1600]{1,0:T(8,128)(2,1)S(1)} %get-tuple-element.33.fresh, s32[32,1]{1,0:T(8,128)} %copy.56.accept, bf16[2,256,1600]{2,1,0:T(8,128)(2,1)} %get-tuple-element.34.current_in, ...), custom_call_target="tpu_custom_call" | custom-call | flops 20000000000 | bytes 150000000 | tf_op jit(solution)/shard_map/pass_2/pallas_call | solution.py:260
  145.3 11.0 %attend.3.heads = bf16[2,256,128]{2,1,0:T(8,128)(2,1)} custom-call(s32[2]{0:T(128)} %copy-done.3, s32[2]{0:T(128)} %and_select_fusion.lengths, bf16[2,256,256]{2,1,0:T(8,128)(2,1)} %get-tuple-element.38.qkv, bf16[4,8192,128]{2,1,0:T(8,128)(2,1)} %bitcast.48), custom_call_target="tpu_custom_call" | custom-call | flops 4400000000 | bytes 33000000 | tf_op jit(solution)/shard_map/attend/pallas_call | solution.py:734
  156.3 0.7 copy.57.accept
  157.0 56.3 %pass_3.1 = bf16[2,8,32,1600]{3,2,1,0:T(8,128)(2,1)} custom-call(bf16[2,256,128]{2,1,0:T(8,128)(2,1)} %attend.3.heads, bf16[32,1600]{1,0:T(8,128)(2,1)} %get-tuple-element.39.fresh, s32[32,1]{1,0:T(8,128)} %copy.57.accept, bf16[256,1600]{1,0:T(8,128)(2,1)} %bitcast.51, bf16[1024,1600]{1,0:T(8,128)(2,1)} %bitcast.50, ...), custom_call_target="tpu_custom_call" | custom-call | flops 20000000000 | bytes 150000000 | tf_op jit(solution)/shard_map/pass_3/pallas_call | solution.py:260
  213.2 3.6 %copy.58 = bf16[2,256,1600]{1,2,0:T(8,128)(2,1)} copy(bf16[2,256,1600]{2,1,0:T(8,128)(2,1)} %bitcast.34) | data formatting | bytes 3276800 | tf_op jit(solution)/shard_map/reshape | solution.py:796
  (6 shorter events, 0.1 us)
Async XLA Ops:
  0.0 0.9 copy-start
  0.0 3.5 %copy-start.1 = (bf16[400,1600]{1,0:T(8,128)(2,1)S(1)}, bf16[400,1600]{1,0:T(8,128)(2,1)}, u32[]{:S(2)}) copy-start(bf16[400,1600]{1,0:T(8,128)(2,1)} %param.18) | copy-start | bytes 3840004
  0.8 5.9 %copy-start.3 = (s32[2]{0:T(128)}, s32[2]{0:T(128)S(1)}, u32[]{:S(2)}) copy-start(s32[2]{0:T(128)S(1)} %get-tuple-element.60.groups) | copy-start | bytes 28
  3.5 3.2 %copy-start.2 = (bf16[3141,100]{0,1:T(8,128)(2,1)S(1)}, bf16[3141,100]{0,1:T(8,128)(2,1)}, u32[]{:S(2)}) copy-start(bf16[3141,100]{0,1:T(8,128)(2,1)} %param.19) | copy-start | bytes 1884604

commit v7 on v6

--- a/solution.py
+++ b/solution.py
@@ -111,7 +111,7 @@
     ring_rest(net, out, ring_sems, half)
 
 
-def mlp(net, every_head, current, w_out, w_mlp, w_mlp_pair, head_rows, middle):
+def mlp(every_head, current, w_out, w_fc, w_proj, w_mlp_pair, head_rows, middle):
     f32, bf16 = jnp.float32, jnp.bfloat16
     for z in range(8):
         head_rows[:, 128 * z : 128 * (z + 1)] = every_head[z]
@@ -120,19 +120,16 @@
     )
     normed = layer_norm(middle[...]).astype(bf16)
 
-    def term(weights):
-        raw = lax.dot_general(
-            normed, weights[0], (((1,), (1,)), ((), ())), preferred_element_type=f32
-        )
+    def term(enter, leave):
+        raw = lax.dot_general(normed, enter, (((1,), (1,)), ((), ())), preferred_element_type=f32)
         rows = jax.nn.gelu(raw, approximate=True).astype(bf16)
-        return jnp.dot(rows, weights[1], preferred_element_type=f32)
-
-    return (term(w_mlp) + term(w_mlp_pair)).astype(bf16)
-
-
-def project(rows_f32, weights):
+        return jnp.dot(rows, leave, preferred_element_type=f32)
+
+    return (term(w_fc[...], w_proj[...]) + term(w_mlp_pair[0], w_mlp_pair[1])).astype(bf16)
+
+
+def project(normed, weights):
     f32, bf16 = jnp.float32, jnp.bfloat16
-    normed = layer_norm(rows_f32).astype(bf16)
     got = lax.dot_general(normed, weights, (((1,), (1,)), ((), ())), preferred_element_type=f32)
     got = jnp.concatenate([got, jnp.zeros((got.shape[0], 64), f32)], 1)
     lane = lax.broadcasted_iota(jnp.int32, (1, 128), 1)
@@ -143,7 +140,7 @@
 def pass_kernel(heads, fresh, accept, current_in, *refs, last):
     net = Net()
     current_in = current_in.at[net.x] if len(current_in.shape) == 3 else current_in
-    loads = 4 if last else 6
+    loads = 5 if last else 7
     sources, refs = (current_in,) + tuple(refs[0 : loads - 1]), refs[loads - 1 :]
     if last:
         out, *refs = refs
@@ -156,7 +153,7 @@
         pltpu.make_async_copy(source, place, load_sems.at[index])
         for index, (source, place) in enumerate(zip(sources, held))
     ]
-    current, w_out, w_mlp, w_mlp_pair = held[0:4]
+    current, w_out, w_fc, w_proj, w_mlp_pair = held[0:5]
     sems, gather_sems, head_sems, pair_sems, swap_sems = (
         tuple(sem_refs[index : index + 2]) for index in range(0, 10, 2)
     )
@@ -169,7 +166,7 @@
     swap_heads(net, heads, peer, every_head, head_sems, pair_sems)
     for copy in copies:
         copy.wait()
-    grown = mlp(net, every_head, current, w_out, w_mlp, w_mlp_pair, head_rows, middle_all)
+    grown = mlp(every_head, current, w_out, w_fc, w_proj, w_mlp_pair, head_rows, middle_all)
     part[...] = grown.reshape(part.shape)
 
     def begin(buf, rows, slot, offset, target):
@@ -220,21 +217,24 @@
         ring_begin(net, out, gather_sems, half, True)
         ring_rest(net, out, gather_sems, half)
         rows_f32 = out[...].reshape(8 * 2 * half, out.shape[2]).astype(f32)
-        w_own, w_pair = held[4:6]
-        stage[...] = project(rows_f32, w_pair[...])
+        w_own, w_pair = held[5:7]
+        normed = layer_norm(rows_f32).astype(bf16)
+        stage[...] = project(normed, w_pair[...])
         net.send(stage, qkv.at[net.x], swap_sems, 0, net.pair)
-        qkv[net.x] = project(rows_f32, w_own[...])
+        qkv[net.x] = project(normed, w_own[...])
         net.arrived(qkv.at[1 - net.x], swap_sems, 0)
     net.finish()
 
 
-def run_pass(heads, current, w_out, w_mlp, w_mlp_pair, fresh, accept, w_qkv_both, collective_id):
+def run_pass(
+    heads, current, w_out, w_fc, w_proj, w_mlp_pair, fresh, accept, w_qkv_both, collective_id
+):
     rows, width = current.shape[-2:]
     lanes, share = heads.shape[2], rows // 8
     bf16 = jnp.bfloat16
     last = w_qkv_both is None
     block = (share // 2, width)
-    operands = (heads, fresh, accept, current, w_out, w_mlp, w_mlp_pair)
+    operands = (heads, fresh, accept, current, w_out, w_fc, w_proj, w_mlp_pair)
     if last:
         shapes = (jax.ShapeDtypeStruct((2, 8, share, width), bf16),)
         first, gather = [], GATHER_SLOTS
@@ -335,7 +335,7 @@
 
 
 def start_kernel(
-    own, w_own, ids, raw_table, tokens_in, w_qkv_in, w_mlp, out, w_all, w_mlp_pair, w_qkv_pair, fresh, rows_out,
+    own, w_own, ids, raw_table, tokens_in, w_qkv_in, w_fc, w_proj, out, w_all, w_mlp_pair, w_qkv_pair, fresh, rows_out,
     qkv, tokens, w_qkv, table, ranks, relatives, sent, got, picked, mine, copy_sems,
     send_sems, recv_sems, send_w, recv_w, send_f, recv_f, send_g, recv_g, send_m, recv_m,
 ):
@@ -421,36 +421,42 @@
     for copy in keeps + loads:
         copy.start()
 
-    units, half_qkv = w_mlp.shape[1] // 5, w_qkv_pair.shape[0] // 2
+    units, half_qkv = w_fc.shape[0] // 5, w_qkv_pair.shape[0] // 2
 
     def pair_pieces(which):
-        for index in range(5):
-            rows = pl.ds(index * units, units)
-            yield w_mlp.at[which, rows], w_mlp_pair.at[which, rows]
+        pieces = [w_mlp_pair.at[which, pl.ds(index * units, units)] for index in range(5)]
         rows = pl.ds(pl.multiple_of(which * half_qkv, half_qkv), half_qkv)
-        yield w_qkv_in.at[rows], w_qkv_pair.at[rows]
+        return pieces + [w_qkv_pair.at[rows]]
 
     def pair_send():
-        for slot, (src, dst) in enumerate(pair_pieces(core)):
-            where = {"blk": net.pair} if slot < 3 else cross
-            copy = pltpu.make_async_remote_copy(
+        def copy_from(src, dst, slot):
+            return pltpu.make_async_remote_copy(
                 src_ref=src,
                 dst_ref=dst,
                 send_sem=m_sems[0].at[slot],
                 recv_sem=m_sems[1].at[slot],
-                device_id=where,
+                device_id={"blk": net.pair} if slot < 3 else cross,
                 device_id_type=MESH,
             )
-            copy.start()
+
+        for slot in range(5):
+            rows = pl.ds(slot * units, units)
+            for which, weights in enumerate((w_fc, w_proj)):
+                copy = copy_from(weights.at[rows], w_mlp_pair.at[which, rows], slot)
+                pl.when(core == which)(copy.start)
             started.append(copy)
+        rows = pl.ds(pl.multiple_of(core * half_qkv, half_qkv), half_qkv)
+        copy = copy_from(w_qkv_in.at[rows], w_qkv_pair.at[rows], 5)
+        copy.start()
+        started.append(copy)
 
     def pair_share():
-        for slot, (_, dst) in enumerate(pair_pieces(core)):
+        for slot, dst in enumerate(pair_pieces(core)):
             net.arrived(dst, m_sems, slot)
             net.send(dst, dst, m_sems, 6 + slot, twin, "req")
 
     def pair_end():
-        for slot, (_, dst) in enumerate(pair_pieces(1 - core)):
+        for slot, dst in enumerate(pair_pieces(1 - core)):
             net.arrived(dst, m_sems, 6 + slot)
 
     def w_begin():
@@ -550,7 +556,7 @@
     def first_qkv(request, _):
         rows_f32 = jnp.transpose(tokens[request].astype(f32))
         rows_out[request] = rows_f32.astype(bf16)
-        qkv[request] = project(rows_f32, w_qkv[...])
+        qkv[request] = project(layer_norm(rows_f32).astype(bf16), w_qkv[...])
         return 0
 
     lax.fori_loop(0, 4, pick, 0)
@@ -580,7 +586,7 @@
             arrived(piece, (DF1 if other_x else DF0) + g - 2)
         share(2, other_x, g)
 
-    for g in PIECES:
+    for index, g in enumerate(PIECES):
         piece = out.at[g, side]
         arrived(piece, SIDE + g)
         send(piece, piece, U1 + g, up)
@@ -588,22 +594,23 @@
         share(0, 1, g)
         from_below(g, 0, U0, UF0)
         from_above(g, 0, D0, DF0)
-        if g == PIECES[0]:
+        if index == 0:
             w_begin()
-        else:
-            w_step(PIECES.index(g) - 1)
-        if g == PIECES[-1]:
-            pair_send()
-            spread()
-    for g in PIECES:
-        from_far(g, 0)
+        elif index == 2:
+            w_step(0)
+    pair_send()
+    w_step(1)
+    spread()
+    for index, g in enumerate(PIECES):
         from_below(g, 1, U1, UF1)
         from_above(g, 1, D1, DF1)
-        if g == PIECES[0]:
-            w_step(3)
-            for load in loads:
-                load.wait()
-            lax.fori_loop(0, 2, first_qkv, 0)
+        from_far(g, 0)
+        if index == 1:
+            w_step(2)
+    for load in loads:
+        load.wait()
+    lax.fori_loop(0, 2, first_qkv, 0)
+    w_step(3)
     for g in PIECES:
         from_far(g, 1)
     for (step, other_x), place in places.items():
@@ -620,7 +627,7 @@
     net.finish()
 
 
-def start_gathers(own, w_own, ids, table, tokens, w_qkv, w_mlp, collective_id):
+def start_gathers(own, w_own, ids, table, tokens, w_qkv, w_fc, w_proj, collective_id):
     groups = own.shape[0]
     count = ids.shape[1]
     columns, vocab_dev = table.shape
@@ -634,13 +641,13 @@
         out_shape=(
             jax.ShapeDtypeStruct((groups, 16) + own.shape[1:], own.dtype),
             jax.ShapeDtypeStruct((8, 2) + w_own.shape, w_own.dtype),
-            jax.ShapeDtypeStruct(w_mlp.shape, w_mlp.dtype),
+            jax.ShapeDtypeStruct((2,) + w_fc.shape, w_fc.dtype),
             jax.ShapeDtypeStruct(w_qkv.shape, w_qkv.dtype),
             jax.ShapeDtypeStruct((count // 16, 16 * columns), bf16),
             jax.ShapeDtypeStruct((requests, rows, width), bf16),
             jax.ShapeDtypeStruct((requests, rows, 256), bf16),
         ),
-        in_specs=anywhere * 2 + whole(2) + anywhere * 3,
+        in_specs=anywhere * 2 + whole(2) + anywhere * 4,
         out_specs=tuple(anywhere * 4 + whole(3)),
         scratch_shapes=[
             pltpu.VMEM(tokens.shape, bf16),
@@ -664,7 +671,7 @@
         ),
         cost_estimate=busy(45),
         name="start_gathers",
-    )(own, w_own, ids, table, tokens, w_qkv, w_mlp)
+    )(own, w_own, ids, table, tokens, w_qkv, w_fc, w_proj)
 
 
 def asked_rows(new_ids):
@@ -762,7 +769,7 @@
     my_groups = lax.dynamic_slice_in_dim(group_ids, req_index * requests, requests)
     lengths = jnp.take(cache_len, my_groups)
     w_own = jnp.transpose(w_qkv[:, 0, :])
-    w_mlp = jnp.stack([jnp.transpose(w_fc), w_proj])
+    w_fc = jnp.transpose(w_fc)
     ids = asked_rows(new_ids)
     every_cache, w_out_all, w_mlp_pair, w_other, fresh, current, qkv = start_gathers(
         cache_kv[:, :, 0, :],
@@ -771,7 +778,8 @@
         jnp.transpose(embed_table),
         jnp.transpose(tokens, (0, 2, 1)),
         w_own,
-        w_mlp,
+        w_fc,
+        w_proj,
         1,
     )
     w_out_all = w_out_all.reshape(16 * head_dim, width)
@@ -785,7 +793,8 @@
             attend(qkv, every_cache, my_groups, lengths),
             current,
             w_out_all,
-            w_mlp,
+            w_fc,
+            w_proj,
             w_mlp_pair,
             fresh[pass_index],
             my_accept[pass_index],

time: 220 us -> 212 us (0.964)
  Pallas kernels: 201 us -> 197 us
  other arithmetic: 5.59 us -> 2.33 us
    pallas_call x1, Pallas kernels: 63.3 us -> 59.8 us  [start_gathers(): pl.pallas_call(start_kernel, out_shape=(jax.ShapeDtypeStruct((groups, 16)...]
    another operation x1 -> x0, other arithmetic: 3.18 us -> none  [shards(): w_mlp = jnp.stack([jnp.transpose(w_fc), w_proj])]
where the time goes in v7:
time: 212 us; the launch traced here: 209 us
  Pallas kernels  197 us (93%)
  local copies, waits for them, and re-layouts  9.5 us (4%)
  other arithmetic  2.33 us (1%)
    pallas_call x2, Pallas kernels, run_pass(): pl.pallas_call(functools.partial(pass_kernel, last=last), out_shape=shape...  115 us
    pallas_call x1, Pallas kernels, start_gathers(): pl.pallas_call(start_kernel, out_shape=(jax.ShapeDtypeStruct((groups, 16)...  59.8 us
    pallas_call x2, Pallas kernels, attend(): pl.pallas_call(functools.partial(attend_kernel, span=min(2048, size)), ou...  21.8 us

profile of v7, /device:TPU:12, one launch (start us, length us, event | category | flops | bytes accessed | tf_op | source)
XLA Modules:
  0.0 209.4 jit_solution(5022777321740000995)
XLA Ops:
  0.0 0.0 copy-start
  0.0 0.7 compare_select_fusion.2
  0.8 0.0 copy-done
  0.8 0.6 gather_fusion.1
  1.4 0.5 and_select_fusion.lengths
  1.9 0.9 reshape.112
  2.9 0.2 copy.61
  3.1 0.3 reshape.113.ids
  3.5 59.8 %start_gathers.1 = (bf16[4,16,512,128]{3,2,1,0:T(8,128)(2,1)}, bf16[8,2,2,32,1600]{4,3,2,1,0:T(8,128)(2,1)}, bf16[2,400,1600]{2,1,0:T(8,128)(2,1)}, bf16[192,160...) custom-call(bf16[4,512,128]{2,1,0:T(8,128)(2,1)} %bitcast.43, ...), custom_call_target="tpu_custom_call" | custom-call | flops 17999998976 | bytes 135000000 | tf_op jit(solution)/shard_map/start_gathers/pallas_call | solution.py:639
  63.3 0.0 copy-done.2
  63.3 0.0 copy-start.1
  63.3 10.8 %attend.2.heads = bf16[2,256,128]{2,1,0:T(8,128)(2,1)} custom-call(s32[2]{0:T(128)} %copy-done.2, s32[2]{0:T(128)} %and_select_fusion.lengths, bf16[2,256,256]{2,1,0:T(8,128)(2,1)} %get-tuple-element.30.qkv, bf16[4,8192,128]{2,1,0:T(8,128)(2,1)} %bitcast.45), custom_call_target="tpu_custom_call" | custom-call | flops 4400000000 | bytes 33000000 | tf_op jit(solution)/shard_map/attend/pallas_call | solution.py:741
  74.2 0.4 convert_reduce_fusion
  74.6 0.6 reduce_max.9
  75.9 0.0 copy-done.1
  75.9 1.6 conditional.1
  75.9 1.6 fusion.1
  77.5 0.8 dynamic-slice_bitcast_fusion
  78.3 0.7 copy.56.accept
  79.0 57.4 %pass_2.1 = (bf16[8,32,1600]{2,1,0:T(8,128)(2,1)}, bf16[2,256,256]{2,1,0:T(8,128)(2,1)}) custom-call(bf16[2,256,128]{2,1,0:T(8,128)(2,1)} %attend.2.heads, bf16[32,1600]{1,0:T(8,128)(2,1)S(1)} %get-tuple-element.33.fresh, s32[32,1]{1,0:T(8,128)} %copy.56.accept, bf16[2,256,1600]{2,1,0:T(8,128)(2,1)} %get-tuple-element.34.current_in, ...), custom_call_target="tpu_custom_call" | custom-call | flops 20000000000 | bytes 150000000 | tf_op jit(solution)/shard_map/pass_2/pallas_call | solution.py:260
  136.4 11.0 %attend.3.heads = bf16[2,256,128]{2,1,0:T(8,128)(2,1)} custom-call(s32[2]{0:T(128)} %copy-done.2, s32[2]{0:T(128)} %and_select_fusion.lengths, bf16[2,256,256]{2,1,0:T(8,128)(2,1)} %get-tuple-element.38.qkv, bf16[4,8192,128]{2,1,0:T(8,128)(2,1)} %bitcast.46), custom_call_target="tpu_custom_call" | custom-call | flops 4400000000 | bytes 33000000 | tf_op jit(solution)/shard_map/attend/pallas_call | solution.py:741
  147.3 0.7 copy.57.accept
  148.0 57.8 %pass_3.1 = bf16[2,8,32,1600]{3,2,1,0:T(8,128)(2,1)} custom-call(bf16[2,256,128]{2,1,0:T(8,128)(2,1)} %attend.3.heads, bf16[32,1600]{1,0:T(8,128)(2,1)} %get-tuple-element.39.fresh, s32[32,1]{1,0:T(8,128)} %copy.57.accept, bf16[256,1600]{1,0:T(8,128)(2,1)} %bitcast.49, bf16[1024,1600]{1,0:T(8,128)(2,1)} %bitcast.48, bf16[400,1600]{1,0:T(8,128)(2,1)} %bitcast.40, ...), custom_call_target="tpu_custom_call" | custom-call | flops 20000000000 | bytes 150000000 | tf_op jit(solution)/shard_map/pass_3/pallas_call | solution.py:260
  205.8 3.6 %copy.58 = bf16[2,256,1600]{1,2,0:T(8,128)(2,1)} copy(bf16[2,256,1600]{2,1,0:T(8,128)(2,1)} %bitcast.31) | data formatting | bytes 3276800 | tf_op jit(solution)/shard_map/reshape | solution.py:805
  (3 shorter events, 0.1 us)
Async XLA Ops:
  0.0 0.8 copy-start
  0.7 62.6 %copy-start.2 = (s32[2]{0:T(128)}, s32[2]{0:T(128)S(1)}, u32[]{:S(2)}) copy-start(s32[2]{0:T(128)S(1)} %get-tuple-element.60.groups) | copy-start | bytes 28
  63.3 12.6 %copy-start.1 = (bf16[3141,100]{0,1:T(8,128)(2,1)S(1)}, bf16[3141,100]{0,1:T(8,128)(2,1)}, u32[]{:S(2)}) copy-start(bf16[3141,100]{0,1:T(8,128)(2,1)} %param.19) | copy-start | bytes 1884604

commit v8 on v7

--- a/solution.py
+++ b/solution.py
@@ -331,7 +331,7 @@
 PIECES = (0, 2, 1, 3)
 
 
-SLOTS = 128
+SLOTS = 112
 
 
 def start_kernel(

time: 212 us -> 211 us (level)
  no operation moved by 1% of the time
where the time goes in v8:
time: 211 us; the launch traced here: 209 us
  Pallas kernels  196 us (93%)
  local copies, waits for them, and re-layouts  9.5 us (5%)
  other arithmetic  2.33 us (1%)
    pallas_call x2, Pallas kernels, run_pass(): pl.pallas_call(functools.partial(pass_kernel, last=last), out_shape=shape...  115 us
    pallas_call x1, Pallas kernels, start_gathers(): pl.pallas_call(start_kernel, out_shape=(jax.ShapeDtypeStruct((groups, 16)...  59.1 us
    pallas_call x2, Pallas kernels, attend(): pl.pallas_call(functools.partial(attend_kernel, span=min(2048, size)), ou...  21.8 us

profile of v8, /device:TPU:12, one launch (start us, length us, event | category | flops | bytes accessed | tf_op | source)
XLA Modules:
  0.0 208.7 jit_solution(6235063390097895763)
XLA Ops:
  0.0 0.0 copy-start
  0.0 0.7 compare_select_fusion.2
  0.8 0.0 copy-done
  0.8 0.6 gather_fusion.1
  1.4 0.5 and_select_fusion.lengths
  1.9 0.9 reshape.112
  2.9 0.2 copy.61
  3.1 0.3 reshape.113.ids
  3.5 59.1 %start_gathers.1 = (bf16[4,16,512,128]{3,2,1,0:T(8,128)(2,1)}, bf16[8,2,2,32,1600]{4,3,2,1,0:T(8,128)(2,1)}, bf16[2,400,1600]{2,1,0:T(8,128)(2,1)}, bf16[192,160...) custom-call(bf16[4,512,128]{2,1,0:T(8,128)(2,1)} %bitcast.43, ...), custom_call_target="tpu_custom_call" | custom-call | flops 17999998976 | bytes 135000000 | tf_op jit(solution)/shard_map/start_gathers/pallas_call | solution.py:639
  62.6 0.0 copy-done.2
  62.6 0.0 copy-start.1
  62.6 10.8 %attend.2.heads = bf16[2,256,128]{2,1,0:T(8,128)(2,1)} custom-call(s32[2]{0:T(128)} %copy-done.2, s32[2]{0:T(128)} %and_select_fusion.lengths, bf16[2,256,256]{2,1,0:T(8,128)(2,1)} %get-tuple-element.30.qkv, bf16[4,8192,128]{2,1,0:T(8,128)(2,1)} %bitcast.45), custom_call_target="tpu_custom_call" | custom-call | flops 4400000000 | bytes 33000000 | tf_op jit(solution)/shard_map/attend/pallas_call | solution.py:741
  73.5 0.4 convert_reduce_fusion
  73.9 0.6 reduce_max.9
  75.2 0.0 copy-done.1
  75.2 1.6 conditional.1
  75.2 1.6 fusion.1
  76.8 0.8 dynamic-slice_bitcast_fusion
  77.6 0.7 copy.56.accept
  78.3 57.3 %pass_2.1 = (bf16[8,32,1600]{2,1,0:T(8,128)(2,1)}, bf16[2,256,256]{2,1,0:T(8,128)(2,1)}) custom-call(bf16[2,256,128]{2,1,0:T(8,128)(2,1)} %attend.2.heads, bf16[32,1600]{1,0:T(8,128)(2,1)S(1)} %get-tuple-element.33.fresh, s32[32,1]{1,0:T(8,128)} %copy.56.accept, bf16[2,256,1600]{2,1,0:T(8,128)(2,1)} %get-tuple-element.34.current_in, ...), custom_call_target="tpu_custom_call" | custom-call | flops 20000000000 | bytes 150000000 | tf_op jit(solution)/shard_map/pass_2/pallas_call | solution.py:260
  135.6 11.0 %attend.3.heads = bf16[2,256,128]{2,1,0:T(8,128)(2,1)} custom-call(s32[2]{0:T(128)} %copy-done.2, s32[2]{0:T(128)} %and_select_fusion.lengths, bf16[2,256,256]{2,1,0:T(8,128)(2,1)} %get-tuple-element.38.qkv, bf16[4,8192,128]{2,1,0:T(8,128)(2,1)} %bitcast.46), custom_call_target="tpu_custom_call" | custom-call | flops 4400000000 | bytes 33000000 | tf_op jit(solution)/shard_map/attend/pallas_call | solution.py:741
  146.6 0.7 copy.57.accept
  147.2 57.9 %pass_3.1 = bf16[2,8,32,1600]{3,2,1,0:T(8,128)(2,1)} custom-call(bf16[2,256,128]{2,1,0:T(8,128)(2,1)} %attend.3.heads, bf16[32,1600]{1,0:T(8,128)(2,1)} %get-tuple-element.39.fresh, s32[32,1]{1,0:T(8,128)} %copy.57.accept, bf16[256,1600]{1,0:T(8,128)(2,1)} %bitcast.49, bf16[1024,1600]{1,0:T(8,128)(2,1)} %bitcast.48, bf16[400,1600]{1,0:T(8,128)(2,1)} %bitcast.40, ...), custom_call_target="tpu_custom_call" | custom-call | flops 20000000000 | bytes 150000000 | tf_op jit(solution)/shard_map/pass_3/pallas_call | solution.py:260
  205.1 3.6 %copy.58 = bf16[2,256,1600]{1,2,0:T(8,128)(2,1)} copy(bf16[2,256,1600]{2,1,0:T(8,128)(2,1)} %bitcast.31) | data formatting | bytes 3276800 | tf_op jit(solution)/shard_map/reshape | solution.py:805
  (3 shorter events, 0.1 us)
Async XLA Ops:
  0.0 0.8 copy-start
  0.7 61.9 %copy-start.2 = (s32[2]{0:T(128)}, s32[2]{0:T(128)S(1)}, u32[]{:S(2)}) copy-start(s32[2]{0:T(128)S(1)} %get-tuple-element.60.groups) | copy-start | bytes 28
  62.6 12.6 %copy-start.1 = (bf16[3141,100]{0,1:T(8,128)(2,1)S(1)}, bf16[3141,100]{0,1:T(8,128)(2,1)}, u32[]{:S(2)}) copy-start(bf16[3141,100]{0,1:T(8,128)(2,1)} %param.19) | copy-start | bytes 1884604
